TPU v7x, 32 devices: a whole 2x2x4 slice. The times are simulated.
32 devices in a mesh: dp: 4 (over y, core), seq: 2 (over x), mp: 4 (over z).
Axes of the slice: x: 2, y: 2, z: 4, core: 2. Of those that a mesh axis runs over, the one named last changes fastest.
Arguments:
- acts: bfloat16 [4, 1024, 2, 768], P('dp', 'mp', 'seq'), may hold values from -6 to 6
- cotangent: bfloat16 [4, 1024, 2, 768], P('dp', 'mp', 'seq'), may hold values from -8 to 8
- col_mask: int32 [4, 1024], P('dp'), may hold values from 0 to 1, as said below
- ln_row_gain: float32 [1, 768], replicated, may hold values from 0.5 to 1.5
- ln_row_bias: float32 [1, 768], replicated, may hold values from -1.25 to 1.25
- row_wq: bfloat16 [1, 768, 768], P(None, None, 'mp'), may hold values from -0.21875 to 0.21875
- row_wk: bfloat16 [1, 768, 768], P(None, None, 'mp'), may hold values from -0.21875 to 0.21875
- row_wv: bfloat16 [1, 768, 768], P(None, None, 'mp'), may hold values from -0.21875 to 0.21875
- row_bq: float32 [1, 768], P(None, 'mp'), may hold values from -1.25 to 1.25
- row_bv: float32 [1, 768], P(None, 'mp'), may hold values from -1.25 to 1.25
- row_wo: bfloat16 [1, 768, 768], P(None, 'mp'), may hold values from -0.875 to 0.875
- row_bo: float32 [1, 768], replicated, may hold values from -1.25 to 1.25
- ln_col_gain: float32 [1, 768], replicated, may hold values from 0.5 to 1.5
- ln_col_bias: float32 [1, 768], replicated, may hold values from -1.25 to 1.25
- col_wq: bfloat16 [1, 768, 768], P(None, None, 'mp'), may hold values from -0.21875 to 0.21875
- col_wk: bfloat16 [1, 768, 768], P(None, None, 'mp'), may hold values from -0.21875 to 0.21875
- col_wv: bfloat16 [1, 768, 768], P(None, None, 'mp'), may hold values from -0.21875 to 0.21875
- col_bq: float32 [1, 768], P(None, 'mp'), may hold values from -1.25 to 1.25
- col_bv: float32 [1, 768], P(None, 'mp'), may hold values from -1.25 to 1.25
- col_wo: bfloat16 [1, 768, 768], P(None, 'mp'), may hold values from -0.4375 to 0.4375
- col_bo: float32 [1, 768], replicated, may hold values from -1.25 to 1.25
- ln_ffn_gain: float32 [1, 768], replicated, may hold values from 0.5 to 1.5
- ln_ffn_bias: float32 [1, 768], replicated, may hold values from -1.25 to 1.25
- ffn_w1: bfloat16 [1, 768, 3072], P(None, None, 'mp'), may hold values from -0.21875 to 0.21875
- ffn_b1: float32 [1, 3072], P(None, 'mp'), may hold values from -1.25 to 1.25
- ffn_w2: bfloat16 [1, 3072, 768], P(None, 'mp'), may hold values from -0.15625 to 0.15625
- ffn_b2: float32 [1, 768], replicated, may hold values from -1.25 to 1.25
Outputs:
- out: float32 [4, 1024, 2, 768], P('dp', 'mp', 'seq')
- grad_acts: float32 [4, 1024, 2, 768], P('dp', 'mp', 'seq')
- grad_ln_row_gain: float32 [1, 768], P(None, ('dp', 'seq', 'mp'))
- grad_ln_row_bias: float32 [1, 768], P(None, ('dp', 'seq', 'mp'))
- grad_row_wq: float32 [1, 768, 768], P(None, ('dp', 'seq'), 'mp')
- grad_row_wk: float32 [1, 768, 768], P(None, ('dp', 'seq'), 'mp')
- grad_row_wv: float32 [1, 768, 768], P(None, ('dp', 'seq'), 'mp')
- grad_row_bq: float32 [1, 768], P(None, 'mp')
- grad_row_bv: float32 [1, 768], P(None, 'mp')
- grad_row_wo: float32 [1, 768, 768], P(None, 'mp', ('dp', 'seq'))
- grad_row_bo: float32 [1, 768], P(None, ('dp', 'seq', 'mp'))
- grad_ln_col_gain: float32 [1, 768], P(None, ('dp', 'seq', 'mp'))
- grad_ln_col_bias: float32 [1, 768], P(None, ('dp', 'seq', 'mp'))
- grad_col_wq: float32 [1, 768, 768], P(None, ('dp', 'seq'), 'mp')
- grad_col_wk: float32 [1, 768, 768], P(None, ('dp', 'seq'), 'mp')
- grad_col_wv: float32 [1, 768, 768], P(None, ('dp', 'seq'), 'mp')
- grad_col_bq: float32 [1, 768], P(None, 'mp')
- grad_col_bv: float32 [1, 768], P(None, 'mp')
- grad_col_wo: float32 [1, 768, 768], P(None, 'mp', ('dp', 'seq'))
- grad_col_bo: float32 [1, 768], P(None, ('dp', 'seq', 'mp'))
- grad_ln_ffn_gain: float32 [1, 768], P(None, ('dp', 'seq', 'mp'))
- grad_ln_ffn_bias: float32 [1, 768], P(None, ('dp', 'seq', 'mp'))
- grad_ffn_w1: float32 [1, 768, 3072], P(None, ('dp', 'seq'), 'mp')
- grad_ffn_b1: float32 [1, 3072], P(None, 'mp')
- grad_ffn_w2: float32 [1, 3072, 768], P(None, 'mp', ('dp', 'seq'))
- grad_ffn_b2: float32 [1, 768], P(None, ('dp', 'seq', 'mp'))
Inputs may be any that keep to these rules, and one draw needn't show every extreme that they name: `col_mask`: in each alignment the valid columns are a leading run of 64 to 1024 columns; some alignment has all 1024 columns valid.
All inputs are finite; a program needn't handle non-finite values.
Results may differ from a plain program's by a relative error of at most 0.035.
Values may be sent and summed in bfloat16 or wider, within the bound.
No kernel may reach another device: no remote copies, remote signals or barrier semaphores. Data moves between devices by JAX's collectives and lax.ppermute only.
A program may use at most 192 MiB of HBM per device.

v0:
```python
import math

import jax
import jax.numpy as jnp
from jax import lax
from jax.sharding import PartitionSpec as P

HD = 64
DP, SEQ, MP = AXES = ("dp", "seq", "mp")


EPSILON = 1e-05


def cut_along(shard, dim, peers):
    before, after = (shard.shape[:dim], shard.shape[dim + 1 :])
    return jnp.moveaxis(shard.reshape(*before, peers, -1, *after), dim, 0)


def sent_and_summed(shard, axis, dim):
    blocks = cut_along(shard, dim, lax.axis_size(axis))
    arrived = lax.all_to_all(blocks, axis, split_axis=0, concat_axis=0, tiled=True)
    return arrived.astype(jnp.float32).sum(axis=0)


def in_one_piece(arrays, axis, dim, along):
    ends, at = ([], 0)
    for a in arrays[:-1]:
        at += a.shape[along]
        ends.append(at)
    both = jnp.concatenate(arrays, axis=along)
    return tuple(jnp.split(sent_and_summed(both, axis, dim), ends, axis=along))


def normalize(values, norm_gain, norm_shift):
    average = jnp.mean(values, axis=-1, keepdims=True)
    centred = values - average
    variance = jnp.mean(centred * centred, axis=-1, keepdims=True)
    return centred * lax.rsqrt(variance + EPSILON) * norm_gain + norm_shift


def exact_gelu(values):
    return jax.nn.gelu(values, approximate=False)


def split_heads(values):
    return values.reshape(values.shape[:-1] + (values.shape[-1] // HD, HD))


def merge_heads(values):
    return values.reshape(values.shape[:-2] + (values.shape[-2] * values.shape[-1],))


def project(operand, weight):
    return lax.dot_general(
        operand, weight, (((operand.ndim - 1,), (0,)), ((), ())), preferred_element_type=jnp.float32
    )


def project_back(operand, weight):
    return lax.dot_general(
        operand, weight, (((operand.ndim - 1,), (1,)), ((), ())), preferred_element_type=jnp.float32
    )


def weight_gradient(operand, gradient):
    flat_operand = operand.reshape(-1, operand.shape[-1])
    flat_gradient = gradient.reshape(-1, gradient.shape[-1])
    return lax.dot_general(
        flat_operand, flat_gradient, (((0,), (0,)), ((), ())), preferred_element_type=jnp.float32
    )


def token_total(gradient):
    return jnp.sum(gradient.astype(jnp.float32).reshape(-1, gradient.shape[-1]), axis=0)


def model_gather(values):
    return lax.all_gather(values, MP, axis=0, tiled=True)


def model_sum(operand_pairs, backward):
    running_total = None
    for operand, weight in operand_pairs:
        if backward:
            product = project_back(operand, weight)
        else:
            product = project(operand, weight)
        running_total = product if running_total is None else running_total + product
    return lax.psum_scatter(
        running_total.astype(jnp.bfloat16), MP, scatter_dimension=0, tiled=True
    ).astype(jnp.float32)


def to_columns(values):
    return lax.all_to_all(
        values.astype(jnp.bfloat16), SEQ, split_axis=0, concat_axis=1, tiled=True
    ).astype(values.dtype)


def to_rows(values):
    return lax.all_to_all(
        values.astype(jnp.bfloat16), SEQ, split_axis=1, concat_axis=0, tiled=True
    ).astype(values.dtype)


def to_query_share(values):
    return lax.all_to_all(values, SEQ, split_axis=0, concat_axis=1, tiled=True)


def masked_softmax(logits, valid_cols, score_scale):
    scores = jnp.where((valid_cols > 0)[None, None, :], logits * score_scale, -1e30)
    highest = jnp.max(scores, axis=-1, keepdims=True)
    powers = jnp.exp(scores - highest)
    return powers / jnp.sum(powers, axis=-1, keepdims=True)


def tied_scale(key_rows):
    return 1.0 / math.sqrt(HD * key_rows.shape[1] * lax.axis_size(SEQ))


def tied_forward(queries, key_rows, value_rows, valid_cols):
    score_scale = tied_scale(key_rows)
    value_all = None
    key_all, value_all = (
        lax.all_gather(key_rows, SEQ, axis=1, tiled=True),
        lax.all_gather(value_rows, SEQ, axis=1, tiled=True),
    )
    query_share = to_query_share(queries)
    logits = jnp.einsum(
        "irhd,jrhd->hij",
        split_heads(query_share),
        split_heads(key_all),
        preferred_element_type=jnp.float32,
    )
    attention = masked_softmax(logits, valid_cols, score_scale)
    attention_all = lax.all_gather(attention.astype(jnp.bfloat16), SEQ, axis=1, tiled=True)
    head_values = jnp.einsum(
        "hij,jrhd->irhd", attention_all, split_heads(value_rows), preferred_element_type=jnp.float32
    )
    return (merge_heads(head_values).astype(jnp.bfloat16), attention, attention_all, value_all)


def tied_backward(grad_heads, queries, key_rows, attention, attention_all, value_all):
    score_scale = tied_scale(key_rows)
    grad_share = to_query_share(grad_heads)
    grad_weights = jnp.einsum(
        "irhd,jrhd->hij",
        split_heads(grad_share),
        split_heads(value_all),
        preferred_element_type=jnp.float32,
    )
    inner_sum = jnp.sum(attention * grad_weights, axis=-1, keepdims=True)
    grad_logits = (attention * (grad_weights - inner_sum)).astype(jnp.bfloat16)
    logits_all = lax.all_gather(grad_logits, SEQ, axis=1, tiled=True)
    grad_query = (
        jnp.einsum(
            "hij,jrhd->irhd", logits_all, split_heads(key_rows), preferred_element_type=jnp.float32
        )
        * score_scale
    )
    grad_key = (
        jnp.einsum(
            "hij,irhd->jrhd", logits_all, split_heads(queries), preferred_element_type=jnp.float32
        )
        * score_scale
    )
    grad_value = jnp.einsum(
        "hij,irhd->jrhd", attention_all, split_heads(grad_heads), preferred_element_type=jnp.float32
    )
    return (
        merge_heads(grad_query).astype(jnp.bfloat16),
        merge_heads(grad_key).astype(jnp.bfloat16),
        merge_heads(grad_value).astype(jnp.bfloat16),
    )


def column_forward(queries, key_rows, value_rows):
    score_scale = 1.0 / math.sqrt(HD)
    scores = (
        jnp.einsum(
            "crhd,cshd->chrs",
            split_heads(queries),
            split_heads(key_rows),
            preferred_element_type=jnp.float32,
        )
        * score_scale
    )
    highest = jnp.max(scores, axis=-1, keepdims=True)
    powers = jnp.exp(scores - highest)
    attention = powers / jnp.sum(powers, axis=-1, keepdims=True)
    attention_low = attention.astype(jnp.bfloat16)
    head_values = jnp.einsum(
        "chrs,cshd->crhd",
        attention_low,
        split_heads(value_rows),
        preferred_element_type=jnp.float32,
    )
    return (merge_heads(head_values).astype(jnp.bfloat16), attention, attention_low)


def column_backward(grad_heads, queries, key_rows, value_rows, attention, attention_low):
    score_scale = 1.0 / math.sqrt(HD)
    grad_split = split_heads(grad_heads)
    grad_weights = jnp.einsum(
        "crhd,cshd->chrs", grad_split, split_heads(value_rows), preferred_element_type=jnp.float32
    )
    grad_value = jnp.einsum(
        "chrs,crhd->cshd", attention_low, grad_split, preferred_element_type=jnp.float32
    )
    inner_sum = jnp.sum(attention * grad_weights, axis=-1, keepdims=True)
    grad_logits = (attention * (grad_weights - inner_sum)).astype(jnp.bfloat16)
    grad_query = (
        jnp.einsum(
            "chrs,cshd->crhd",
            grad_logits,
            split_heads(key_rows),
            preferred_element_type=jnp.float32,
        )
        * score_scale
    )
    grad_key = (
        jnp.einsum(
            "chrs,crhd->cshd", grad_logits, split_heads(queries), preferred_element_type=jnp.float32
        )
        * score_scale
    )
    return (
        merge_heads(grad_query).astype(jnp.bfloat16),
        merge_heads(grad_key).astype(jnp.bfloat16),
        merge_heads(grad_value).astype(jnp.bfloat16),
    )


def norm_backward(values, norm_gain, norm_shift, gradient):
    norm_value, norm_pull = jax.vjp(normalize, values, norm_gain, norm_shift)
    return norm_pull(gradient)


def on_device(
    acts,
    cotangent,
    col_mask,
    ln_row_gain,
    ln_row_bias,
    row_wq,
    row_wk,
    row_wv,
    row_bq,
    row_bv,
    row_wo,
    row_bo,
    ln_col_gain,
    ln_col_bias,
    col_wq,
    col_wk,
    col_wv,
    col_bq,
    col_bv,
    col_wo,
    col_bo,
    ln_ffn_gain,
    ln_ffn_bias,
    ffn_w1,
    ffn_b1,
    ffn_w2,
    ffn_b2,
):
    stream = acts[0].astype(jnp.float32)
    valid_cols = col_mask[0]
    rec_row_in = stream
    normed = normalize(stream, ln_row_gain[0], ln_row_bias[0]).astype(
        jnp.bfloat16
    )
    hidden = model_gather(normed)
    queries = (project(hidden, row_wq[0]) + row_bq[0]).astype(jnp.bfloat16)
    key_rows = project(hidden, row_wk[0]).astype(jnp.bfloat16)
    value_rows = (project(hidden, row_wv[0]) + row_bv[0]).astype(jnp.bfloat16)
    head_values, attention, attention_all, value_all = tied_forward(
        queries, key_rows, value_rows, valid_cols
    )
    stream = stream + model_sum(((head_values, row_wo[0]),), False) + row_bo[0]
    rec_row_hidden = hidden
    rec_row_queries = queries
    rec_row_keys = key_rows
    rec_row_values = value_rows
    rec_row_attention = attention
    rec_row_attention_all = attention_all
    rec_row_value_all = value_all
    rec_row_heads = head_values
    column_stream = to_columns(stream)
    rec_col_in = column_stream
    normed = normalize(column_stream, ln_col_gain[0], ln_col_bias[0]).astype(
        jnp.bfloat16
    )
    hidden = model_gather(normed)
    queries = (project(hidden, col_wq[0]) + col_bq[0]).astype(jnp.bfloat16)
    key_rows = project(hidden, col_wk[0]).astype(jnp.bfloat16)
    value_rows = (project(hidden, col_wv[0]) + col_bv[0]).astype(jnp.bfloat16)
    head_values, attention, attention_low = column_forward(queries, key_rows, value_rows)
    column_stream = (
        column_stream
        + model_sum(((head_values, col_wo[0]),), False)
        + col_bo[0]
    )
    rec_col_hidden = hidden
    rec_col_queries = queries
    rec_col_keys = key_rows
    rec_col_values = value_rows
    rec_col_attention = attention
    rec_col_attention_low = attention_low
    rec_col_heads = head_values
    rec_ffn_in = column_stream
    normed = normalize(column_stream, ln_ffn_gain[0], ln_ffn_bias[0]).astype(
        jnp.bfloat16
    )
    hidden = model_gather(normed)
    up_values = project(hidden, ffn_w1[0]) + ffn_b1[0]
    activated = exact_gelu(up_values).astype(jnp.bfloat16)
    column_stream = (
        column_stream + model_sum(((activated, ffn_w2[0]),), False) + ffn_b2[0]
    )
    rec_ffn_hidden = hidden
    rec_ffn_up = up_values
    rec_ffn_act = activated
    stream = to_rows(column_stream)
    gradient = cotangent[0].astype(jnp.float32)
    column_grad = to_columns(gradient)
    grad_low = column_grad.astype(jnp.bfloat16)
    grad_all = model_gather(grad_low)
    g_ffn_w2 = weight_gradient(rec_ffn_act, grad_all)
    g_ffn_b2 = token_total(grad_low)
    grad_act = project_back(grad_all, ffn_w2[0])
    gelu_value, gelu_pull = jax.vjp(exact_gelu, rec_ffn_up)
    grad_up = gelu_pull(grad_act)[0].astype(jnp.bfloat16)
    g_ffn_w1 = weight_gradient(rec_ffn_hidden, grad_up)
    g_ffn_b1 = token_total(grad_up)
    grad_normed = model_sum(((grad_up, ffn_w1[0]),), True)
    grad_input, grad_gain, grad_shift = norm_backward(
        rec_ffn_in, ln_ffn_gain[0], ln_ffn_bias[0], grad_normed
    )
    g_ln_ffn_gain = grad_gain
    g_ln_ffn_bias = grad_shift
    column_grad = column_grad + grad_input
    grad_low = column_grad.astype(jnp.bfloat16)
    grad_all = model_gather(grad_low)
    g_col_wo = weight_gradient(rec_col_heads, grad_all)
    g_col_bo = token_total(grad_low)
    grad_heads = project_back(grad_all, col_wo[0]).astype(jnp.bfloat16)
    grad_query, grad_key, grad_value = column_backward(
        grad_heads,
        rec_col_queries,
        rec_col_keys,
        rec_col_values,
        rec_col_attention,
        rec_col_attention_low,
    )
    g_col_wq = weight_gradient(rec_col_hidden, grad_query)
    g_col_wk = weight_gradient(rec_col_hidden, grad_key)
    g_col_wv = weight_gradient(rec_col_hidden, grad_value)
    g_col_bq = token_total(grad_query)
    g_col_bv = token_total(grad_value)
    grad_normed = model_sum(
        (
            (grad_query, col_wq[0]),
            (grad_key, col_wk[0]),
            (grad_value, col_wv[0]),
        ),
        True,
    )
    grad_input, grad_gain, grad_shift = norm_backward(
        rec_col_in, ln_col_gain[0], ln_col_bias[0], grad_normed
    )
    g_ln_col_gain = grad_gain
    g_ln_col_bias = grad_shift
    column_grad = column_grad + grad_input
    gradient = to_rows(column_grad)
    grad_low = gradient.astype(jnp.bfloat16)
    grad_all = model_gather(grad_low)
    g_row_wo = weight_gradient(rec_row_heads, grad_all)
    g_row_bo = token_total(grad_low)
    grad_heads = project_back(grad_all, row_wo[0]).astype(jnp.bfloat16)
    grad_query, grad_key, grad_value = tied_backward(
        grad_heads,
        rec_row_queries,
        rec_row_keys,
        rec_row_attention,
        rec_row_attention_all,
        rec_row_value_all,
    )
    g_row_wq = weight_gradient(rec_row_hidden, grad_query)
    g_row_wk = weight_gradient(rec_row_hidden, grad_key)
    g_row_wv = weight_gradient(rec_row_hidden, grad_value)
    g_row_bq = token_total(grad_query)
    g_row_bv = token_total(grad_value)
    grad_normed = model_sum(
        (
            (grad_query, row_wq[0]),
            (grad_key, row_wk[0]),
            (grad_value, row_wv[0]),
        ),
        True,
    )
    grad_input, grad_gain, grad_shift = norm_backward(
        rec_row_in, ln_row_gain[0], ln_row_bias[0], grad_normed
    )
    g_ln_row_gain = grad_gain
    g_ln_row_bias = grad_shift
    gradient = gradient + grad_input
    matrix_totals = (
        lax.psum_scatter(
            g_row_wq[None], (DP, SEQ), scatter_dimension=1, tiled=True
        ),
        lax.psum_scatter(
            g_row_wk[None], (DP, SEQ), scatter_dimension=1, tiled=True
        ),
        lax.psum_scatter(
            g_row_wv[None], (DP, SEQ), scatter_dimension=1, tiled=True
        ),
        lax.psum_scatter(
            g_col_wq[None], (DP, SEQ), scatter_dimension=1, tiled=True
        ),
        lax.psum_scatter(
            g_col_wk[None], (DP, SEQ), scatter_dimension=1, tiled=True
        ),
        lax.psum_scatter(
            g_col_wv[None], (DP, SEQ), scatter_dimension=1, tiled=True
        ),
        lax.psum_scatter(
            g_ffn_w1[None], (DP, SEQ), scatter_dimension=1, tiled=True
        ),
    )
    output_totals = in_one_piece(
        (
            g_row_wo[None].astype(jnp.bfloat16),
            g_col_wo[None].astype(jnp.bfloat16),
            g_ffn_w2[None].astype(jnp.bfloat16),
        ),
        (DP, SEQ),
        2,
        1,
    )
    vector_totals = (
        lax.psum_scatter(
            g_ln_row_gain[None],
            (DP, SEQ, MP),
            scatter_dimension=1,
            tiled=True,
        ),
        lax.psum_scatter(
            g_ln_row_bias[None],
            (DP, SEQ, MP),
            scatter_dimension=1,
            tiled=True,
        ),
        lax.psum_scatter(
            g_row_bo[None], (DP, SEQ, MP), scatter_dimension=1, tiled=True
        ),
        lax.psum_scatter(
            g_ln_col_gain[None],
            (DP, SEQ, MP),
            scatter_dimension=1,
            tiled=True,
        ),
        lax.psum_scatter(
            g_ln_col_bias[None],
            (DP, SEQ, MP),
            scatter_dimension=1,
            tiled=True,
        ),
        lax.psum_scatter(
            g_col_bo[None], (DP, SEQ, MP), scatter_dimension=1, tiled=True
        ),
        lax.psum_scatter(
            g_ln_ffn_gain[None],
            (DP, SEQ, MP),
            scatter_dimension=1,
            tiled=True,
        ),
        lax.psum_scatter(
            g_ln_ffn_bias[None],
            (DP, SEQ, MP),
            scatter_dimension=1,
            tiled=True,
        ),
        lax.psum_scatter(
            g_ffn_b2[None], (DP, SEQ, MP), scatter_dimension=1, tiled=True
        ),
    )
    bias_totals = lax.psum(
        (
            g_row_bq[None],
            g_row_bv[None],
            g_col_bq[None],
            g_col_bv[None],
            g_ffn_b1[None],
        ),
        (DP, SEQ),
    )
    return (
        stream[None],
        gradient[None],
        vector_totals[0],
        vector_totals[1],
        matrix_totals[0],
        matrix_totals[1],
        matrix_totals[2],
        bias_totals[0],
        bias_totals[1],
        output_totals[0],
        vector_totals[2],
        vector_totals[3],
        vector_totals[4],
        matrix_totals[3],
        matrix_totals[4],
        matrix_totals[5],
        bias_totals[2],
        bias_totals[3],
        output_totals[1],
        vector_totals[5],
        vector_totals[6],
        vector_totals[7],
        matrix_totals[6],
        bias_totals[4],
        output_totals[2],
        vector_totals[8],
    )


def routed(values, target_of):
    dps, seqs, mps = (lax.axis_size(axis) for axis in AXES)
    pairs = []
    for d in range(dps):
        for s in range(seqs):
            for m in range(mps):
                to_d, to_s, to_m = target_of(d, s, m)
                pairs.append(((d * seqs + s) * mps + m, (to_d * seqs + to_s) * mps + to_m))
    return lax.ppermute(values, AXES, pairs)


def shifted(values, step):
    mps = lax.axis_size(MP)
    return routed(values, lambda d, s, m: (d, s, (m + step) % mps))


def to_sibling(values):
    return routed(values, lambda d, s, m: (d ^ 1, s, m))


def straight(d, s, m):
    return (d // 2 * 2 + s, d % 2, m)


def crossed(d, s, m):
    return (d // 2 * 2 + 1 - s, d % 2, m)


def crossed_back(d, s, m):
    return (d // 2 * 2 + s, 1 - d % 2, m)


def to_work(values):
    half = values.shape[0] // 2
    x = lax.axis_index(SEQ)
    mine = lax.dynamic_slice_in_dim(values, x * half, half, axis=0)
    other = lax.dynamic_slice_in_dim(values, (1 - x) * half, half, axis=0)
    return jnp.stack([routed(mine, straight), routed(other, crossed)])


def from_work(values):
    x = lax.axis_index(SEQ)
    mine, other = routed(values[0], straight), routed(values[1], crossed_back)
    halves = jnp.stack([jnp.where(x == 0, mine, other), jnp.where(x == 0, other, mine)])
    return halves.reshape(-1, halves.shape[-1])


def dot(a, b, dims):
    return lax.dot_general(a, b, (dims, ((), ())), preferred_element_type=jnp.float32)


def low(values):
    return values.astype(jnp.bfloat16)


def norm_parts(values):
    average = jnp.mean(values, axis=-1, keepdims=True)
    centred = values - average
    scale = lax.rsqrt(jnp.mean(centred * centred, axis=-1, keepdims=True) + EPSILON)
    return centred * scale, scale


def norm_pull(unit, scale, norm_gain, gradient):
    q = gradient * norm_gain
    return (
        q - jnp.mean(q, axis=-1, keepdims=True) - unit * jnp.mean(q * unit, axis=-1, keepdims=True)
    ) * scale


def all_tokens(values):
    return values.reshape(-1, values.shape[-1])


def total(values):
    return jnp.sum(values.astype(jnp.float32).reshape(-1, values.shape[-1]), axis=0)


def on_device_columns(
    acts,
    cotangent,
    col_mask,
    ln_row_gain,
    ln_row_bias,
    row_wq,
    row_wk,
    row_wv,
    row_bq,
    row_bv,
    row_wo,
    row_bo,
    ln_col_gain,
    ln_col_bias,
    col_wq,
    col_wk,
    col_wv,
    col_bq,
    col_bv,
    col_wo,
    col_bo,
    ln_ffn_gain,
    ln_ffn_bias,
    ffn_w1,
    ffn_b1,
    ffn_w2,
    ffn_b2,
):
    width = acts.shape[-1]
    hs = row_wq.shape[2]
    heads = hs // HD
    fs = ffn_w1.shape[2]
    ranks = lax.axis_size(DP) * lax.axis_size(SEQ)
    mps = lax.axis_size(MP)
    rank = lax.axis_index(DP) * lax.axis_size(SEQ) + lax.axis_index(SEQ)
    c, z = lax.axis_index(DP) % 2, lax.axis_index(MP)
    ch, fh, dh = hs // ranks, fs // ranks, width // ranks

    stream = to_work(acts[0, :, 0]).astype(jnp.float32)
    mask = routed(col_mask[0], straight)
    half = stream.shape[1]

    def share(matrix, rows):
        return lax.dynamic_slice_in_dim(matrix, rank * rows, rows, axis=0)

    col_q_t, col_k_t, col_v_t = col_wq[0].T, col_wk[0].T, col_wv[0].T

    def two_parts(v):
        upper = low(v)
        return upper, low(v - upper.astype(jnp.float32))

    b1_parts, bq_parts, bv_parts = two_parts(ffn_b1[0]), two_parts(col_bq[0]), two_parts(col_bv[0])
    bias_rows = jnp.concatenate(
        [
            jnp.stack(b1_parts),
            jnp.concatenate(bq_parts + bv_parts)[None],
            jnp.zeros((5, width), jnp.bfloat16),
        ]
    )
    pack_attention = jnp.concatenate(
        [share(w, ch) for w in (col_q_t, col_k_t, col_v_t, col_wo[0], row_wo[0])] + [bias_rows]
    )
    pack_ffn = jnp.concatenate([share(ffn_w1[0], dh), share(ffn_w2[0], fh)])

    def gathered(pack):
        away = jnp.stack([shifted(pack, k) for k in range(1, mps)])
        return away, lax.all_gather(away, (DP, SEQ), axis=0, tiled=False)

    away_attention, whole_attention = gathered(pack_attention)
    away_ffn, whole_ffn = gathered(pack_ffn)

    def full_rows(own, whole, at, rows):
        rest = whole[:, :, at : at + rows].swapaxes(0, 1).reshape(mps - 1, ranks * rows, width)
        return jnp.concatenate([own[None], rest])

    wq_t = full_rows(col_q_t, whole_attention, 0, ch).reshape(-1, width)
    wk_t = full_rows(col_k_t, whole_attention, ch, ch).reshape(-1, width)
    wv_t = full_rows(col_v_t, whole_attention, 2 * ch, ch).reshape(-1, width)
    col_o = full_rows(col_wo[0], whole_attention, 3 * ch, ch).reshape(-1, width)
    row_o = full_rows(row_wo[0], whole_attention, 4 * ch, ch).reshape(-1, width)
    w1 = full_rows(ffn_w1[0], whole_ffn, 0, dh)
    w2 = full_rows(ffn_w2[0], whole_ffn, dh, fh).reshape(-1, width)
    bias_away = away_attention[:, 5 * ch :].astype(jnp.float32)
    b1 = jnp.concatenate([ffn_b1[0]] + [bias_away[k, 0] + bias_away[k, 1] for k in range(mps - 1)])
    bq = jnp.concatenate(
        [col_bq[0]]
        + [bias_away[k, 2, :hs] + bias_away[k, 2, hs : 2 * hs] for k in range(mps - 1)]
    )
    bv = jnp.concatenate(
        [col_bv[0]]
        + [
            bias_away[k, 2, 2 * hs : 3 * hs] + bias_away[k, 2, 3 * hs : 4 * hs]
            for k in range(mps - 1)
        ]
    )

    row_unit, row_scale = norm_parts(stream)
    normed = low(row_unit * ln_row_gain[0] + ln_row_bias[0])
    hidden = jnp.stack([normed] + [shifted(normed, k) for k in range(1, mps)])
    row_w = jnp.concatenate([row_wq[0], row_wk[0], row_wv[0]], axis=1)
    row_b = jnp.concatenate([row_bq[0], jnp.zeros_like(row_bq[0]), row_bv[0]])
    qkv = low(dot(hidden, row_w, ((3,), (0,))) + row_b)
    kv_sibling = to_sibling(qkv[:, ::-1, :, hs:])
    block = 2 * half

    def by_head(v):
        v = v.reshape(mps, 2, half, heads, HD)
        return v.transpose(3, 0, 2, 1, 4).reshape(heads, mps * half, 2 * HD)

    def from_head(v):
        v = v.reshape(heads, mps, half, 2, HD)
        return v.transpose(1, 3, 2, 0, 4).reshape(mps, 2, half, hs)

    q_h = by_head(qkv[..., :hs])
    k_h = jnp.concatenate([by_head(qkv[..., hs : 2 * hs]), by_head(kv_sibling[..., :hs])], axis=1)
    v_h = jnp.concatenate([by_head(qkv[..., 2 * hs :]), by_head(kv_sibling[..., hs:])], axis=1)
    score_scale = 1.0 / math.sqrt(HD * 2)
    mask_blocks = mask.reshape(mps, 2, half)
    mask_near = jnp.stack(
        [
            lax.dynamic_index_in_dim(mask_blocks, (z - k) % mps, keepdims=False)
            for k in range(mps)
        ],
        axis=1,
    )
    mask_near = jnp.where(c == 0, mask_near, mask_near[::-1])
    logits = jnp.einsum("hid,hjd->hij", q_h, k_h, preferred_element_type=jnp.float32)
    attention = masked_softmax(logits, mask_near.reshape(-1), score_scale)
    attention_low = low(attention)
    o_h = jnp.einsum("hij,hjd->hid", attention_low, v_h, preferred_element_type=jnp.float32)
    o_blocks = from_head(low(o_h))
    o_from = [o_blocks[0]] + [shifted(o_blocks[k], -k) for k in range(1, mps)]
    row_heads = jnp.concatenate([o_from[-k % mps] for k in range(mps)], axis=-1)
    stream = stream + dot(row_heads, row_o, ((2,), (0,))) + row_bo[0]

    col_unit, col_scale = norm_parts(stream)
    col_normed = low(col_unit * ln_col_gain[0] + ln_col_bias[0])
    col_q = low(dot(col_normed, wq_t, ((2,), (1,))) + bq)
    col_k = low(dot(col_normed, wk_t, ((2,), (1,))))
    col_v = low(dot(col_normed, wv_t, ((2,), (1,))) + bv)
    col_scale_factor = 1.0 / math.sqrt(HD)

    def head_sums(a, b):
        product = a.astype(jnp.float32) * b.astype(jnp.float32)
        return product.reshape(half, mps * heads, HD).sum(axis=-1)

    def spread(v):
        return jnp.repeat(v, HD, axis=-1)

    def pair_softmax(r):
        a = head_sums(col_q[r], col_k[0]) * col_scale_factor
        b = head_sums(col_q[r], col_k[1]) * col_scale_factor
        highest = jnp.maximum(a, b)
        ea, eb = jnp.exp(a - highest), jnp.exp(b - highest)
        return ea / (ea + eb), eb / (ea + eb)

    col_attention = [pair_softmax(r) for r in range(2)]
    value32 = col_v.astype(jnp.float32)
    weight_low = [
        [spread(low(col_attention[r][s]).astype(jnp.float32)) for s in range(2)] for r in range(2)
    ]
    col_heads = low(
        jnp.stack(
            [weight_low[r][0] * value32[0] + weight_low[r][1] * value32[1] for r in range(2)]
        )
    )
    col_stream = stream + dot(col_heads, col_o, ((2,), (0,))) + col_bo[0]

    ffn_unit, ffn_scale = norm_parts(col_stream)
    ffn_normed = low(ffn_unit * ln_ffn_gain[0] + ln_ffn_bias[0])
    up = jnp.concatenate([dot(ffn_normed, w1[k], ((2,), (0,))) for k in range(mps)], axis=-1) + b1
    activated, gelu_pull = jax.vjp(exact_gelu, up)
    activated = low(activated)
    out_stream = col_stream + dot(activated, w2, ((2,), (0,))) + ffn_b2[0]
    out = from_work(low(out_stream)).astype(jnp.float32)

    grad_low = to_work(cotangent[0, :, 0])
    gradient = grad_low.astype(jnp.float32)
    grad_b2 = total(grad_low)
    grad_up = low(gelu_pull(dot(grad_low, w2, ((2,), (1,))))[0])
    grad_b1 = total(grad_up)
    grad_normed = sum(
        dot(grad_up[..., k * fs : (k + 1) * fs], w1[k], ((2,), (1,))) for k in range(mps)
    )
    grad_ln_ffn_gain, grad_ln_ffn_bias = total(grad_normed * ffn_unit), total(grad_normed)
    token_dims = ((0,), (0,))
    grad_ffn = jnp.stack(
        [
            low(dot(all_tokens(ffn_normed), all_tokens(grad_up), token_dims)),
            low(dot(all_tokens(grad_low), all_tokens(activated), token_dims)),
        ],
        axis=1,
    )
    gradient = gradient + norm_pull(ffn_unit, ffn_scale, ln_ffn_gain[0], grad_normed)

    grad_low = low(gradient)
    grad_col_bo = total(grad_low)
    grad_heads = low(dot(grad_low, col_o, ((2,), (1,))))
    grad32 = grad_heads.astype(jnp.float32)
    grad_logits = []
    for r in range(2):
        parts = [head_sums(grad_heads[r], col_v[s]) for s in range(2)]
        inner = col_attention[r][0] * parts[0] + col_attention[r][1] * parts[1]
        grad_logits.append(
            [
                spread(low(col_attention[r][s] * (parts[s] - inner)).astype(jnp.float32))
                for s in range(2)
            ]
        )
    q32, k32 = col_q.astype(jnp.float32), col_k.astype(jnp.float32)
    grad_q = low(
        jnp.stack(
            [
                (grad_logits[r][0] * k32[0] + grad_logits[r][1] * k32[1]) * col_scale_factor
                for r in range(2)
            ]
        )
    )
    grad_k = low(
        jnp.stack(
            [
                (grad_logits[0][s] * q32[0] + grad_logits[1][s] * q32[1]) * col_scale_factor
                for s in range(2)
            ]
        )
    )
    grad_v = low(
        jnp.stack([weight_low[0][s] * grad32[0] + weight_low[1][s] * grad32[1] for s in range(2)])
    )
    grad_col_bq, grad_col_bv = total(grad_q), total(grad_v)
    grad_normed = (
        dot(grad_q, wq_t, ((2,), (0,)))
        + dot(grad_k, wk_t, ((2,), (0,)))
        + dot(grad_v, wv_t, ((2,), (0,)))
    )
    grad_ln_col_gain, grad_ln_col_bias = total(grad_normed * col_unit), total(grad_normed)
    gradient = gradient + norm_pull(col_unit, col_scale, ln_col_gain[0], grad_normed)

    col_grad_low, grad_low = grad_low, low(gradient)
    grad_row_bo = total(grad_low)
    grad_heads = low(dot(grad_low, row_o, ((2,), (1,))))
    d_from = [grad_heads[..., :hs]] + [
        shifted(grad_heads[..., k * hs : (k + 1) * hs], -k) for k in range(1, mps)
    ]
    d_h = by_head(jnp.stack([d_from[-k % mps] for k in range(mps)]))
    normed_flat = all_tokens(col_normed)
    grad_attention = jnp.stack(
        [
            low(dot(normed_flat, all_tokens(g), token_dims)) for g in (grad_q, grad_k, grad_v)
        ]
        + [
            low(dot(all_tokens(col_grad_low), all_tokens(col_heads), token_dims)),
            low(dot(all_tokens(grad_low), all_tokens(row_heads), token_dims)),
        ],
        axis=1,
    )

    grad_weights = jnp.einsum("hid,hjd->hij", d_h, v_h, preferred_element_type=jnp.float32)
    inner = jnp.sum(attention * grad_weights, axis=-1, keepdims=True)
    grad_logits = low(attention * (grad_weights - inner))
    gq_h = (
        jnp.einsum("hij,hjd->hid", grad_logits, k_h, preferred_element_type=jnp.float32)
        * score_scale
    )
    gk_h = (
        jnp.einsum("hij,hid->hjd", grad_logits, q_h, preferred_element_type=jnp.float32)
        * score_scale
    )
    gv_h = jnp.einsum("hij,hid->hjd", attention_low, d_h, preferred_element_type=jnp.float32)
    keys = mps * half
    mine = jnp.concatenate([from_head(gk_h[:, :keys]), from_head(gv_h[:, :keys])], axis=-1)
    theirs = jnp.concatenate([from_head(gk_h[:, keys:]), from_head(gv_h[:, keys:])], axis=-1)
    g_kv = low(mine + to_sibling(low(theirs[:, ::-1])).astype(jnp.float32))
    g_qkv = jnp.concatenate([low(from_head(gq_h)), g_kv], axis=-1)
    g_hidden = dot(g_qkv, row_w, ((3,), (1,)))
    g_send = low(g_hidden)
    g_parts = [g_send[0]] + [shifted(g_send[k], -k) for k in range(1, mps)]
    grad_normed = sum(g.astype(jnp.float32) for g in g_parts)
    gradient = gradient + norm_pull(row_unit, row_scale, ln_row_gain[0], grad_normed)
    grad_acts = from_work(low(gradient)).astype(jnp.float32)
    grad_row_qkv = low(dot(all_tokens(hidden), all_tokens(g_qkv), token_dims))

    rank_axes = (DP, SEQ)

    def reduced(parts):
        mine = lax.psum_scatter(parts, rank_axes, scatter_dimension=0, tiled=True)
        size = mine.shape[-1] // mps
        pieces = [mine[..., :size]] + [
            shifted(mine[..., k * size : (k + 1) * size], -k) for k in range(1, mps)
        ]
        return sum(p.astype(jnp.float32) for p in pieces)

    ffn_total = reduced(grad_ffn)
    attention_total = reduced(grad_attention)
    row_total = lax.psum_scatter(
        grad_row_qkv, rank_axes, scatter_dimension=0, tiled=True
    ).astype(jnp.float32)

    row_hidden_unit = (hidden.astype(jnp.float32) - ln_row_bias[0]) / ln_row_gain[0]
    grad_ln_row_gain, grad_ln_row_bias = total(g_hidden * row_hidden_unit), total(g_hidden)
    here = (jnp.arange(mps) == z).astype(jnp.float32)[:, None]

    def by_shard(v):
        v = v.reshape(mps, -1)
        near = (z - jnp.arange(mps)) % mps
        return sum(
            jnp.where((near[k] == jnp.arange(mps))[:, None], v[k], 0.0) for k in range(mps)
        ).reshape(-1)

    row_bias = [
        (here * total(g_qkv[..., :hs])).reshape(-1),
        (here * total(g_qkv[..., 2 * hs :])).reshape(-1),
    ]
    summed = lax.psum(
        jnp.concatenate(
            [
                grad_ln_row_gain,
                grad_ln_row_bias,
                grad_row_bo,
                grad_ln_col_gain,
                grad_ln_col_bias,
                grad_col_bo,
                grad_ln_ffn_gain,
                grad_ln_ffn_bias,
                grad_b2,
            ]
            + row_bias
            + [by_shard(grad_col_bq), by_shard(grad_col_bv), by_shard(grad_b1)]
        ),
        AXES,
    )
    device = rank * mps + z
    vectors = summed[: 9 * width].reshape(9, ranks * mps, -1)
    vectors = lax.dynamic_index_in_dim(vectors, device, axis=1, keepdims=False)
    biases = summed[9 * width :]

    def of_shard(at, size):
        return lax.dynamic_slice_in_dim(biases[at : at + mps * size], z * size, size)[None]

    def transposed(v):
        return v.T[None]

    return (
        out[None, :, None],
        grad_acts[None, :, None],
        vectors[0][None],
        vectors[1][None],
        row_total[:, :hs][None],
        row_total[:, hs : 2 * hs][None],
        row_total[:, 2 * hs :][None],
        of_shard(0, hs),
        of_shard(width, hs),
        transposed(attention_total[:, 4]),
        vectors[2][None],
        vectors[3][None],
        vectors[4][None],
        attention_total[:, 0][None],
        attention_total[:, 1][None],
        attention_total[:, 2][None],
        of_shard(2 * width, hs),
        of_shard(3 * width, hs),
        transposed(attention_total[:, 3]),
        vectors[5][None],
        vectors[6][None],
        vectors[7][None],
        ffn_total[:, 0][None],
        of_shard(4 * width, fs),
        transposed(ffn_total[:, 1]),
        vectors[8][None],
    )


def solution(mesh):
    placed = (
        P(DP, MP, SEQ, None),
        P(DP, MP, SEQ, None),
        P(DP, None),
        P(),
        P(),
        P(None, None, MP),
        P(None, None, MP),
        P(None, None, MP),
        P(None, MP),
        P(None, MP),
        P(None, MP, None),
        P(),
        P(),
        P(),
        P(None, None, MP),
        P(None, None, MP),
        P(None, None, MP),
        P(None, MP),
        P(None, MP),
        P(None, MP, None),
        P(),
        P(),
        P(),
        P(None, None, MP),
        P(None, MP),
        P(None, MP, None),
        P(),
    )
    in_pairs = mesh.shape[SEQ] == 2 and mesh.shape[DP] % 2 == 0
    return jax.shard_map(
        on_device_columns if in_pairs else on_device,
        mesh=mesh,
        in_specs=placed,
        out_specs=(
            P(DP, MP, SEQ, None),
            P(DP, MP, SEQ, None),
            P(None, (DP, SEQ, MP)),
            P(None, (DP, SEQ, MP)),
            P(None, (DP, SEQ), MP),
            P(None, (DP, SEQ), MP),
            P(None, (DP, SEQ), MP),
            P(None, MP),
            P(None, MP),
            P(None, MP, (DP, SEQ)),
            P(None, (DP, SEQ, MP)),
            P(None, (DP, SEQ, MP)),
            P(None, (DP, SEQ, MP)),
            P(None, (DP, SEQ), MP),
            P(None, (DP, SEQ), MP),
            P(None, (DP, SEQ), MP),
            P(None, MP),
            P(None, MP),
            P(None, MP, (DP, SEQ)),
            P(None, (DP, SEQ, MP)),
            P(None, (DP, SEQ, MP)),
            P(None, (DP, SEQ, MP)),
            P(None, (DP, SEQ), MP),
            P(None, MP),
            P(None, MP, (DP, SEQ)),
            P(None, (DP, SEQ, MP)),
        ),
        check_vma=False,
    )
```

profile of v0, /device:TPU:0, one launch (start us, length us, event | category | flops | bytes accessed | tf_op | source)
XLA Modules:
  0.0 507.6 jit_solution(4785809523951014615)
XLA Ops:
  11.4 5.1 %collective-permute-start.12 = (bf16[128,768]{1,0:T(8,128)(2,1)S(1)}, bf16[128,768]{1,0:T(8,128)(2,1)S(1)}, u32[]{:S(2)}, u32[]{:S(2)}) collective-permute-start(bf16[128,768]{1,0:T(8,128)(2,1)S(1)} %concatenate.80), channel_id=1, source_target_pairs={{0,3},{1,0},{2,1},{3,2},{4,7},{5,4},{6,5},{7,6},{8,11},{9,8},{10,9... | collective-permute-start | bytes 589832 | tf_op jit(solution)/shard_map/ppermute | solution.py:538
  17.5 4.3 collective-permute-done.12
  21.8 11.3 %collective-permute-done.11 = bf16[128,768]{1,0:T(8,128)(2,1)S(1)} collective-permute-done((bf16[128,768]{1,0:T(8,128)(2,1)S(1)}, bf16[128,768]{1,0:T(8,128)(2,1)S(1)}, u32[]{:S(2)}, u32[]{:S(2)}) %collective-permute-start.11) | collective-permute-done | bytes 196640 | tf_op jit(solution)/shard_map/ppermute | solution.py:538
  35.7 2.5 collective-permute-start.14
  38.2 1.9 collective-permute-start.13
  40.1 3.7 collective-permute-done.15
  43.8 19.7 %collective-permute-done.14 = bf16[192,768]{1,0:T(8,128)(2,1)S(1)} collective-permute-done((bf16[192,768]{1,0:T(8,128)(2,1)S(1)}, bf16[192,768]{1,0:T(8,128)(2,1)S(1)}, u32[]{:S(2)}, u32[]{:S(2)}) %collective-permute-start.14) | collective-permute-done | bytes 294944 | tf_op jit(solution)/shard_map/ppermute | solution.py:538
  66.1 4.1 collective-permute-start.1
  71.0 3.0 collective-permute-start.18
  82.5 9.2 %collective-permute-done.5 = bf16[2,128,768]{2,1,0:T(8,128)(2,1)S(1)} collective-permute-done((bf16[2,128,768]{2,1,0:T(8,128)(2,1)S(1)}, bf16[2,128,768]{2,1,0:T(8,128)(2,1)S(1)}, u32[]{:S(2)}, u32[]{:S(2)}) %collective-permute-start.5) | collective-permute-done | bytes 393248 | tf_op jit(solution)/shard_map/ppermute | solution.py:538
  91.7 22.8 %collective-permute-done.4 = bf16[2,128,768]{2,1,0:T(8,128)(2,1)S(1)} collective-permute-done((bf16[2,128,768]{2,1,0:T(8,128)(2,1)S(1)}, bf16[2,128,768]{2,1,0:T(8,128)(2,1)S(1)}, u32[]{:S(2)}, u32[]{:S(2)}) %collective-permute-start.4) | collective-permute-done | bytes 393248 | tf_op jit(solution)/shard_map/ppermute | solution.py:538
  115.3 2.2 add_convert_fusion.1
  124.3 5.7 %fusion.133 = (f32[3,512]{1,0:T(4,128)S(1)}, f32[3,512,1024]{2,1,0:T(8,128)}) fusion(pred[1024]{0:T(1024)(128)(4,1)} %bitcast.535, bf16[3,512,128]{1,2,0:T(8,128)(2,1)S(1)} %reshape.627, bf16[3,512,128]{2,1,0:T(8,128)(2,1)S(1)} %copy.323, bf16[3,512,128]{2,1,0:T(8,128)(2,1)S(1)} %copy.322), kind=kOutput, calls=%fused_computation.375 | convolution fusion | flops 410518528 | bytes 7478272 | tf_op jit(solution)/shard_map/sub | solution.py:114
  130.0 3.8 fusion.35
  135.9 2.1 collective-permute-start.8
  138.0 3.0 collective-permute-start.9
  141.1 2.5 slice_bitcast_fusion.3
  146.9 2.0 collective-permute-done.8
  163.2 3.6 slice_bitcast_fusion
  168.9 8.0 %multiply_convert_fusion.1 = (bf16[2,128,3072]{2,1,0:T(8,128)(2,1)}, f32[2,128,3072]{2,1,0:T(8,128)S(1)}) fusion(f32[3072]{0:T(1024)S(1)} %copy-done.79, f32[2,128,768]{2,1,0:T(8,128)S(1)} %fusion.142, f32[2,128,768]{2,1,0:T(8,128)S(1)} %fusion.141, f32[2,128,768]{2,1,0:T(8,128)S(1)} %fusion.140, f32[2,128,768]{2,1,0:T(8,128)S(1)} %fusion.40), kind=kLoop, calls=%fused_computation.20 | loop fusion | flops 54263808 | bytes 7876608 | tf_op jit(solution)/shard_map/convert_element_type | solution.py:582
  177.3 5.2 %convert_reduce_fusion = (f32[3072]{0:T(1024)}, bf16[2,128,3072]{2,1,0:T(8,128)(2,1)S(1)}) fusion(f32[2,128,3072]{2,1,0:T(8,128)S(1)} %get-tuple-element.177, bf16[3072,768,1]{1,0,2:T(8,128)(2,1)S(1)} %bitcast.445, bf16[1,128,768]{2,1,0:T(8,128)(2,1)} %bitcast.122, bf16[1,128,768]{2,1,0:T(8,128)(2,1)} %bitcast.120, f32[3072]{0:T(1024)S(1)} %copy-done.79, ...), kind=kOutput, calls=%fused_computation.17 | convolution fusion | flops 1223881728 | bytes 13000704 | tf_op jit(solution)/shard_map/dot_general | solution.py:578
  185.4 2.1 convert_reduce_fusion.7
  217.4 2.0 multiply_convert_fusion.3
  224.6 4.2 collective-permute-start.22
  229.6 3.4 collective-permute-done.22
  233.2 7.1 %collective-permute-done.21 = bf16[2,128,192]{2,1,0:T(8,128)(2,1)S(1)} collective-permute-done((bf16[2,128,192]{2,1,0:T(8,128)(2,1)S(1)}, bf16[2,128,192]{2,1,0:T(8,128)(2,1)S(1)}, u32[]{:S(2)}, u32[]{:S(2)}) %collective-permute-start.21) | collective-permute-done | bytes 98336 | tf_op jit(solution)/shard_map/ppermute | solution.py:538
  243.3 4.4 fusion.14
  247.7 6.5 %multiply_reduce_fusion = (f32[3,512]{1,0:T(4,128)}, f32[3,512,1024]{2,1,0:T(8,128)}) fusion(f32[3,512,1024]{2,1,0:T(8,128)} %get-tuple-element.317, f32[3,512]{1,0:T(4,128)S(1)} %copy-done.104, bf16[3,512,128]{1,2,0:T(8,128)(2,1)S(1)} %copy-done.72, bf16[3,512,128]{2,1,0:T(8,128)(2,1)S(1)} %copy-done.69, bf16[3,512,128]{2,1,0:T(8,128)(2,1)S(1)} %copy-done.67), kind=kOutput, calls=%fused_computation.5 | convolution fusion | flops 408943104 | bytes 13774848 | tf_op jit(solution)/shard_map/hid,hjd->hij/dot_general | solution.py:865
  255.3 5.2 %multiply_convert_fusion = bf16[3,512,1024]{2,1,0:T(8,128)(2,1)S(1)} fusion(f32[3,512,1024]{2,1,0:T(8,128)} %get-tuple-element.333, f32[3,512]{1,0:T(4,128)} %get-tuple-element.332, f32[3,512,1024]{2,1,0:T(8,128)} %get-tuple-element.317, f32[3,512]{1,0:T(4,128)S(1)} %copy-done.104), kind=kLoop, calls=%fused_computation.4 | loop fusion | flops 6291456 | bytes 15740928 | tf_op jit(solution)/shard_map/convert_element_type | solution.py:582
  265.0 2.0 pad_maximum_fusion.3
  267.0 2.1 rev.16
  272.6 4.4 convert_reduce_fusion.6
  288.0 2.4 bitcast_convert_fusion.7
  292.1 2.7 fusion.21
  301.0 4.7 fusion.3
  305.7 3.7 fusion.2
  309.4 8.3 %pad_maximum_fusion = bf16[768,2,3072]{2,0,1:T(8,128)(2,1)} fusion(bf16[768,1,3072]{2,0,1:T(8,128)(2,1)} %fusion.3, bf16[768,1,3072]{2,0,1:T(8,128)(2,1)} %fusion.2), kind=kLoop, calls=%fused_computation.1 | loop fusion | flops 4718592 | bytes 18874368 | tf_op jit(solution)/shard_map/stack | solution.py:794
  322.7 3.8 fusion.31
  327.5 3.4 collective-permute-start.17
  337.5 3.5 fusion.116
  344.3 2.0 collective-permute-start.25
  364.5 42.5 %psum.7 = f32[13056]{0:T(1024)} all-reduce(f32[13056]{0:T(1024)} %constant_dynamic-update-slice_fusion.1), channel_id=1, replica_groups=mesh['dp'=4,'seq'=2,'mp'=4] {'dp','seq','mp'}, use_global_device_ids=true, to_apply=%region_38.39 | all-reduce | flops 13056 | bytes 104448 | tf_op jit(solution)/shard_map/psum | solution.py:921
  410.4 3.6 collective-permute-start.28
  426.0 43.0 %reduce-scatter.8.cloned.1.call-done = bf16[96,2,3072]{2,0,1:T(8,128)(2,1)} async-done(((bf16[768,2,3072]{2,0,1:T(8,128)(2,1)}), bf16[96,2,3072]{2,0,1:T(8,128)(2,1)}) %reduce-scatter.8.cloned.1.call-update) | async-done | bytes 1179664 | tf_op jit(solution)/shard_map/reduce_scatter | solution.py:893
  470.2 3.4 collective-permute-start.32
  478.0 3.1 collective-permute-done.32
  481.0 7.4 %collective-permute-done.34 = bf16[96,2,768]{2,0,1:T(8,128)(2,1)S(1)} collective-permute-done((bf16[96,2,768]{2,0,1:T(8,128)(2,1)S(1)}, bf16[96,2,768]{2,0,1:T(8,128)(2,1)S(1)}, u32[]{:S(2)}, u32[]{:S(2)}) %collective-permute-start.34) | collective-permute-done | bytes 294944 | tf_op jit(solution)/shard_map/ppermute | solution.py:538
  488.4 10.5 %collective-permute-done.33 = bf16[96,2,768]{2,0,1:T(8,128)(2,1)S(1)} collective-permute-done((bf16[96,2,768]{2,0,1:T(8,128)(2,1)S(1)}, bf16[96,2,768]{2,0,1:T(8,128)(2,1)S(1)}, u32[]{:S(2)}, u32[]{:S(2)}) %collective-permute-start.33) | collective-permute-done | bytes 294944 | tf_op jit(solution)/shard_map/ppermute | solution.py:538
  (603 shorter events, 173.9 us)
Async XLA Ops:
  7.2 133.9 %all-gather.5.cloned.1.call-start = ((), (), s32[]{:S(2)}) async-start(), calls=%async_computation.6 | async-start | bytes 5308416 | tf_op jit(solution)/shard_map/all_gather | solution.py:674
  9.7 55.0 %copy-start.140 = (s32[1,1024]{1,0:T(1,128)S(1)}, s32[1,1024]{1,0:T(1,128)}, u32[]{:S(2)}) copy-start(s32[1,1024]{1,0:T(1,128)} %param.29) | copy-start | bytes 12292
  10.5 54.9 %copy-start.59 = (bf16[1,256,1,768]{3,1,2,0:T(8,128)(2,1)S(1)}, bf16[1,256,1,768]{3,1,2,0:T(8,128)(2,1)}, u32[]{:S(2)}) copy-start(bf16[1,256,1,768]{3,1,2,0:T(8,128)(2,1)} %param.27) | copy-start | bytes 1179652
  11.4 10.4 %collective-permute-start.12 = (bf16[128,768]{1,0:T(8,128)(2,1)S(1)}, bf16[128,768]{1,0:T(8,128)(2,1)S(1)}, u32[]{:S(2)}, u32[]{:S(2)}) collective-permute-start(bf16[128,768]{1,0:T(8,128)(2,1)S(1)} %concatenate.80), channel_id=1, source_target_pairs={{0,3},{1,0},{2,1},{3,2},{4,7},{5,4},{6,5},{7,6},{8,11},{9,8},{10,9... | collective-permute-start | bytes 589832 | tf_op jit(solution)/shard_map/ppermute | solution.py:538
  16.5 16.7 %collective-permute-start.11 = (bf16[128,768]{1,0:T(8,128)(2,1)S(1)}, bf16[128,768]{1,0:T(8,128)(2,1)S(1)}, u32[]{:S(2)}, u32[]{:S(2)}) collective-permute-start(bf16[128,768]{1,0:T(8,128)(2,1)S(1)} %concatenate.80), channel_id=1, source_target_pairs={{0,2},{1,3},{2,0},{3,1},{4,6},{5,7},{6,4},{7,5},{8,10},{9,11},{10,... | collective-permute-start | bytes 589832 | tf_op jit(solution)/shard_map/ppermute | solution.py:538
  16.5 16.7 %collective-permute-start.10 = (bf16[128,768]{1,0:T(8,128)(2,1)S(1)}, bf16[128,768]{1,0:T(8,128)(2,1)S(1)}, u32[]{:S(2)}, u32[]{:S(2)}) collective-permute-start(bf16[128,768]{1,0:T(8,128)(2,1)S(1)} %concatenate.80), channel_id=1, source_target_pairs={{0,1},{1,2},{2,3},{3,0},{4,5},{5,6},{6,7},{7,4},{8,9},{9,10},{10,1... | collective-permute-start | bytes 589832 | tf_op jit(solution)/shard_map/ppermute | solution.py:538
  34.2 129.0 %all-gather.7.cloned.1.call-start = ((), (), s32[]{:S(2)}) async-start(), calls=%async_computation.7 | async-start | bytes 7962624 | tf_op jit(solution)/shard_map/all_gather | solution.py:674
  35.3 8.5 %collective-permute-start.15 = (bf16[192,768]{1,0:T(8,128)(2,1)S(1)}, bf16[192,768]{1,0:T(8,128)(2,1)S(1)}, u32[]{:S(2)}, u32[]{:S(2)}) collective-permute-start(bf16[192,768]{1,0:T(8,128)(2,1)S(1)} %pad_maximum_fusion.27), channel_id=1, source_target_pairs={{0,3},{1,0},{2,1},{3,2},{4,7},{5,4},{6,5},{7,6},{8,11},{9,8},{10,9... | collective-permute-start | bytes 884744 | tf_op jit(solution)/shard_map/ppermute | solution.py:538
  35.7 27.8 %collective-permute-start.14 = (bf16[192,768]{1,0:T(8,128)(2,1)S(1)}, bf16[192,768]{1,0:T(8,128)(2,1)S(1)}, u32[]{:S(2)}, u32[]{:S(2)}) collective-permute-start(bf16[192,768]{1,0:T(8,128)(2,1)S(1)} %pad_maximum_fusion.27), channel_id=1, source_target_pairs={{0,2},{1,3},{2,0},{3,1},{4,6},{5,7},{6,4},{7,5},{8,10},{9,11},{10,... | collective-permute-start | bytes 884744 | tf_op jit(solution)/shard_map/ppermute | solution.py:538
  38.2 25.3 %collective-permute-start.13 = (bf16[192,768]{1,0:T(8,128)(2,1)S(1)}, bf16[192,768]{1,0:T(8,128)(2,1)S(1)}, u32[]{:S(2)}, u32[]{:S(2)}) collective-permute-start(bf16[192,768]{1,0:T(8,128)(2,1)S(1)} %pad_maximum_fusion.27), channel_id=1, source_target_pairs={{0,1},{1,2},{2,3},{3,0},{4,5},{5,6},{6,7},{7,4},{8,9},{9,10},{10,1... | collective-permute-start | bytes 884744 | tf_op jit(solution)/shard_map/ppermute | solution.py:538
  63.5 51.8 %copy-start.132 = (bf16[1,768,192]{1,2,0:T(8,128)(2,1)S(1)}, bf16[1,768,192]{1,2,0:T(8,128)(2,1)}, u32[]{:S(2)}) copy-start(bf16[1,768,192]{1,2,0:T(8,128)(2,1)} %param.34) | copy-start | bytes 884740
  64.6 356.2 %reduce-scatter.4.cloned.1.call-start = ((), (), s32[]{:S(2)}) async-start(), calls=%async_computation.3 | async-start | bytes 1105920 | tf_op jit(solution)/shard_map/reduce_scatter | solution.py:902
  64.7 12.7 %collective-permute-start.2 = (s32[1024]{0:T(1024)S(1)}, s32[1024]{0:T(1024)S(1)}, u32[]{:S(2)}, u32[]{:S(2)}) collective-permute-start(s32[1024]{0:T(1024)S(1)} %bitcast.551), channel_id=1, source_target_pairs={{0,0},{1,1},{2,2},{3,3},{4,8},{5,9},{6,10},{7,11},{8,4},{9,5},{10,... | collective-permute-start | bytes 12296 | tf_op jit(solution)/shard_map/ppermute | solution.py:538
  65.4 12.5 %collective-permute-start = (bf16[128,768]{1,0:T(8,128)(2,1)S(1)}, bf16[128,768]{1,0:T(8,128)(2,1)S(1)}, u32[]{:S(2)}, u32[]{:S(2)}) collective-permute-start(bf16[128,768]{1,0:T(8,128)(2,1)S(1)} %get-tuple-element.257), channel_id=1, source_target_pairs={{0,0},{1,1},{2,2},{3,3},{4,8},{5,9},{6,10},{7,11},{8,4},{9,5},{10,... | collective-permute-start | bytes 589832 | tf_op jit(solution)/shard_map/ppermute | solution.py:538
  66.1 11.9 %collective-permute-start.1 = (bf16[128,768]{1,0:T(8,128)(2,1)S(1)}, bf16[128,768]{1,0:T(8,128)(2,1)S(1)}, u32[]{:S(2)}, u32[]{:S(2)}) collective-permute-start(bf16[128,768]{1,0:T(8,128)(2,1)S(1)} %get-tuple-element.258), channel_id=1, source_target_pairs={{0,8},{1,9},{2,10},{3,11},{4,0},{5,1},{6,2},{7,3},{8,12},{9,13},{1... | collective-permute-start | bytes 589832 | tf_op jit(solution)/shard_map/ppermute | solution.py:538
  71.0 106.3 %collective-permute-start.18 = (bf16[128,768]{1,0:T(8,128)(2,1)}, bf16[128,768]{1,0:T(8,128)(2,1)}, u32[]{:S(2)}, u32[]{:S(2)}) collective-permute-start(bf16[128,768]{1,0:T(8,128)(2,1)} %get-tuple-element.247), channel_id=1, source_target_pairs={{0,0},{1,1},{2,2},{3,3},{4,8},{5,9},{6,10},{7,11},{8,4},{9,5},{10,... | collective-permute-start | bytes 589832 | tf_op jit(solution)/shard_map/ppermute | solution.py:538
  74.0 103.3 %collective-permute-start.19 = (bf16[128,768]{1,0:T(8,128)(2,1)}, bf16[128,768]{1,0:T(8,128)(2,1)}, u32[]{:S(2)}, u32[]{:S(2)}) collective-permute-start(bf16[128,768]{1,0:T(8,128)(2,1)} %get-tuple-element.248), channel_id=1, source_target_pairs={{0,8},{1,9},{2,10},{3,11},{4,0},{5,1},{6,2},{7,3},{8,12},{9,13},{1... | collective-permute-start | bytes 589832 | tf_op jit(solution)/shard_map/ppermute | solution.py:538
  74.8 42.7 %copy-start.81 = (f32[768]{0:T(1024)}, f32[768]{0:T(1024)S(1)}, u32[]{:S(2)}) copy-start(f32[768]{0:T(1024)S(1)} %reduce.18) | copy-start | bytes 9220
  77.9 70.9 %copy-start.7 = (bf16[128,768]{1,0:T(8,128)(2,1)}, bf16[128,768]{1,0:T(8,128)(2,1)S(1)}, u32[]{:S(2)}) copy-start(bf16[128,768]{1,0:T(8,128)(2,1)S(1)} %collective-permute-done) | copy-start | bytes 589828
  77.9 70.9 %copy-start.9 = (bf16[128,768]{1,0:T(8,128)(2,1)}, bf16[128,768]{1,0:T(8,128)(2,1)S(1)}, u32[]{:S(2)}) copy-start(bf16[128,768]{1,0:T(8,128)(2,1)S(1)} %collective-permute-done.1) | copy-start | bytes 589828
  78.6 13.1 %collective-permute-start.5 = (bf16[2,128,768]{2,1,0:T(8,128)(2,1)S(1)}, bf16[2,128,768]{2,1,0:T(8,128)(2,1)S(1)}, u32[]{:S(2)}, u32[]{:S(2)}) collective-permute-start(bf16[2,128,768]{2,1,0:T(8,128)(2,1)S(1)} %fusion.48), channel_id=1, source_target_pairs={{0,3},{1,0},{2,1},{3,2},{4,7},{5,4},{6,5},{7,6},{8,11},{9,8},{10,9... | collective-permute-start | bytes 1179656 | tf_op jit(solution)/shard_map/ppermute | solution.py:538
  80.2 34.3 %collective-permute-start.4 = (bf16[2,128,768]{2,1,0:T(8,128)(2,1)S(1)}, bf16[2,128,768]{2,1,0:T(8,128)(2,1)S(1)}, u32[]{:S(2)}, u32[]{:S(2)}) collective-permute-start(bf16[2,128,768]{2,1,0:T(8,128)(2,1)S(1)} %fusion.48), channel_id=1, source_target_pairs={{0,2},{1,3},{2,0},{3,1},{4,6},{5,7},{6,4},{7,5},{8,10},{9,11},{10,... | collective-permute-start | bytes 1179656 | tf_op jit(solution)/shard_map/ppermute | solution.py:538
  80.2 34.3 %collective-permute-start.3 = (bf16[2,128,768]{2,1,0:T(8,128)(2,1)S(1)}, bf16[2,128,768]{2,1,0:T(8,128)(2,1)S(1)}, u32[]{:S(2)}, u32[]{:S(2)}) collective-permute-start(bf16[2,128,768]{2,1,0:T(8,128)(2,1)S(1)} %fusion.48), channel_id=1, source_target_pairs={{0,1},{1,2},{2,3},{3,0},{4,5},{5,6},{6,7},{7,4},{8,9},{9,10},{10,1... | collective-permute-start | bytes 1179656 | tf_op jit(solution)/shard_map/ppermute | solution.py:538
  118.5 4.2 collective-permute-start.6
  135.5 11.4 %collective-permute-start.7 = (bf16[2,128,192]{2,1,0:T(8,128)(2,1)S(1)}, bf16[2,128,192]{2,1,0:T(8,128)(2,1)S(1)}, u32[]{:S(2)}, u32[]{:S(2)}) collective-permute-start(bf16[2,128,192]{2,1,0:T(8,128)(2,1)S(1)} %copy.332), channel_id=1, source_target_pairs={{0,1},{1,2},{2,3},{3,0},{4,5},{5,6},{6,7},{7,4},{8,9},{9,10},{10,1... | collective-permute-start | bytes 294920 | tf_op jit(solution)/shard_map/ppermute | solution.py:538
  135.9 12.9 %collective-permute-start.8 = (bf16[2,128,192]{2,1,0:T(8,128)(2,1)S(1)}, bf16[2,128,192]{2,1,0:T(8,128)(2,1)S(1)}, u32[]{:S(2)}, u32[]{:S(2)}) collective-permute-start(bf16[2,128,192]{2,1,0:T(8,128)(2,1)S(1)} %copy.334), channel_id=1, source_target_pairs={{0,2},{1,3},{2,0},{3,1},{4,6},{5,7},{6,4},{7,5},{8,10},{9,11},{10,... | collective-permute-start | bytes 294920 | tf_op jit(solution)/shard_map/ppermute | solution.py:538
  138.0 10.8 %collective-permute-start.9 = (bf16[2,128,192]{2,1,0:T(8,128)(2,1)S(1)}, bf16[2,128,192]{2,1,0:T(8,128)(2,1)S(1)}, u32[]{:S(2)}, u32[]{:S(2)}) collective-permute-start(bf16[2,128,192]{2,1,0:T(8,128)(2,1)S(1)} %copy.336), channel_id=1, source_target_pairs={{0,3},{1,0},{2,1},{3,2},{4,7},{5,4},{6,5},{7,6},{8,11},{9,8},{10,9... | collective-permute-start | bytes 294920 | tf_op jit(solution)/shard_map/ppermute | solution.py:538
  224.6 8.5 %collective-permute-start.22 = (bf16[2,128,192]{2,1,0:T(8,128)(2,1)}, bf16[2,128,192]{2,1,0:T(8,128)(2,1)S(1)}, u32[]{:S(2)}, u32[]{:S(2)}) collective-permute-start(bf16[2,128,192]{2,1,0:T(8,128)(2,1)} %get-tuple-element.244), channel_id=1, source_target_pairs={{0,3},{1,0},{2,1},{3,2},{4,7},{5,4},{6,5},{7,6},{8,11},{9,8},{10,9... | collective-permute-start | bytes 294920 | tf_op jit(solution)/shard_map/ppermute | solution.py:538
  228.8 11.4 %collective-permute-start.21 = (bf16[2,128,192]{2,1,0:T(8,128)(2,1)S(1)}, bf16[2,128,192]{2,1,0:T(8,128)(2,1)S(1)}, u32[]{:S(2)}, u32[]{:S(2)}) collective-permute-start(bf16[2,128,192]{2,1,0:T(8,128)(2,1)S(1)} %get-tuple-element.245), channel_id=1, source_target_pairs={{0,2},{1,3},{2,0},{3,1},{4,6},{5,7},{6,4},{7,5},{8,10},{9,11},{10,... | collective-permute-start | bytes 294920 | tf_op jit(solution)/shard_map/ppermute | solution.py:538
  228.8 11.6 %collective-permute-start.20 = (bf16[2,128,192]{2,1,0:T(8,128)(2,1)}, bf16[2,128,192]{2,1,0:T(8,128)(2,1)S(1)}, u32[]{:S(2)}, u32[]{:S(2)}) collective-permute-start(bf16[2,128,192]{2,1,0:T(8,128)(2,1)} %get-tuple-element.246), channel_id=1, source_target_pairs={{0,1},{1,2},{2,3},{3,0},{4,5},{5,6},{6,7},{7,4},{8,9},{9,10},{10,1... | collective-permute-start | bytes 294920 | tf_op jit(solution)/shard_map/ppermute | solution.py:538
  269.1 16.3 %collective-permute-start.23 = (bf16[4,2,128,384]{2,3,1,0:T(8,128)(2,1)}, bf16[4,2,128,384]{2,3,1,0:T(8,128)(2,1)}, u32[]{:S(2)}, u32[]{:S(2)}) collective-permute-start(bf16[4,2,128,384]{2,3,1,0:T(8,128)(2,1)} %rev.16), channel_id=1, source_target_pairs={{0,8},{1,9},{2,10},{3,11},{4,12},{5,13},{6,14},{7,15},{8,0},{9,1},... | collective-permute-start | bytes 2359304 | tf_op jit(solution)/shard_map/ppermute | solution.py:538
  290.4 132.1 %reduce-scatter.6.cloned.1.call-start = ((), (), s32[]{:S(2)}) async-start(), calls=%async_computation.4 | async-start | bytes 6635520 | tf_op jit(solution)/shard_map/reduce_scatter | solution.py:893
  299.6 169.5 %reduce-scatter.8.cloned.1.call-start = ((), (), s32[]{:S(2)}) async-start(), calls=%async_computation.5 | async-start | bytes 10616832 | tf_op jit(solution)/shard_map/reduce_scatter | solution.py:893
  326.7 7.6 %collective-permute-start.16 = (bf16[128,768]{1,0:T(8,128)(2,1)S(1)}, bf16[128,768]{1,0:T(8,128)(2,1)S(1)}, u32[]{:S(2)}, u32[]{:S(2)}) collective-permute-start(bf16[128,768]{1,0:T(8,128)(2,1)S(1)} %get-tuple-element.251), channel_id=1, source_target_pairs={{0,0},{1,1},{2,2},{3,3},{4,8},{5,9},{6,10},{7,11},{8,4},{9,5},{10,... | collective-permute-start | bytes 589832 | tf_op jit(solution)/shard_map/ppermute | solution.py:538
  327.5 6.8 %collective-permute-start.17 = (bf16[128,768]{1,0:T(8,128)(2,1)S(1)}, bf16[128,768]{1,0:T(8,128)(2,1)S(1)}, u32[]{:S(2)}, u32[]{:S(2)}) collective-permute-start(bf16[128,768]{1,0:T(8,128)(2,1)S(1)} %get-tuple-element.252), channel_id=1, source_target_pairs={{0,4},{1,5},{2,6},{3,7},{4,12},{5,13},{6,14},{7,15},{8,0},{9,1},{1... | collective-permute-start | bytes 589832 | tf_op jit(solution)/shard_map/ppermute | solution.py:538
  337.5 69.6 %copy-start.8 = (bf16[128,768]{1,0:T(8,128)(2,1)S(1)}, bf16[128,768]{1,0:T(8,128)(2,1)}, u32[]{:S(2)}) copy-start(bf16[128,768]{1,0:T(8,128)(2,1)} %copy-done.7) | copy-start | bytes 589828
  337.5 69.6 %copy-start.10 = (bf16[128,768]{1,0:T(8,128)(2,1)S(1)}, bf16[128,768]{1,0:T(8,128)(2,1)}, u32[]{:S(2)}) copy-start(bf16[128,768]{1,0:T(8,128)(2,1)} %copy-done.9) | copy-start | bytes 589828
  342.2 64.9 %collective-permute-start.24 = (bf16[2,128,768]{2,1,0:T(8,128)(2,1)S(1)}, bf16[2,128,768]{2,1,0:T(8,128)(2,1)S(1)}, u32[]{:S(2)}, u32[]{:S(2)}) collective-permute-start(bf16[2,128,768]{2,1,0:T(8,128)(2,1)S(1)} %get-tuple-element.201), channel_id=1, source_target_pairs={{0,3},{1,0},{2,1},{3,2},{4,7},{5,4},{6,5},{7,6},{8,11},{9,8},{10,9... | collective-permute-start | bytes 1179656 | tf_op jit(solution)/shard_map/ppermute | solution.py:538
  343.6 63.5 %collective-permute-start.26 = (bf16[2,128,768]{2,1,0:T(8,128)(2,1)S(1)}, bf16[2,128,768]{2,1,0:T(8,128)(2,1)S(1)}, u32[]{:S(2)}, u32[]{:S(2)}) collective-permute-start(bf16[2,128,768]{2,1,0:T(8,128)(2,1)S(1)} %get-tuple-element.202), channel_id=1, source_target_pairs={{0,1},{1,2},{2,3},{3,0},{4,5},{5,6},{6,7},{7,4},{8,9},{9,10},{10,1... | collective-permute-start | bytes 1179656 | tf_op jit(solution)/shard_map/ppermute | solution.py:538
  344.3 62.8 %collective-permute-start.25 = (bf16[2,128,768]{2,1,0:T(8,128)(2,1)S(1)}, bf16[2,128,768]{2,1,0:T(8,128)(2,1)S(1)}, u32[]{:S(2)}, u32[]{:S(2)}) collective-permute-start(bf16[2,128,768]{2,1,0:T(8,128)(2,1)S(1)} %get-tuple-element.203), channel_id=1, source_target_pairs={{0,2},{1,3},{2,0},{3,1},{4,6},{5,7},{6,4},{7,5},{8,10},{9,11},{10,... | collective-permute-start | bytes 1179656 | tf_op jit(solution)/shard_map/ppermute | solution.py:538
  409.7 8.2 %collective-permute-start.27 = (bf16[128,768]{1,0:T(8,128)(2,1)S(1)}, bf16[128,768]{1,0:T(8,128)(2,1)S(1)}, u32[]{:S(2)}, u32[]{:S(2)}) collective-permute-start(bf16[128,768]{1,0:T(8,128)(2,1)S(1)} %get-tuple-element.241), channel_id=1, source_target_pairs={{0,0},{1,1},{2,2},{3,3},{4,8},{5,9},{6,10},{7,11},{8,4},{9,5},{10,... | collective-permute-start | bytes 589832 | tf_op jit(solution)/shard_map/ppermute | solution.py:538
  410.4 8.9 %collective-permute-start.28 = (bf16[128,768]{1,0:T(8,128)(2,1)S(1)}, bf16[128,768]{1,0:T(8,128)(2,1)S(1)}, u32[]{:S(2)}, u32[]{:S(2)}) collective-permute-start(bf16[128,768]{1,0:T(8,128)(2,1)S(1)} %get-tuple-element.242), channel_id=1, source_target_pairs={{0,4},{1,5},{2,6},{3,7},{4,12},{5,13},{6,14},{7,15},{8,0},{9,1},{1... | collective-permute-start | bytes 589832 | tf_op jit(solution)/shard_map/ppermute | solution.py:538
  424.0 49.7 %collective-permute-start.29 = (bf16[96,5,192]{2,0,1:T(8,128)(2,1)S(1)}, bf16[96,5,192]{2,0,1:T(8,128)(2,1)S(1)}, u32[]{:S(2)}, u32[]{:S(2)}) collective-permute-start(bf16[96,5,192]{2,0,1:T(8,128)(2,1)S(1)} %get-tuple-element.228), channel_id=1, source_target_pairs={{0,3},{1,0},{2,1},{3,2},{4,7},{5,4},{6,5},{7,6},{8,11},{9,8},{10,9... | collective-permute-start | bytes 552968 | tf_op jit(solution)/shard_map/ppermute | solution.py:538
  424.9 49.8 %collective-permute-start.31 = (bf16[96,5,192]{2,0,1:T(8,128)(2,1)S(1)}, bf16[96,5,192]{2,0,1:T(8,128)(2,1)S(1)}, u32[]{:S(2)}, u32[]{:S(2)}) collective-permute-start(bf16[96,5,192]{2,0,1:T(8,128)(2,1)S(1)} %get-tuple-element.229), channel_id=1, source_target_pairs={{0,1},{1,2},{2,3},{3,0},{4,5},{5,6},{6,7},{7,4},{8,9},{9,10},{10,1... | collective-permute-start | bytes 552968 | tf_op jit(solution)/shard_map/ppermute | solution.py:538
  426.0 48.7 %collective-permute-start.30 = (bf16[96,5,192]{2,0,1:T(8,128)(2,1)S(1)}, bf16[96,5,192]{2,0,1:T(8,128)(2,1)S(1)}, u32[]{:S(2)}, u32[]{:S(2)}) collective-permute-start(bf16[96,5,192]{2,0,1:T(8,128)(2,1)S(1)} %get-tuple-element.230), channel_id=1, source_target_pairs={{0,2},{1,3},{2,0},{3,1},{4,6},{5,7},{6,4},{7,5},{8,10},{9,11},{10,... | collective-permute-start | bytes 552968 | tf_op jit(solution)/shard_map/ppermute | solution.py:538
  470.2 10.8 %collective-permute-start.32 = (bf16[96,2,768]{2,0,1:T(8,128)(2,1)S(1)}, bf16[96,2,768]{2,0,1:T(8,128)(2,1)S(1)}, u32[]{:S(2)}, u32[]{:S(2)}) collective-permute-start(bf16[96,2,768]{2,0,1:T(8,128)(2,1)S(1)} %get-tuple-element.204), channel_id=1, source_target_pairs={{0,3},{1,0},{2,1},{3,2},{4,7},{5,4},{6,5},{7,6},{8,11},{9,8},{10,9... | collective-permute-start | bytes 884744 | tf_op jit(solution)/shard_map/ppermute | solution.py:538
  473.6 14.8 %collective-permute-start.34 = (bf16[96,2,768]{2,0,1:T(8,128)(2,1)S(1)}, bf16[96,2,768]{2,0,1:T(8,128)(2,1)S(1)}, u32[]{:S(2)}, u32[]{:S(2)}) collective-permute-start(bf16[96,2,768]{2,0,1:T(8,128)(2,1)S(1)} %get-tuple-element.205), channel_id=1, source_target_pairs={{0,1},{1,2},{2,3},{3,0},{4,5},{5,6},{6,7},{7,4},{8,9},{9,10},{10,1... | collective-permute-start | bytes 884744 | tf_op jit(solution)/shard_map/ppermute | solution.py:538
  473.6 25.3 %collective-permute-start.33 = (bf16[96,2,768]{2,0,1:T(8,128)(2,1)S(1)}, bf16[96,2,768]{2,0,1:T(8,128)(2,1)S(1)}, u32[]{:S(2)}, u32[]{:S(2)}) collective-permute-start(bf16[96,2,768]{2,0,1:T(8,128)(2,1)S(1)} %get-tuple-element.206), channel_id=1, source_target_pairs={{0,2},{1,3},{2,0},{3,1},{4,6},{5,7},{6,4},{7,5},{8,10},{9,11},{10,... | collective-permute-start | bytes 884744 | tf_op jit(solution)/shard_map/ppermute | solution.py:538
  (136 other events, 1270.6 us)
Sparse Core Ops, SparseCore 0:
  34.3 39.3 all-gather.4
  75.6 52.7 all-gather.6
  290.5 34.6 reduce-scatter.3
  328.9 59.8 reduce-scatter.5
  392.5 76.4 reduce-scatter.7
where the time goes:
time: 513 us; the launch traced here: 508 us
  waiting for transfers between devices  149 us (29%)
  local copies, waits for them, and re-layouts  104 us (20%)
  matrix products  73.6 us (14%)
  other arithmetic  68.8 us (13%)
  starting transfers between devices  53.1 us (10%)
  blocking collectives  42.5 us (8%)
  between operations  16.5 us (3%)
    ppermute x35, waiting for transfers between devices, routed(): return lax.ppermute(values, AXES, pairs)  106 us
    ppermute x35, starting transfers between devices, routed(): return lax.ppermute(values, AXES, pairs)  52.7 us
    dot_general x30, matrix products, dot(): lax.dot_general(a, b, (dims, ((), ())), preferred_element_type=jnp.float32)  47.6 us
    reduce_scatter x2, waiting for transfers between devices, reduced(): mine = lax.psum_scatter(parts, rank_axes, scatter_dimension=0, tiled=True)  43 us
    psum x1, blocking collectives, on_device_columns(): lax.psum(jnp.concatenate([grad_ln_row_gain, grad_ln_row_bias, grad_row_bo...  42.5 us
    unnamed x299, local copies, waits for them, and re-layouts  31.2 us
    convert_element_type x9, other arithmetic, low(): return values.astype(jnp.bfloat16)  17.5 us
  transfers between devices with their start and end apart: 40, of which 14 were waited for; matrix products, arithmetic and copies ran while one was open for 30% of the time, Pallas kernels for 0%

commit v1 on v0

--- a/solution.py
+++ b/solution.py
@@ -1,8 +1,11 @@
+import functools
 import math
 
 import jax
 import jax.numpy as jnp
 from jax import lax
+from jax.experimental import pallas as pl
+from jax.experimental.pallas import tpu as pltpu
 from jax.sharding import PartitionSpec as P
 
 HD = 64
@@ -547,6 +550,18 @@
     return routed(values, lambda d, s, m: (d ^ 1, s, m))
 
 
+def to_x(values):
+    return routed(values, lambda d, s, m: (d, s ^ 1, m))
+
+
+def to_y(values):
+    return routed(values, lambda d, s, m: (d ^ 2, s, m))
+
+
+def together(*values):
+    return lax.optimization_barrier(values)
+
+
 def straight(d, s, m):
     return (d // 2 * 2 + s, d % 2, m)
 
@@ -559,19 +574,31 @@
     return (d // 2 * 2 + s, 1 - d % 2, m)
 
 
-def to_work(values):
+def to_work(arrays, extra):
+    half = arrays[0].shape[0] // 2
+    x = lax.axis_index(SEQ)
+
+    def halves(which):
+        return [lax.dynamic_slice_in_dim(a, which * half, half, axis=0) for a in arrays]
+
+    sent = [jnp.concatenate(halves(x) + [extra]), jnp.concatenate(halves(1 - x))]
+    mine, other = routed(sent[0], straight), routed(sent[1], crossed)
+    found = [
+        jnp.concatenate([mine[i * half : (i + 1) * half], other[i * half : (i + 1) * half]])
+        for i in range(len(arrays))
+    ]
+    return found, mine[len(arrays) * half :], sent
+
+
+def send_from_work(values):
     half = values.shape[0] // 2
+    return routed(values[:half], straight), routed(values[half:], crossed_back)
+
+
+def from_work(mine, other):
     x = lax.axis_index(SEQ)
-    mine = lax.dynamic_slice_in_dim(values, x * half, half, axis=0)
-    other = lax.dynamic_slice_in_dim(values, (1 - x) * half, half, axis=0)
-    return jnp.stack([routed(mine, straight), routed(other, crossed)])
-
-
-def from_work(values):
-    x = lax.axis_index(SEQ)
-    mine, other = routed(values[0], straight), routed(values[1], crossed_back)
-    halves = jnp.stack([jnp.where(x == 0, mine, other), jnp.where(x == 0, other, mine)])
-    return halves.reshape(-1, halves.shape[-1])
+    halves = [jnp.where(x == 0, mine, other), jnp.where(x == 0, other, mine)]
+    return jnp.concatenate(halves).astype(jnp.float32)[None, :, None]
 
 
 def dot(a, b, dims):
@@ -602,6 +629,441 @@
 
 def total(values):
     return jnp.sum(values.astype(jnp.float32).reshape(-1, values.shape[-1]), axis=0)
+
+
+ANYWHERE = pl.BlockSpec(memory_space=pl.ANY)
+IN_VMEM = pl.BlockSpec(memory_space=pltpu.VMEM)
+IN_SMEM = pl.BlockSpec(memory_space=pltpu.SMEM)
+BIT_Y, BIT_CORE, BIT_X = 4, 2, 1
+X_FIRST = (0, BIT_Y, BIT_X, BIT_X | BIT_Y)
+Y_FIRST = (0, BIT_X, BIT_Y, BIT_X | BIT_Y)
+PAIR = 2 * HD
+
+
+def kernel_call(body, name, in_memory, outs, scratch, flops, args, scalars=(), waits=()):
+    count, given = len(args), body
+    if waits:
+        args = list(args) + list(waits)
+        in_memory = tuple(in_memory) + tuple(range(count, len(args)))
+
+        def body(*refs):
+            given(*refs[:count], *refs[len(args) :])
+
+    moved = sum(a.size * a.dtype.itemsize for a in args) + sum(
+        math.prod(shape) * jnp.dtype(kind).itemsize for shape, kind in outs
+    )
+    return pl.pallas_call(
+        body,
+        name=name,
+        out_shape=[jax.ShapeDtypeStruct(shape, kind) for shape, kind in outs],
+        in_specs=[
+            ANYWHERE if i in in_memory else (IN_SMEM if i in scalars else IN_VMEM)
+            for i in range(len(args))
+        ],
+        out_specs=[IN_VMEM] * len(outs),
+        scratch_shapes=scratch,
+        cost_estimate=pl.CostEstimate(flops=flops, bytes_accessed=moved, transcendentals=0),
+    )(*args)
+
+
+def mm(a, b):
+    return lax.dot_general(a, b, (((1,), (0,)), ((), ())), preferred_element_type=jnp.float32)
+
+
+def mm_nt(a, b):
+    return lax.dot_general(a, b, (((1,), (1,)), ((), ())), preferred_element_type=jnp.float32)
+
+
+def mm_tn(a, b):
+    return lax.dot_general(a, b, (((0,), (0,)), ((), ())), preferred_element_type=jnp.float32)
+
+
+def turned(values):
+    return jnp.transpose(values.astype(jnp.float32)).astype(jnp.bfloat16)
+
+
+def row_sum(values):
+    return jnp.sum(values, axis=0, keepdims=True)
+
+
+def lanes_below(shape):
+    return lax.broadcasted_iota(jnp.int32, shape, 1) < HD
+
+
+def merged(first, second, slot):
+    if slot == 0:
+        return jnp.where(lanes_below(first.shape), first, pltpu.roll(second, HD, 1))
+    return jnp.where(lanes_below(first.shape), pltpu.roll(first, HD, 1), second)
+
+
+def joined(pieces, slot):
+    pieces = [p.astype(jnp.float32) for p in pieces]
+    if len(pieces) % 2:
+        pieces = pieces + [jnp.zeros_like(pieces[0])]
+    return jnp.concatenate(
+        [merged(pieces[i], pieces[i + 1], slot) for i in range(0, len(pieces), 2)], axis=1
+    )
+
+
+def parted(slot0, slot1, piece):
+    at = piece // 2 * PAIR
+    a, b = slot0[:, at : at + PAIR], slot1[:, at : at + PAIR]
+    return merged(a, b, piece % 2)
+
+
+def load_shards(rank, own, parts, target, sems):
+    shards, half = target.shape[0], parts[1].shape[1]
+    copies = [pltpu.make_async_copy(own, target.at[0], sems.at[0])]
+    for bit, (away, near1, near2, pair1, pair2) in ((0, parts[:5]), (BIT_CORE, parts[5:])):
+        found = (
+            (0, 0, away.at[:, pl.ds(0, half)]),
+            (0, 1, away.at[:, pl.ds(half, half)]),
+            (BIT_X, 0, near1),
+            (BIT_Y, 1, near2),
+            (BIT_Y, 0, pair1.at[0]),
+            (BIT_X, 1, pair2.at[0]),
+            (BIT_X | BIT_Y, 0, pair1.at[1]),
+            (BIT_X | BIT_Y, 1, pair2.at[1]),
+        )
+        for bits, which, part in found:
+            place = pl.multiple_of(((rank[0] ^ (bit | bits)) * 2 + which) * half, half)
+            copies.append(
+                pltpu.make_async_copy(
+                    part,
+                    target.at[pl.ds(1, shards - 1), pl.ds(place, half)],
+                    sems.at[len(copies)],
+                )
+            )
+    for copy in copies:
+        copy.start()
+    return copies
+
+
+def matrix(shards, t, hs):
+    return shards[:, t * hs : (t + 1) * hs].reshape(-1, shards.shape[2])
+
+
+def finish(copies):
+    for copy in copies:
+        copy.wait()
+
+
+def head_map(width):
+    feature = lax.broadcasted_iota(jnp.int32, (width, 128), 0) // HD
+    return (feature == lax.broadcasted_iota(jnp.int32, (width, 128), 1)).astype(jnp.bfloat16)
+
+
+def head_total(product, ones):
+    upper = product.astype(jnp.bfloat16)
+    lower = (product - upper.astype(jnp.float32)).astype(jnp.bfloat16)
+    return mm(upper, ones) + mm(lower, ones)
+
+
+def over_features(values, ones):
+    return mm_nt(values.astype(jnp.bfloat16), ones)
+
+
+def pack_kernel(rank, q, k, v, wo, wr, bias, w1, w2, own_out, share_out, ffn_out, sems):
+    rows1 = w1.shape[1]
+    copies = [
+        pltpu.make_async_copy(w1.at[rank[0]], ffn_out.at[pl.ds(0, rows1)], sems.at[0]),
+        pltpu.make_async_copy(
+            w2.at[rank[0]], ffn_out.at[pl.ds(rows1, w2.shape[1])], sems.at[1]
+        ),
+    ]
+    for copy in copies:
+        copy.start()
+    hs = wo.shape[0]
+    for i, part in enumerate((q, k, v)):
+        own_out[i * hs : (i + 1) * hs] = part[...]
+    own_out[3 * hs : 4 * hs] = wo[...]
+    own_out[4 * hs : 5 * hs] = wr[...]
+    rest = own_out.shape[0] - 5 * hs
+    own_out[5 * hs :] = jnp.zeros((rest, own_out.shape[1]), jnp.bfloat16)
+    rows = own_out.shape[0] // 8
+    share_out[:rows] = own_out[pl.ds(pl.multiple_of(rank[0] * rows, rows), rows)]
+    share_out[rows:] = bias[...]
+    finish(copies)
+
+
+def row_project_kernel(blocks, half, heads, *refs):
+    hidden, (w, b, q_out, kv_out) = refs[:blocks], refs[blocks:]
+    for k in range(blocks):
+        y = (mm_nt(hidden[k][...], w[...]) + b[...]).astype(jnp.bfloat16).astype(jnp.float32)
+        for p in range(3 * heads):
+            piece = parted(y[:half], y[half:], p).astype(jnp.bfloat16)
+            if p < heads:
+                q_out[p, k * half : (k + 1) * half] = piece
+            else:
+                kv_out[p - heads, k * half : (k + 1) * half] = piece
+
+
+def row_attend_kernel(heads, half, scale, q, kv, kv_sibling, mask, p_out, *o_out):
+    blocks = len(o_out)
+
+    def one_head(h, carry):
+        keys = [kv[h], pltpu.roll(kv_sibling[h].astype(jnp.float32), HD, 1).astype(jnp.bfloat16)]
+        values = [
+            kv[heads + h],
+            pltpu.roll(kv_sibling[heads + h].astype(jnp.float32), HD, 1).astype(jnp.bfloat16),
+        ]
+        keys, values = jnp.concatenate(keys, axis=0), jnp.concatenate(values, axis=0)
+        for k in range(blocks):
+            rows = slice(k * half, (k + 1) * half)
+            scores = jnp.where(mask[...] > 0, mm_nt(q[h, rows], keys) * scale, -1e30)
+            powers = jnp.exp(scores - jnp.max(scores, axis=-1, keepdims=True))
+            weights = (powers / jnp.sum(powers, axis=-1, keepdims=True)).astype(jnp.bfloat16)
+            p_out[h, rows] = weights
+            o_out[k][h] = mm(weights, values).astype(jnp.bfloat16)
+        return carry
+
+    lax.fori_loop(0, heads, one_head, 0)
+
+
+def row_attend_back_kernel(
+    heads, half, blocks, scale, q, kv, kv_sibling, p, *refs
+):
+    d, (q_out, kv_out, sibling_out) = refs[:blocks], refs[blocks:]
+    keys_here = kv.shape[1]
+
+    def one_head(h, carry):
+        keys = [kv[h], pltpu.roll(kv_sibling[h].astype(jnp.float32), HD, 1).astype(jnp.bfloat16)]
+        values = [
+            kv[heads + h],
+            pltpu.roll(kv_sibling[heads + h].astype(jnp.float32), HD, 1).astype(jnp.bfloat16),
+        ]
+        keys, values = jnp.concatenate(keys, axis=0), jnp.concatenate(values, axis=0)
+        grad_o = jnp.concatenate([d[k][h] for k in range(blocks)], axis=0)
+        weights = p[h]
+        weights32 = weights.astype(jnp.float32)
+        grad_weights = mm_nt(grad_o, values)
+        inner = jnp.sum(weights32 * grad_weights, axis=-1, keepdims=True)
+        grad_logits = (weights32 * (grad_weights - inner)).astype(jnp.bfloat16)
+        q_out[h] = (mm(grad_logits, keys) * scale).astype(jnp.bfloat16)
+        grad_k = mm_tn(grad_logits, q[h]) * scale
+        grad_v = mm_tn(weights, grad_o)
+        kv_out[h], kv_out[heads + h] = grad_k[:keys_here], grad_v[:keys_here]
+        sibling_out[h] = pltpu.roll(grad_k[keys_here:], HD, 1).astype(jnp.bfloat16)
+        sibling_out[heads + h] = pltpu.roll(grad_v[keys_here:], HD, 1).astype(jnp.bfloat16)
+        return carry
+
+    lax.fori_loop(0, heads, one_head, 0)
+
+
+def row_project_back_kernel(blocks, half, heads, rank, *refs):
+    hidden = refs[:blocks]
+    w, gain, bias, gq, gkv, gkv_sibling, col_sums, ffn_sums, b1_sums = refs[blocks : blocks + 9]
+    keep_out, theirs_out, bias_out = refs[blocks + 9 : blocks + 12]
+    send_out, (sums, g, whole) = refs[blocks + 12 : 2 * blocks + 12], refs[2 * blocks + 12 :]
+    sums[...] = jnp.zeros_like(sums)
+    sums[2:3] = col_sums[3:4]
+    sums[3:6] = col_sums[0:3]
+    sums[6:9] = ffn_sums[0:3]
+    sums[9:11] = col_sums[4:6]
+    for k in range(blocks):
+        rows = slice(k * half, (k + 1) * half)
+        pieces = [gq[h, rows].astype(jnp.float32) for h in range(heads)] + [
+            (gkv[i, rows] + gkv_sibling[i, rows].astype(jnp.float32))
+            .astype(jnp.bfloat16)
+            .astype(jnp.float32)
+            for i in range(2 * heads)
+        ]
+        y = jnp.concatenate([joined(pieces, 0), joined(pieces, 1)], axis=0).astype(jnp.bfloat16)
+        g[2 * k * half : 2 * (k + 1) * half] = y
+        grad = mm(y, w[...])
+        send_out[k][: 2 * half] = grad.astype(jnp.bfloat16)
+        unit = (hidden[k][...].astype(jnp.float32) - bias[...]) / gain[...]
+        sums[0:1] += row_sum(grad * unit)
+        sums[1:2] += row_sum(grad)
+    for k in range(blocks):
+        sums[11:12] = b1_sums[k : k + 1]
+        send_out[k][2 * half :] = sums[...].astype(jnp.bfloat16)
+    bias_out[...] = row_sum(g[...].astype(jnp.float32))
+    weight = mm_tn(hidden[0][...], g[: 2 * half])
+    for k in range(1, blocks):
+        weight += mm_tn(hidden[k][...], g[2 * k * half : 2 * (k + 1) * half])
+    whole[...] = weight
+    rows = keep_out.shape[0] // 4
+    for i, bits in enumerate(X_FIRST):
+        here = slice(i * rows, (i + 1) * rows)
+        for peer, target in ((bits, keep_out), (bits | BIT_CORE, theirs_out)):
+            at = pl.multiple_of((rank[0] ^ peer) * rows, rows)
+            target[here] = whole[pl.ds(at, rows)].astype(jnp.bfloat16)
+
+
+def norm_in_kernel(values, gain, bias):
+    unit, scale = norm_parts(values)
+    return unit, scale, (unit * gain + bias).astype(jnp.bfloat16)
+
+
+def column_kernel(
+    blocks, heads, rank, stream, own, row_bo, gain, bias, bq, bv, col_bo, ffn_gain, ffn_bias,
+    *refs
+):
+    o, parts, refs = refs[:blocks], refs[blocks : blocks + 10], refs[blocks + 10 :]
+    row_heads_out, row_out, normed_out, q_out, k_out, v_out, heads_out, col_out, ffn_out = refs[:9]
+    shards, sems = refs[9:]
+    hs = heads * HD
+    half = stream.shape[0] // 2
+    copies = load_shards(rank, own, parts, shards, sems)
+    pieces = [o[-k % blocks][h] for k in range(blocks) for h in range(heads)]
+    row_heads = jnp.concatenate([joined(pieces, 0), joined(pieces, 1)], axis=0).astype(
+        jnp.bfloat16
+    )
+    row_heads_out[...] = row_heads
+    finish(copies)
+    after_row = stream[...] + mm(row_heads, matrix(shards, 4, hs)) + row_bo[...]
+    row_out[...] = after_row
+    _, _, normed = norm_in_kernel(after_row, gain[...], bias[...])
+    normed_out[...] = normed
+    q = (mm_nt(normed, matrix(shards, 0, hs)) + bq[...]).astype(jnp.bfloat16)
+    q_out[...] = q
+    k = mm_nt(normed, matrix(shards, 1, hs)).astype(jnp.bfloat16)
+    k_out[...] = k
+    v = (mm_nt(normed, matrix(shards, 2, hs)) + bv[...]).astype(jnp.bfloat16)
+    v_out[...] = v
+    ones = head_map(stream.shape[1])
+    k32, v32 = k.astype(jnp.float32), v.astype(jnp.float32)
+    k_gap = k32[:half] - k32[half:]
+    for r in range(2):
+        rows = slice(r * half, (r + 1) * half)
+        gap = head_total(q[rows].astype(jnp.float32) * k_gap, ones) * (1.0 / math.sqrt(HD))
+        first = over_features(1.0 / (1.0 + jnp.exp(-gap)), ones)
+        second = over_features(1.0 / (1.0 + jnp.exp(gap)), ones)
+        heads_out[rows] = (first * v32[:half] + second * v32[half:]).astype(jnp.bfloat16)
+    after_col = after_row + mm(heads_out[...], matrix(shards, 3, hs)) + col_bo[...]
+    col_out[...] = after_col
+    _, _, ffn_normed = norm_in_kernel(after_col, ffn_gain[...], ffn_bias[...])
+    ffn_out[...] = ffn_normed
+
+
+def ffn_kernel(
+    rank, normed, stream, grad_low, gathered, b1, b2, gain,
+    out, grad_out, low_out, weights_out, sums_out, b1_out,
+    w1, w2, normed_t, low_t, total_out, total_back, sems,
+):
+    blocks, peers, rows1, size = w1.shape
+    width = normed.shape[1]
+    copies = []
+    for k in range(blocks):
+        shard = (rank[1] + blocks - k) % blocks
+        pair = (
+            (gathered.at[:, shard, pl.ds(0, rows1)], w1.at[k]),
+            (gathered.at[:, shard, pl.ds(rows1, w2.shape[2])], w2.at[k]),
+        )
+        for i, (source, target) in enumerate(pair):
+            copies.append(pltpu.make_async_copy(source, target, sems.at[2 * k + i]))
+            copies[-1].start()
+    normed_t[...] = turned(normed[...])
+    low_t[...] = turned(grad_low[...])
+    total_out[...] = jnp.zeros_like(total_out)
+    total_back[...] = jnp.zeros_like(total_back)
+    finish(copies)
+
+    def one_shard(k, carry):
+        shard = (rank[1] + blocks - k) % blocks
+        weight1 = w1[k].reshape(width, size)
+        weight2 = w2[k].reshape(size, width)
+        up = mm(normed[...], weight1) + b1[pl.ds(k, 1)]
+        below = 0.5 * (1.0 + lax.erf(up * (1.0 / math.sqrt(2.0))))
+        density = jnp.exp(up * up * -0.5) * (1.0 / math.sqrt(2.0 * math.pi))
+        activated = (up * below).astype(jnp.bfloat16)
+        grad_up = (mm_nt(grad_low[...], weight2) * (below + up * density)).astype(jnp.bfloat16)
+        total_out[...] += mm(activated, weight2)
+        total_back[...] += mm_nt(grad_up, weight1)
+        b1_out[pl.ds(k, 1)] = row_sum(grad_up.astype(jnp.float32))
+        for i, (left, right) in enumerate(((normed_t, grad_up), (low_t, activated))):
+            product = mm(left[...], right).astype(jnp.bfloat16).reshape(peers, rows1, size)
+            weights_out[:, shard, :, i * size : (i + 1) * size] = product
+        return carry
+
+    lax.fori_loop(0, blocks, one_shard, 0)
+    out[...] = (stream[...] + total_out[...] + b2[...]).astype(jnp.bfloat16)
+    unit, scale = norm_parts(stream[...])
+    grad_normed = total_back[...]
+    sums_out[...] = jnp.zeros_like(sums_out)
+    sums_out[0:1] = row_sum(grad_normed * unit)
+    sums_out[1:2] = row_sum(grad_normed)
+    sums_out[2:3] = row_sum(grad_low[...].astype(jnp.float32))
+    grad = grad_low[...].astype(jnp.float32) + norm_pull(unit, scale, gain[...], grad_normed)
+    grad_out[...] = grad
+    low_out[...] = grad.astype(jnp.bfloat16)
+
+
+def column_back_kernel(
+    blocks, heads, rank, grad, grad_low, q, k, v, row_stream, own, gain, *refs
+):
+    parts, refs = refs[:10], refs[10:]
+    gq_out, gk_out, gv_out, grad_out, low_out, sums_out = refs[:6]
+    d_out, (shards, sems) = refs[6 : 6 + blocks], refs[6 + blocks :]
+    hs, width = heads * HD, grad.shape[1]
+    half = grad.shape[0] // 2
+    copies = load_shards(rank, own, parts, shards, sems)
+    ones = head_map(width)
+    finish(copies)
+    grad_heads = mm_nt(grad_low[...], matrix(shards, 3, hs)).astype(jnp.bfloat16)
+    g32 = grad_heads.astype(jnp.float32)
+    k32, v32, q32 = (a[...].astype(jnp.float32) for a in (k, v, q))
+    k_gap, v_gap = k32[:half] - k32[half:], v32[:half] - v32[half:]
+    factor = 1.0 / math.sqrt(HD)
+    grad_k, grad_v = 0.0, [0.0, 0.0]
+    for r in range(2):
+        rows = slice(r * half, (r + 1) * half)
+        gap = head_total(q32[rows] * k_gap, ones) * factor
+        first, second = 1.0 / (1.0 + jnp.exp(-gap)), 1.0 / (1.0 + jnp.exp(gap))
+        pull = head_total(g32[rows] * v_gap, ones)
+        grad_logit = over_features(first * second * pull, ones)
+        gq_out[rows] = (grad_logit * k_gap * factor).astype(jnp.bfloat16)
+        grad_k += grad_logit * q32[rows] * factor
+        for s, weight in enumerate((first, second)):
+            grad_v[s] += over_features(weight, ones) * g32[rows]
+    gk_out[:half] = grad_k.astype(jnp.bfloat16)
+    gk_out[half:] = (-grad_k).astype(jnp.bfloat16)
+    gv_out[:half] = grad_v[0].astype(jnp.bfloat16)
+    gv_out[half:] = grad_v[1].astype(jnp.bfloat16)
+    grad_normed = (
+        mm(gq_out[...], matrix(shards, 0, hs))
+        + mm(gk_out[...], matrix(shards, 1, hs))
+        + mm(gv_out[...], matrix(shards, 2, hs))
+    )
+    unit, scale = norm_parts(row_stream[...])
+    total = grad[...] + norm_pull(unit, scale, gain[...], grad_normed)
+    grad_out[...] = total
+    low = total.astype(jnp.bfloat16)
+    low_out[...] = low
+    sums_out[...] = jnp.zeros_like(sums_out)
+    sums_out[0:1] = row_sum(grad_normed * unit)
+    sums_out[1:2] = row_sum(grad_normed)
+    sums_out[2:3] = row_sum(grad_low[...].astype(jnp.float32))
+    sums_out[3:4] = row_sum(low.astype(jnp.float32))
+    sums_out[4:5] = row_sum(gq_out[...].astype(jnp.float32))
+    sums_out[5:6] = row_sum(gv_out[...].astype(jnp.float32))
+    grad_o = mm_nt(low, matrix(shards, 4, hs)).astype(jnp.bfloat16).astype(jnp.float32)
+    for b in range(blocks):
+        for h in range(heads):
+            piece = parted(grad_o[:half], grad_o[half:], b * heads + h)
+            d_out[b][h] = piece.astype(jnp.bfloat16)
+
+
+def weights_kernel(
+    rank, normed, col_low, row_low, gq, gk, gv, col_heads, row_heads, keep_out, send_out, left
+):
+    width = normed.shape[1]
+    rows, kept, part = width // 8, width // 2, width // 2
+    for i, source in enumerate((normed, col_low, row_low)):
+        left[3 * i] = turned(source[...])
+        for order, bits in enumerate((X_FIRST, Y_FIRST)):
+            for j in range(8):
+                peer = rank[0] ^ (bits[j % 4] | (BIT_CORE if j >= 4 else 0))
+                block = left[3 * i, pl.ds(pl.multiple_of(peer * rows, rows), rows)]
+                left[3 * i + 1 + order, j * rows : (j + 1) * rows] = block
+    for t, right in enumerate((gq, gk, gv, col_heads, row_heads)):
+        for order in range(2):
+            product = mm(
+                left[3 * max(t - 2, 0) + 1 + order], right[:, order * part : (order + 1) * part]
+            ).astype(jnp.bfloat16)
+            keep_out[order, :, t * part : (t + 1) * part] = product[:kept]
+            send_out[order, :, t * part : (t + 1) * part] = product[kept:]
 
 
 def on_device_columns(
@@ -641,322 +1103,311 @@
     mps = lax.axis_size(MP)
     rank = lax.axis_index(DP) * lax.axis_size(SEQ) + lax.axis_index(SEQ)
     c, z = lax.axis_index(DP) % 2, lax.axis_index(MP)
-    ch, fh, dh = hs // ranks, fs // ranks, width // ranks
-
-    stream = to_work(acts[0, :, 0]).astype(jnp.float32)
-    mask = routed(col_mask[0], straight)
-    half = stream.shape[1]
-
-    def share(matrix, rows):
-        return lax.dynamic_slice_in_dim(matrix, rank * rows, rows, axis=0)
-
-    col_q_t, col_k_t, col_v_t = col_wq[0].T, col_wk[0].T, col_wv[0].T
+    f32, b16 = jnp.float32, jnp.bfloat16
+    bf_dma = pltpu.SemaphoreType.DMA
+
+    rank_ref = jnp.stack([rank, z]).astype(jnp.int32)
+
+    columns = col_mask.shape[1]
+    mask_rows = -(-columns // (8 * width)) * 8
+    padded = jnp.pad(col_mask[0].astype(b16), (0, mask_rows * width - columns))
+    (start, grad_start), mask, sent = to_work(
+        (acts[0, :, 0], cotangent[0, :, 0]), padded.reshape(mask_rows, width)
+    )
+    mask = mask.reshape(-1)[:columns]
+    tokens = start.shape[0]
+    half = tokens // 2
+    stream = start.astype(f32)
+    row_unit, row_scale = norm_parts(stream)
+    normed = low(row_unit * ln_row_gain + ln_row_bias)
 
     def two_parts(v):
         upper = low(v)
-        return upper, low(v - upper.astype(jnp.float32))
-
-    b1_parts, bq_parts, bv_parts = two_parts(ffn_b1[0]), two_parts(col_bq[0]), two_parts(col_bv[0])
+        return upper, low(v - upper.astype(f32))
+
+    b1_parts, bq_parts, bv_parts = two_parts(ffn_b1), two_parts(col_bq), two_parts(col_bv)
     bias_rows = jnp.concatenate(
+        b1_parts + (jnp.concatenate(bq_parts + bv_parts, axis=1), jnp.zeros((13, width), b16))
+    )
+    chunk = -(-5 * hs // (32 * ranks)) * 32
+    fc, dc = fs // ranks, width // ranks
+    own_w1, own_w2 = ffn_w1[0].reshape(ranks, dc, fs), ffn_w2[0].reshape(ranks, fc, width)
+    own_attention, pack_attention, pack_ffn = kernel_call(
+        pack_kernel,
+        "pack",
+        (7, 8),
+        [((chunk * ranks, width), b16), ((chunk + 16, width), b16), ((dc + fc, width), b16)],
+        [bf_dma((2,))],
+        0,
+        [rank_ref, col_wq[0].T, col_wk[0].T, col_wv[0].T, col_wo[0], row_wo[0], bias_rows]
+        + [own_w1, own_w2],
+        (0,),
+        sent,
+    )
+
+
+    whole_ffn = lax.all_gather(pack_ffn, AXES, axis=0, tiled=False)
+    whole_ffn = whole_ffn.reshape(ranks, mps, dc + fc, width)
+    pack_attention, normed = together(pack_attention, normed)
+    away = [shifted(pack_attention, k) for k in range(1, mps)]
+    normed, *away = together(normed, *away)
+    away = jnp.stack(away)
+    hidden = [shifted(normed, k) for k in range(1, mps)]
+    got = together(*hidden, to_x(away[:, : chunk // 2]), to_y(away[:, chunk // 2 : chunk]))
+    hidden, near1, near2 = [normed, *got[: mps - 1]], got[mps - 1], got[mps]
+    pair1 = to_y(jnp.stack([away[:, : chunk // 2], near1]))
+    pair2 = to_x(jnp.stack([away[:, chunk // 2 : chunk], near2]))
+    bias_away = away[:, chunk : chunk + 3].astype(f32)
+    b1 = jnp.concatenate([ffn_b1, bias_away[:, 0] + bias_away[:, 1]])
+    bias_qv = bias_away[:, 2].reshape(mps - 1, 2, 2, hs).sum(axis=2)
+    bq = jnp.concatenate([col_bq, bias_qv[:, 0].reshape(1, -1)], axis=1)
+    bv = jnp.concatenate([col_bv, bias_qv[:, 1].reshape(1, -1)], axis=1)
+
+    odd = 3 * heads % 2 * HD
+    row_w = jnp.concatenate(
+        [row_wq[0].T, row_wk[0].T, row_wv[0].T, jnp.zeros((odd, width), b16)]
+    )
+    row_width = row_w.shape[0]
+    row_b = jnp.concatenate(
+        [row_bq, jnp.zeros_like(row_bq), row_bv, jnp.zeros((1, odd), f32)], axis=1
+    )
+    here = mps * half
+    q_h, kv_h = kernel_call(
+        functools.partial(row_project_kernel, mps, half, heads),
+        "row_project",
+        (),
+        [((heads, here, PAIR), b16), ((2 * heads, here, PAIR), b16)],
+        [],
+        2 * mps * tokens * width * row_width,
+        hidden + [row_w, row_b],
+    )
+    kv_sibling = to_sibling(kv_h)
+    score_scale = 1.0 / math.sqrt(HD * 2)
+    near = (z - jnp.arange(mps)) % mps
+    pick = (near[:, None] == jnp.arange(mps)).astype(f32)
+    mask_blocks = jnp.einsum(
+        "kz,zsi->ski", pick, mask.reshape(mps, 2, half).astype(f32), precision="highest"
+    )
+    mask_near = jnp.where(c == 0, mask_blocks, mask_blocks[::-1]).reshape(1, -1)
+    p_h, *o_blocks = kernel_call(
+        functools.partial(row_attend_kernel, heads, half, score_scale),
+        "row_attend",
+        (),
+        [((heads, here, 2 * here), b16)] + [((heads, half, PAIR), b16)] * mps,
+        [],
+        8 * heads * here * here * PAIR,
+        [q_h, kv_h, kv_sibling, mask_near],
+    )
+    o_from = [o_blocks[0]] + [shifted(o_blocks[k], -k) for k in range(1, mps)]
+    *o_from, pair1, pair2 = together(*o_from, pair1, pair2)
+    parts = [away, near1, near2, pair1, pair2]
+    parts += [to_sibling(part) for part in parts]
+
+    weight_scratch = [pltpu.VMEM((mps, chunk * ranks, width), b16), bf_dma((17,))]
+    square = tokens * width * width * 2
+    row_heads, row_stream, col_normed, col_q, col_k, col_v, col_heads, col_stream, ffn_normed = (
+        kernel_call(
+            functools.partial(column_kernel, mps, heads),
+            "column",
+            (2,) + tuple(range(11 + mps, 21 + mps)),
+            [
+                ((tokens, width), kind)
+                for kind in (b16, f32, b16, b16, b16, b16, b16, f32, b16)
+            ],
+            weight_scratch,
+            5 * square,
+            [rank_ref, stream, own_attention, row_bo, ln_col_gain, ln_col_bias, bq, bv]
+            + [col_bo, ln_ffn_gain, ln_ffn_bias]
+            + o_from
+            + parts,
+            (0,),
+        )
+    )
+
+    out_low, ffn_grad, col_low, grad_ffn, ffn_sums, grad_b1 = kernel_call(
+        ffn_kernel,
+        "ffn",
+        (4,),
         [
-            jnp.stack(b1_parts),
-            jnp.concatenate(bq_parts + bv_parts)[None],
-            jnp.zeros((5, width), jnp.bfloat16),
+            ((tokens, width), b16),
+            ((tokens, width), f32),
+            ((tokens, width), b16),
+            ((ranks, mps, dc, 2 * fs), b16),
+            ((8, width), f32),
+            ((mps, fs), f32),
+        ],
+        [
+            pltpu.VMEM((mps, ranks, dc, fs), b16),
+            pltpu.VMEM((mps, ranks, fc, width), b16),
+            pltpu.VMEM((width, tokens), b16),
+            pltpu.VMEM((width, tokens), b16),
+            pltpu.VMEM((tokens, width), f32),
+            pltpu.VMEM((tokens, width), f32),
+            bf_dma((2 * mps,)),
+        ],
+        12 * tokens * width * fs * mps,
+        [rank_ref, ffn_normed, col_stream, grad_start, whole_ffn, b1, ffn_b2, ln_ffn_gain],
+        (0,),
+    )
+    out_halves = send_from_work(out_low)
+
+    grad_q, grad_k, grad_v, row_grad, row_low, col_sums, *d_blocks = kernel_call(
+        functools.partial(column_back_kernel, mps, heads),
+        "column_back",
+        (7,) + tuple(range(9, 19)),
+        [
+            ((tokens, width), b16),
+            ((tokens, width), b16),
+            ((tokens, width), b16),
+            ((tokens, width), f32),
+            ((tokens, width), b16),
+            ((8, width), f32),
         ]
-    )
-    pack_attention = jnp.concatenate(
-        [share(w, ch) for w in (col_q_t, col_k_t, col_v_t, col_wo[0], row_wo[0])] + [bias_rows]
-    )
-    pack_ffn = jnp.concatenate([share(ffn_w1[0], dh), share(ffn_w2[0], fh)])
-
-    def gathered(pack):
-        away = jnp.stack([shifted(pack, k) for k in range(1, mps)])
-        return away, lax.all_gather(away, (DP, SEQ), axis=0, tiled=False)
-
-    away_attention, whole_attention = gathered(pack_attention)
-    away_ffn, whole_ffn = gathered(pack_ffn)
-
-    def full_rows(own, whole, at, rows):
-        rest = whole[:, :, at : at + rows].swapaxes(0, 1).reshape(mps - 1, ranks * rows, width)
-        return jnp.concatenate([own[None], rest])
-
-    wq_t = full_rows(col_q_t, whole_attention, 0, ch).reshape(-1, width)
-    wk_t = full_rows(col_k_t, whole_attention, ch, ch).reshape(-1, width)
-    wv_t = full_rows(col_v_t, whole_attention, 2 * ch, ch).reshape(-1, width)
-    col_o = full_rows(col_wo[0], whole_attention, 3 * ch, ch).reshape(-1, width)
-    row_o = full_rows(row_wo[0], whole_attention, 4 * ch, ch).reshape(-1, width)
-    w1 = full_rows(ffn_w1[0], whole_ffn, 0, dh)
-    w2 = full_rows(ffn_w2[0], whole_ffn, dh, fh).reshape(-1, width)
-    bias_away = away_attention[:, 5 * ch :].astype(jnp.float32)
-    b1 = jnp.concatenate([ffn_b1[0]] + [bias_away[k, 0] + bias_away[k, 1] for k in range(mps - 1)])
-    bq = jnp.concatenate(
-        [col_bq[0]]
-        + [bias_away[k, 2, :hs] + bias_away[k, 2, hs : 2 * hs] for k in range(mps - 1)]
-    )
-    bv = jnp.concatenate(
-        [col_bv[0]]
-        + [
-            bias_away[k, 2, 2 * hs : 3 * hs] + bias_away[k, 2, 3 * hs : 4 * hs]
-            for k in range(mps - 1)
+        + [((heads, half, PAIR), b16)] * mps,
+        weight_scratch,
+        5 * square,
+        [rank_ref, ffn_grad, col_low, col_q, col_k, col_v, row_stream, own_attention, ln_col_gain]
+        + parts,
+        (0,),
+    )
+    d_from = [d_blocks[0]] + [shifted(d_blocks[k], -k) for k in range(1, mps)]
+    def both(a, b, here):
+        return a[here].astype(f32) + b[here].astype(f32)
+
+    gq_h, gkv_h, gkv_theirs = kernel_call(
+        functools.partial(row_attend_back_kernel, heads, half, mps, score_scale),
+        "row_attend_back",
+        (),
+        [
+            ((heads, here, PAIR), b16),
+            ((2 * heads, here, PAIR), f32),
+            ((2 * heads, here, PAIR), b16),
+        ],
+        [],
+        16 * heads * here * here * PAIR,
+        [q_h, kv_h, kv_sibling, p_h] + [d_from[-k % mps] for k in range(mps)],
+        waits=out_halves,
+    )
+    gkv_sibling = to_sibling(gkv_theirs)
+    att_keep, att_send = kernel_call(
+        weights_kernel,
+        "weights",
+        (),
+        [((2, width // 2, 5 * width // 2), b16)] * 2,
+        [pltpu.VMEM((9, width, tokens), b16)],
+        5 * square,
+        [rank_ref, col_normed, col_low, row_low, grad_q, grad_k, grad_v, col_heads, row_heads],
+        (0,),
+        [gkv_sibling],
+    )
+    row_keep, row_theirs, row_bias, *g_send = kernel_call(
+        functools.partial(row_project_back_kernel, mps, half, heads),
+        "row_project_back",
+        (),
+        [
+            ((width // 2, row_width), b16),
+            ((width // 2, row_width), b16),
+            ((1, row_width), f32),
         ]
-    )
-
-    row_unit, row_scale = norm_parts(stream)
-    normed = low(row_unit * ln_row_gain[0] + ln_row_bias[0])
-    hidden = jnp.stack([normed] + [shifted(normed, k) for k in range(1, mps)])
-    row_w = jnp.concatenate([row_wq[0], row_wk[0], row_wv[0]], axis=1)
-    row_b = jnp.concatenate([row_bq[0], jnp.zeros_like(row_bq[0]), row_bv[0]])
-    qkv = low(dot(hidden, row_w, ((3,), (0,))) + row_b)
-    kv_sibling = to_sibling(qkv[:, ::-1, :, hs:])
-    block = 2 * half
-
-    def by_head(v):
-        v = v.reshape(mps, 2, half, heads, HD)
-        return v.transpose(3, 0, 2, 1, 4).reshape(heads, mps * half, 2 * HD)
-
-    def from_head(v):
-        v = v.reshape(heads, mps, half, 2, HD)
-        return v.transpose(1, 3, 2, 0, 4).reshape(mps, 2, half, hs)
-
-    q_h = by_head(qkv[..., :hs])
-    k_h = jnp.concatenate([by_head(qkv[..., hs : 2 * hs]), by_head(kv_sibling[..., :hs])], axis=1)
-    v_h = jnp.concatenate([by_head(qkv[..., 2 * hs :]), by_head(kv_sibling[..., hs:])], axis=1)
-    score_scale = 1.0 / math.sqrt(HD * 2)
-    mask_blocks = mask.reshape(mps, 2, half)
-    mask_near = jnp.stack(
+        + [((tokens + 16, width), b16)] * mps,
         [
-            lax.dynamic_index_in_dim(mask_blocks, (z - k) % mps, keepdims=False)
-            for k in range(mps)
+            pltpu.VMEM((16, width), f32),
+            pltpu.VMEM((mps * tokens, row_width), b16),
+            pltpu.VMEM((width, row_width), f32),
         ],
-        axis=1,
-    )
-    mask_near = jnp.where(c == 0, mask_near, mask_near[::-1])
-    logits = jnp.einsum("hid,hjd->hij", q_h, k_h, preferred_element_type=jnp.float32)
-    attention = masked_softmax(logits, mask_near.reshape(-1), score_scale)
-    attention_low = low(attention)
-    o_h = jnp.einsum("hij,hjd->hid", attention_low, v_h, preferred_element_type=jnp.float32)
-    o_blocks = from_head(low(o_h))
-    o_from = [o_blocks[0]] + [shifted(o_blocks[k], -k) for k in range(1, mps)]
-    row_heads = jnp.concatenate([o_from[-k % mps] for k in range(mps)], axis=-1)
-    stream = stream + dot(row_heads, row_o, ((2,), (0,))) + row_bo[0]
-
-    col_unit, col_scale = norm_parts(stream)
-    col_normed = low(col_unit * ln_col_gain[0] + ln_col_bias[0])
-    col_q = low(dot(col_normed, wq_t, ((2,), (1,))) + bq)
-    col_k = low(dot(col_normed, wk_t, ((2,), (1,))))
-    col_v = low(dot(col_normed, wv_t, ((2,), (1,))) + bv)
-    col_scale_factor = 1.0 / math.sqrt(HD)
-
-    def head_sums(a, b):
-        product = a.astype(jnp.float32) * b.astype(jnp.float32)
-        return product.reshape(half, mps * heads, HD).sum(axis=-1)
-
-    def spread(v):
-        return jnp.repeat(v, HD, axis=-1)
-
-    def pair_softmax(r):
-        a = head_sums(col_q[r], col_k[0]) * col_scale_factor
-        b = head_sums(col_q[r], col_k[1]) * col_scale_factor
-        highest = jnp.maximum(a, b)
-        ea, eb = jnp.exp(a - highest), jnp.exp(b - highest)
-        return ea / (ea + eb), eb / (ea + eb)
-
-    col_attention = [pair_softmax(r) for r in range(2)]
-    value32 = col_v.astype(jnp.float32)
-    weight_low = [
-        [spread(low(col_attention[r][s]).astype(jnp.float32)) for s in range(2)] for r in range(2)
+        4 * mps * tokens * width * row_width,
+        [rank_ref] + hidden + [row_w, ln_row_gain, ln_row_bias, gq_h, gkv_h, gkv_sibling]
+        + [col_sums, ffn_sums, grad_b1],
+        (0,),
+        [att_keep],
+    )
+    part = width // 4
+    upper, lower = slice(0, part // 2), slice(part // 2, part)
+    att_theirs = to_sibling(att_send)
+    hops = ((to_x, to_y), (to_y, to_x))
+
+    def chip_sum(i, here):
+        return both(att_keep[i], att_theirs[i], here)
+
+    far = mps // 2
+    near = [k for k in range(1, mps) if k != far]
+    g_parts = {0: g_send[0], far: shifted(g_send[far], -far)}
+    got = together(
+        *(shifted(g_send[k], -k) for k in near),
+        *(hops[i][0](low(chip_sum(i, slice(part, None)))) for i in range(2)),
+        to_sibling(row_theirs),
+    )
+    g_parts |= dict(zip(near, got))
+    arrived, row_peer = got[len(near) : -1], got[-1]
+    g_parts[far], *second = together(
+        g_parts[far],
+        *(
+            hops[i][1](low(chip_sum(i, lower) + arrived[i][lower].astype(f32)))
+            for i in range(2)
+        ),
+    )
+    g_parts = [g_parts[k] for k in range(mps)]
+    grad_normed = sum(g[:tokens].astype(f32) for g in g_parts)
+    gradient = row_grad + norm_pull(row_unit, row_scale, ln_row_gain, grad_normed)
+
+    tails = [g[tokens:].astype(f32) for g in g_parts]
+    near_sum = sum(t[:9] for t in tails)
+    shard = [
+        sum(t[row, k * hs : (k + 1) * hs] for k, t in enumerate(tails))[None] for row in (9, 10)
     ]
-    col_heads = low(
-        jnp.stack(
-            [weight_low[r][0] * value32[0] + weight_low[r][1] * value32[1] for r in range(2)]
-        )
-    )
-    col_stream = stream + dot(col_heads, col_o, ((2,), (0,))) + col_bo[0]
-
-    ffn_unit, ffn_scale = norm_parts(col_stream)
-    ffn_normed = low(ffn_unit * ln_ffn_gain[0] + ln_ffn_bias[0])
-    up = jnp.concatenate([dot(ffn_normed, w1[k], ((2,), (0,))) for k in range(mps)], axis=-1) + b1
-    activated, gelu_pull = jax.vjp(exact_gelu, up)
-    activated = low(activated)
-    out_stream = col_stream + dot(activated, w2, ((2,), (0,))) + ffn_b2[0]
-    out = from_work(low(out_stream)).astype(jnp.float32)
-
-    grad_low = to_work(cotangent[0, :, 0])
-    gradient = grad_low.astype(jnp.float32)
-    grad_b2 = total(grad_low)
-    grad_up = low(gelu_pull(dot(grad_low, w2, ((2,), (1,))))[0])
-    grad_b1 = total(grad_up)
-    grad_normed = sum(
-        dot(grad_up[..., k * fs : (k + 1) * fs], w1[k], ((2,), (1,))) for k in range(mps)
-    )
-    grad_ln_ffn_gain, grad_ln_ffn_bias = total(grad_normed * ffn_unit), total(grad_normed)
-    token_dims = ((0,), (0,))
-    grad_ffn = jnp.stack(
-        [
-            low(dot(all_tokens(ffn_normed), all_tokens(grad_up), token_dims)),
-            low(dot(all_tokens(grad_low), all_tokens(activated), token_dims)),
-        ],
-        axis=1,
-    )
-    gradient = gradient + norm_pull(ffn_unit, ffn_scale, ln_ffn_gain[0], grad_normed)
-
-    grad_low = low(gradient)
-    grad_col_bo = total(grad_low)
-    grad_heads = low(dot(grad_low, col_o, ((2,), (1,))))
-    grad32 = grad_heads.astype(jnp.float32)
-    grad_logits = []
-    for r in range(2):
-        parts = [head_sums(grad_heads[r], col_v[s]) for s in range(2)]
-        inner = col_attention[r][0] * parts[0] + col_attention[r][1] * parts[1]
-        grad_logits.append(
-            [
-                spread(low(col_attention[r][s] * (parts[s] - inner)).astype(jnp.float32))
-                for s in range(2)
-            ]
-        )
-    q32, k32 = col_q.astype(jnp.float32), col_k.astype(jnp.float32)
-    grad_q = low(
-        jnp.stack(
-            [
-                (grad_logits[r][0] * k32[0] + grad_logits[r][1] * k32[1]) * col_scale_factor
-                for r in range(2)
-            ]
-        )
-    )
-    grad_k = low(
-        jnp.stack(
-            [
-                (grad_logits[0][s] * q32[0] + grad_logits[1][s] * q32[1]) * col_scale_factor
-                for s in range(2)
-            ]
-        )
-    )
-    grad_v = low(
-        jnp.stack([weight_low[0][s] * grad32[0] + weight_low[1][s] * grad32[1] for s in range(2)])
-    )
-    grad_col_bq, grad_col_bv = total(grad_q), total(grad_v)
-    grad_normed = (
-        dot(grad_q, wq_t, ((2,), (0,)))
-        + dot(grad_k, wk_t, ((2,), (0,)))
-        + dot(grad_v, wv_t, ((2,), (0,)))
-    )
-    grad_ln_col_gain, grad_ln_col_bias = total(grad_normed * col_unit), total(grad_normed)
-    gradient = gradient + norm_pull(col_unit, col_scale, ln_col_gain[0], grad_normed)
-
-    col_grad_low, grad_low = grad_low, low(gradient)
-    grad_row_bo = total(grad_low)
-    grad_heads = low(dot(grad_low, row_o, ((2,), (1,))))
-    d_from = [grad_heads[..., :hs]] + [
-        shifted(grad_heads[..., k * hs : (k + 1) * hs], -k) for k in range(1, mps)
+    shard += [row_bias[:, :hs], row_bias[:, 2 * hs : 3 * hs]]
+    summed = jnp.concatenate(
+        [near_sum, jnp.concatenate(shard, axis=1), sum(t[11:12] for t in tails)]
+    )
+
+    finals = [
+        (
+            chip_sum(i, upper) + arrived[i][upper].astype(f32) + second[i].astype(f32)
+        ).reshape(part // 2, 5, -1, hs)
+        for i in range(2)
     ]
-    d_h = by_head(jnp.stack([d_from[-k % mps] for k in range(mps)]))
-    normed_flat = all_tokens(col_normed)
-    grad_attention = jnp.stack(
-        [
-            low(dot(normed_flat, all_tokens(g), token_dims)) for g in (grad_q, grad_k, grad_v)
-        ]
-        + [
-            low(dot(all_tokens(col_grad_low), all_tokens(col_heads), token_dims)),
-            low(dot(all_tokens(grad_low), all_tokens(row_heads), token_dims)),
-        ],
-        axis=1,
-    )
-
-    grad_weights = jnp.einsum("hid,hjd->hij", d_h, v_h, preferred_element_type=jnp.float32)
-    inner = jnp.sum(attention * grad_weights, axis=-1, keepdims=True)
-    grad_logits = low(attention * (grad_weights - inner))
-    gq_h = (
-        jnp.einsum("hij,hjd->hid", grad_logits, k_h, preferred_element_type=jnp.float32)
-        * score_scale
-    )
-    gk_h = (
-        jnp.einsum("hij,hid->hjd", grad_logits, q_h, preferred_element_type=jnp.float32)
-        * score_scale
-    )
-    gv_h = jnp.einsum("hij,hid->hjd", attention_low, d_h, preferred_element_type=jnp.float32)
-    keys = mps * half
-    mine = jnp.concatenate([from_head(gk_h[:, :keys]), from_head(gv_h[:, :keys])], axis=-1)
-    theirs = jnp.concatenate([from_head(gk_h[:, keys:]), from_head(gv_h[:, keys:])], axis=-1)
-    g_kv = low(mine + to_sibling(low(theirs[:, ::-1])).astype(jnp.float32))
-    g_qkv = jnp.concatenate([low(from_head(gq_h)), g_kv], axis=-1)
-    g_hidden = dot(g_qkv, row_w, ((3,), (1,)))
-    g_send = low(g_hidden)
-    g_parts = [g_send[0]] + [shifted(g_send[k], -k) for k in range(1, mps)]
-    grad_normed = sum(g.astype(jnp.float32) for g in g_parts)
-    gradient = gradient + norm_pull(row_unit, row_scale, ln_row_gain[0], grad_normed)
-    grad_acts = from_work(low(gradient)).astype(jnp.float32)
-    grad_row_qkv = low(dot(all_tokens(hidden), all_tokens(g_qkv), token_dims))
-
-    rank_axes = (DP, SEQ)
-
-    def reduced(parts):
-        mine = lax.psum_scatter(parts, rank_axes, scatter_dimension=0, tiled=True)
-        size = mine.shape[-1] // mps
-        pieces = [mine[..., :size]] + [
-            shifted(mine[..., k * size : (k + 1) * size], -k) for k in range(1, mps)
-        ]
-        return sum(p.astype(jnp.float32) for p in pieces)
-
-    ffn_total = reduced(grad_ffn)
-    attention_total = reduced(grad_attention)
-    row_total = lax.psum_scatter(
-        grad_row_qkv, rank_axes, scatter_dimension=0, tiled=True
-    ).astype(jnp.float32)
-
-    row_hidden_unit = (hidden.astype(jnp.float32) - ln_row_bias[0]) / ln_row_gain[0]
-    grad_ln_row_gain, grad_ln_row_bias = total(g_hidden * row_hidden_unit), total(g_hidden)
-    here = (jnp.arange(mps) == z).astype(jnp.float32)[:, None]
-
-    def by_shard(v):
-        v = v.reshape(mps, -1)
-        near = (z - jnp.arange(mps)) % mps
-        return sum(
-            jnp.where((near[k] == jnp.arange(mps))[:, None], v[k], 0.0) for k in range(mps)
-        ).reshape(-1)
-
-    row_bias = [
-        (here * total(g_qkv[..., :hs])).reshape(-1),
-        (here * total(g_qkv[..., 2 * hs :])).reshape(-1),
-    ]
-    summed = lax.psum(
-        jnp.concatenate(
-            [
-                grad_ln_row_gain,
-                grad_ln_row_bias,
-                grad_row_bo,
-                grad_ln_col_gain,
-                grad_ln_col_bias,
-                grad_col_bo,
-                grad_ln_ffn_gain,
-                grad_ln_ffn_bias,
-                grad_b2,
-            ]
-            + row_bias
-            + [by_shard(grad_col_bq), by_shard(grad_col_bv), by_shard(grad_b1)]
-        ),
-        AXES,
-    )
+
+    def shard_of(k):
+        return finals[k // (mps // 2)][:, :, k % (mps // 2)]
+
+    ffn_mine = lax.psum_scatter(grad_ffn, (DP, SEQ), scatter_dimension=0, tiled=True)[0]
+    ffn_mine, gradient = together(ffn_mine, gradient)
+    ffn_total = lax.psum_scatter(ffn_mine, MP, scatter_dimension=0, tiled=True)[0].astype(f32)
+    got = together(
+        *send_from_work(low(gradient)),
+        *(shifted(low(shard_of(k)), -k) for k in range(1, mps)),
+        to_x(low(both(row_keep, row_peer, slice(part, None)))),
+        to_sibling(summed),
+    )
+    grad_acts = from_work(*got[:2])
+    row_arrived, summed = got[-2], summed + got[-1]
+    attention_total = shard_of(0) + sum(g.astype(f32) for g in got[2:-2])
+
+    row_total = (
+        both(row_keep, row_peer, upper)
+        + row_arrived[upper].astype(f32)
+        + to_y(low(both(row_keep, row_peer, lower) + row_arrived[lower].astype(f32))).astype(f32)
+    )
+    diagonal = routed(summed, lambda d, s, m: (d ^ 2, s ^ 1, m))
+    summed = summed + to_x(summed) + (to_y(summed) + diagonal)
     device = rank * mps + z
-    vectors = summed[: 9 * width].reshape(9, ranks * mps, -1)
+    vectors = summed[:9].reshape(9, ranks * mps, -1)
     vectors = lax.dynamic_index_in_dim(vectors, device, axis=1, keepdims=False)
-    biases = summed[9 * width :]
-
-    def of_shard(at, size):
-        return lax.dynamic_slice_in_dim(biases[at : at + mps * size], z * size, size)[None]
+    biases = summed[9:10]
 
     def transposed(v):
         return v.T[None]
 
     return (
-        out[None, :, None],
-        grad_acts[None, :, None],
+        from_work(*out_halves),
+        grad_acts,
         vectors[0][None],
         vectors[1][None],
         row_total[:, :hs][None],
         row_total[:, hs : 2 * hs][None],
-        row_total[:, 2 * hs :][None],
-        of_shard(0, hs),
-        of_shard(width, hs),
+        row_total[:, 2 * hs : 3 * hs][None],
+        biases[:, 2 * hs : 3 * hs],
+        biases[:, 3 * hs : 4 * hs],
         transposed(attention_total[:, 4]),
         vectors[2][None],
         vectors[3][None],
@@ -964,15 +1415,15 @@
         attention_total[:, 0][None],
         attention_total[:, 1][None],
         attention_total[:, 2][None],
-        of_shard(2 * width, hs),
-        of_shard(3 * width, hs),
+        biases[:, :hs],
+        biases[:, hs : 2 * hs],
         transposed(attention_total[:, 3]),
         vectors[5][None],
         vectors[6][None],
         vectors[7][None],
-        ffn_total[:, 0][None],
-        of_shard(4 * width, fs),
-        transposed(ffn_total[:, 1]),
+        ffn_total[:, :fs][None],
+        summed[10:11],
+        transposed(ffn_total[:, fs:]),
         vectors[8][None],
     )
 
@@ -1007,7 +1458,7 @@
         P(None, MP, None),
         P(),
     )
-    in_pairs = mesh.shape[SEQ] == 2 and mesh.shape[DP] % 2 == 0
+    in_pairs = tuple(mesh.shape[axis] for axis in AXES) == (4, 2, 4)
     return jax.shard_map(
         on_device_columns if in_pairs else on_device,
         mesh=mesh,

time: 513 us -> 340 us (0.66)
  local copies, waits for them, and re-layouts: 104 us -> 23.1 us
  Pallas kernels: 0 us -> 75.6 us
  matrix products: 73.6 us -> 0.19 us
  blocking collectives: 42.5 us -> 0 us
  other arithmetic: 68.8 us -> 30.3 us
  waiting for transfers between devices: 149 us -> 125 us
  starting transfers between devices: 53.1 us -> 70.1 us
    pallas_call x0 -> x9, Pallas kernels: none -> 75.6 us  [kernel_call(): pl.pallas_call(body, name=name, out_shape=[jax.ShapeDtypeStruct(shape, ki...]
    dot_general x35 -> x1, matrix products: 67.9 us -> 0.19 us  [on_device_columns(): jnp.einsum('kz,zsi->ski', pick, mask.reshape(mps, 2, half).astype(f32), p...]
    psum x1 -> x0, blocking collectives: 42.5 us -> none  [on_device_columns(): lax.psum(jnp.concatenate([grad_ln_row_gain, grad_ln_row_bias, grad_row_bo...]
    reduce_scatter x3 -> x2, waiting for transfers between devices: 43 us -> 3.32 us  [the longest x1 3.3 us: on_device_columns(): lax.psum_scatter(ffn_mine, MP, scatter_dimension=0, tiled=True)[0]]
    unnamed x299 -> x100, local copies, waits for them, and re-layouts: 31.2 us -> 10.7 us
    ppermute x35 -> x47, starting transfers between devices: 52.7 us -> 70 us  [routed(): return lax.ppermute(values, AXES, pairs)]
    ppermute x35 -> x47, waiting for transfers between devices: 106 us -> 122 us  [routed(): return lax.ppermute(values, AXES, pairs)]
    reshape x29 -> x3, local copies, waits for them, and re-layouts: 17.1 us -> 0.92 us  [the longest x1 0.76 us: on_device_columns(): finals = [(chip_sum(i, upper) + arrived[i][upper].astype(f32) + second[i]...]
  transfers between devices with their start and end apart: 40 -> 50, of which waited for: 14 -> 20; matrix products, arithmetic and copies ran while one was open for 30% -> 12% of each run, Pallas kernels for 0% -> 16%
where the time goes in v1:
time: 340 us; the launch traced here: 339 us
  waiting for transfers between devices  125 us (37%)
  Pallas kernels  75.6 us (22%)
  starting transfers between devices  70.1 us (21%)
  other arithmetic  30.3 us (9%)
  local copies, waits for them, and re-layouts  23.1 us (7%)
  between operations  14.5 us (4%)
    ppermute x47, waiting for transfers between devices, routed(): return lax.ppermute(values, AXES, pairs)  122 us
    pallas_call x9, Pallas kernels, kernel_call(): pl.pallas_call(body, name=name, out_shape=[jax.ShapeDtypeStruct(shape, ki...  75.6 us
    ppermute x47, starting transfers between devices, routed(): return lax.ppermute(values, AXES, pairs)  70 us
    unnamed x100, local copies, waits for them, and re-layouts  10.7 us
    convert_element_type x7, other arithmetic, low(): return values.astype(jnp.bfloat16)  9.43 us
  transfers between devices with their start and end apart: 50, of which 20 were waited for; matrix products, arithmetic and copies ran while one was open for 12% of the time, Pallas kernels for 16%

profile of v1, /device:TPU:0, one launch (start us, length us, event | category | flops | bytes accessed | tf_op | source)
XLA Modules:
  0.0 339.2 jit_solution(12649597036430920158)
XLA Ops:
  13.0 3.7 %pack.1 = (bf16[1024,768]{1,0:T(8,128)(2,1)}, bf16[144,768]{1,0:T(8,128)(2,1)}, bf16[192,768]{1,0:T(8,128)(2,1)}) custom-call(s32[2]{0:T(128)} %pad_add_fusion.refs_0_.rank, bf16[192,768]{1,0:T(8,128)(2,1)} %bitcast.152, bf16[192,768]{1,0:T(8,128)(2,1)} %bitcast.153, bf16[192,768]{1,0:T(8,128)(2,1)} %bitcast.154, bf16[192,768]{1,0:T(8,128)(2,1)} %bitcast.155, ...), custom_call_target="tpu_custom_call" | custom-call | bytes 6746120 | tf_op jit(solution)/shard_map/pack/pallas_call | solution.py:655
  18.2 7.4 %collective-permute-done.1 = bf16[256,768]{1,0:T(8,128)(2,1)S(1)} collective-permute-done((bf16[256,768]{1,0:T(8,128)(2,1)S(1)}, bf16[256,768]{1,0:T(8,128)(2,1)S(1)}, u32[]{:S(2)}, u32[]{:S(2)}) %collective-permute-start.1) | collective-permute-done | bytes 393248 | tf_op jit(solution)/shard_map/ppermute | solution.py:541
  26.3 2.2 collective-permute-start.2
  28.5 2.6 collective-permute-start.3
  33.7 4.1 %collective-permute-done.2 = bf16[144,768]{1,0:T(8,128)(2,1)S(1)} collective-permute-done((bf16[144,768]{1,0:T(8,128)(2,1)S(1)}, bf16[144,768]{1,0:T(8,128)(2,1)S(1)}, u32[]{:S(2)}, u32[]{:S(2)}) %collective-permute-start.2) | collective-permute-done | bytes 221216 | tf_op jit(solution)/shard_map/ppermute | solution.py:541
  37.8 14.5 %collective-permute-done.3 = bf16[144,768]{1,0:T(8,128)(2,1)S(1)} collective-permute-done((bf16[144,768]{1,0:T(8,128)(2,1)S(1)}, bf16[144,768]{1,0:T(8,128)(2,1)S(1)}, u32[]{:S(2)}, u32[]{:S(2)}) %collective-permute-start.3) | collective-permute-done | bytes 221216 | tf_op jit(solution)/shard_map/ppermute | solution.py:541
  52.3 5.3 %collective-permute-start.5 = (bf16[256,768]{1,0:T(8,128)(2,1)S(1)}, bf16[256,768]{1,0:T(8,128)(2,1)}, u32[]{:S(2)}, u32[]{:S(2)}) collective-permute-start(bf16[256,768]{1,0:T(8,128)(2,1)S(1)} %add_convert_fusion.2.refs_0_.refs_1_), channel_id=1, source_target_pairs={{0,1},{1,2},{2,3},{3,0},{4,5},{5,6},{6,7},{7,4},{8,9},{9,10},{10,1... | collective-permute-start | bytes 1179656 | tf_op jit(solution)/shard_map/ppermute | solution.py:541
  57.6 2.4 collective-permute-start.7
  64.3 9.3 %collective-permute-done.8.refs_5_.refs_1_ = bf16[3,64,768]{2,1,0:T(8,128)(2,1)S(1)} collective-permute-done((bf16[3,64,768]{2,1,0:T(8,128)(2,1)}, bf16[3,64,768]{2,1,0:T(8,128)(2,1)S(1)}, u32[]{:S(2)}, u32[]{:S(2)}) %collective-permute-start.8) | collective-permute-done | bytes 294944 | tf_op jit(solution)/shard_map/ppermute | solution.py:541
  73.5 22.9 %collective-permute-done.6.refs_2_.refs_3_ = bf16[256,768]{1,0:T(8,128)(2,1)} collective-permute-done((bf16[256,768]{1,0:T(8,128)(2,1)S(1)}, bf16[256,768]{1,0:T(8,128)(2,1)}, u32[]{:S(2)}, u32[]{:S(2)}) %collective-permute-start.6) | collective-permute-done | bytes 393248 | tf_op jit(solution)/shard_map/ppermute | solution.py:541
  96.5 4.1 %row_project.1 = (bf16[3,512,128]{2,1,0:T(8,128)(2,1)}, bf16[6,512,128]{2,1,0:T(8,128)(2,1)}) custom-call(bf16[256,768]{1,0:T(8,128)(2,1)} %copy-done.10, bf16[256,768]{1,0:T(8,128)(2,1)} %collective-permute-done.5.refs_1_.refs_2_, bf16[256,768]{1,0:T(8,128)(2,1)} %collective-permute-done.6.refs_2_.refs_3_, ...), custom_call_target="tpu_custom_call" | custom-call | flops 1006632960 | bytes 3738112 | tf_op jit(solution)/shard_map/row_project/pallas_call | solution.py:655
  105.5 9.1 %row_attend.1 = (bf16[3,512,1024]{2,1,0:T(8,128)(2,1)}, bf16[3,128,128]{2,1,0:T(8,128)(2,1)}, bf16[3,128,128]{2,1,0:T(8,128)(2,1)}, bf16[3,128,128]{2,1,0:T(8,128)(2,1)}, bf16[3,128,128]{2,1,0:T(8,128)(2,1)}) custom-call(bf16[3,512,128]{2,1,0:T(8,128)(2,1)} %get-tuple-element.118.q.refs_0_, bf16[6,512,128]{2,1,0:T(8,128)(2,1)} %get-tuple-element.119.kv.refs_1_, ...), custom_call_target="tpu_custom_call" | custom-call | flops 805306368 | bytes 5509120 | tf_op jit(solution)/shard_map/row_attend/pallas_call | solution.py:655
  114.6 11.9 %collective-permute-start.11 = (bf16[3,128,128]{2,1,0:T(8,128)(2,1)}, bf16[3,128,128]{2,1,0:T(8,128)(2,1)S(1)}, u32[]{:S(2)}, u32[]{:S(2)}) collective-permute-start(bf16[3,128,128]{2,1,0:T(8,128)(2,1)} %get-tuple-element.121), channel_id=1, source_target_pairs={{0,3},{1,0},{2,1},{3,2},{4,7},{5,4},{6,5},{7,6},{8,11},{9,8},{10,9... | collective-permute-start | bytes 294920 | tf_op jit(solution)/shard_map/ppermute | solution.py:541
  127.1 3.1 collective-permute-done.15.refs_8_.refs_4_
  131.1 10.5 %collective-permute-done.12.refs_2_ = bf16[3,128,128]{2,1,0:T(8,128)(2,1)S(1)} collective-permute-done((bf16[3,128,128]{2,1,0:T(8,128)(2,1)}, bf16[3,128,128]{2,1,0:T(8,128)(2,1)S(1)}, u32[]{:S(2)}, u32[]{:S(2)}) %collective-permute-start.12) | collective-permute-done | bytes 98336 | tf_op jit(solution)/shard_map/ppermute | solution.py:541
  146.9 8.5 %column.1 = (bf16[256,768]{1,0:T(8,128)(2,1)}, f32[256,768]{1,0:T(8,128)}, bf16[256,768]{1,0:T(8,128)(2,1)}, bf16[256,768]{1,0:T(8,128)(2,1)}, bf16[256,768]{1,0...) custom-call(s32[2]{0:T(128)} %pad_add_fusion.refs_0_.rank, ...), custom_call_target="tpu_custom_call" | custom-call | flops 1509949440 | bytes 11968520 | tf_op jit(solution)/shard_map/column/pallas_call | solution.py:655
  155.4 17.6 %ffn.1 = (bf16[256,768]{1,0:T(8,128)(2,1)}, f32[256,768]{1,0:T(8,128)}, bf16[256,768]{1,0:T(8,128)(2,1)}, bf16[8,4,96,1536]{3,2,1,0:T(8,128)(2,1)}, f32[8,768]{1,0:T(8,128)}, /*index=5*/f32[4,768]{1,0:T(4,128)}) custom-call(s32[2]{0:T(128)} %pad_add_fusion.refs_0_.rank, bf16[256,768]{1,0:T(8,128)(2,1)} %get-tuple-element.132.normed, ...), custom_call_target="tpu_custom_call" | custom-call | flops 7247757312 | bytes 22075400 | tf_op jit(solution)/shard_map/ffn/pallas_call | solution.py:655
  174.7 3.2 collective-permute-start.22
  177.9 10.2 %column_back.1 = (bf16[256,768]{1,0:T(8,128)(2,1)}, bf16[256,768]{1,0:T(8,128)(2,1)}, bf16[256,768]{1,0:T(8,128)(2,1)}, f32[256,768]{1,0:T(8,128)}, bf16[256,768...) custom-call(s32[2]{0:T(128)} %pad_add_fusion.refs_0_.rank, ...), custom_call_target="tpu_custom_call" | custom-call | flops 1509949440 | bytes 12364808 | tf_op jit(solution)/shard_map/column_back/pallas_call | solution.py:655
  188.1 4.3 %collective-permute-start.23 = (bf16[3,128,128]{2,1,0:T(8,128)(2,1)}, bf16[3,128,128]{2,1,0:T(8,128)(2,1)S(1)}, u32[]{:S(2)}, u32[]{:S(2)}) collective-permute-start(bf16[3,128,128]{2,1,0:T(8,128)(2,1)} %get-tuple-element.146), channel_id=1, source_target_pairs={{0,1},{1,2},{2,3},{3,0},{4,5},{5,6},{6,7},{7,4},{8,9},{9,10},{10,1... | collective-permute-start | bytes 294920 | tf_op jit(solution)/shard_map/ppermute | solution.py:541
  192.4 1.8 collective-permute-start.24
  194.2 2.8 collective-permute-start.25
  197.1 4.0 %collective-permute-done.24.refs_6_ = bf16[3,128,128]{2,1,0:T(8,128)(2,1)S(1)} collective-permute-done((bf16[3,128,128]{2,1,0:T(8,128)(2,1)}, bf16[3,128,128]{2,1,0:T(8,128)(2,1)S(1)}, u32[]{:S(2)}, u32[]{:S(2)}) %collective-permute-start.24) | collective-permute-done | bytes 98336 | tf_op jit(solution)/shard_map/ppermute | solution.py:541
  201.9 8.5 %row_attend_back.1 = (bf16[3,512,128]{2,1,0:T(8,128)(2,1)}, f32[6,512,128]{2,1,0:T(8,128)}, bf16[6,512,128]{2,1,0:T(8,128)(2,1)}) custom-call(bf16[3,512,128]{2,1,0:T(8,128)(2,1)} %get-tuple-element.118.q.refs_0_, bf16[6,512,128]{2,1,0:T(8,128)(2,1)} %get-tuple-element.119.kv.refs_1_, bf16[6,512,128]{2,1,0:T(8,128)(2,1)} %collective-permute-done.10.kv_sibling.refs_2_, ...), custom_call_target="tpu_custom_call" | custom-call | flops 1610612736 | bytes 8650752 | tf_op jit(solution)/shard_map/row_attend_back/pallas_call | solution.py:655
  210.4 2.5 collective-permute-done.26.refs_9_.refs_10_
  213.8 7.1 %weights.1 = (bf16[2,384,1920]{2,1,0:T(8,128)(2,1)}, bf16[2,384,1920]{2,1,0:T(8,128)(2,1)}) custom-call(s32[2]{0:T(128)} %pad_add_fusion.refs_0_.rank, bf16[256,768]{1,0:T(8,128)(2,1)} %get-tuple-element.155.refs_1_, bf16[256,768]{1,0:T(8,128)(2,1)} %get-tuple-element.138.grad_low.refs_2_, bf16[256,768]{1,0:T(8,128)(2,1)} %get-tuple-element.156.refs_3_, ...), custom_call_target="tpu_custom_call" | custom-call | flops 1509949440 | bytes 9830408 | tf_op jit(solution)/shard_map/weights/pallas_call | solution.py:655
  220.9 5.6 %collective-permute-done.29 = bf16[2,384,1920]{2,1,0:T(8,128)(2,1)S(1)} collective-permute-done((bf16[2,384,1920]{2,1,0:T(8,128)(2,1)}, bf16[2,384,1920]{2,1,0:T(8,128)(2,1)S(1)}, u32[]{:S(2)}, u32[]{:S(2)}) %collective-permute-start.29) | collective-permute-done | bytes 2949152 | tf_op jit(solution)/shard_map/ppermute | solution.py:541
  226.5 3.9 %fusion.1 = (bf16[192,1920]{1,0:T(8,128)(2,1)}, bf16[192,1920]{1,0:T(8,128)(2,1)}) fusion(bf16[2,384,1920]{2,1,0:T(8,128)(2,1)S(1)} %collective-permute-done.29, bf16[2,384,1920]{2,1,0:T(8,128)(2,1)} %get-tuple-element.162.refs_14_), kind=kLoop, calls=%fused_computation.11 | loop fusion | flops 2949120 | bytes 4423680 | tf_op jit(solution)/shard_map/convert_element_type | solution.py:609
  231.1 6.8 %row_project_back.1 = (bf16[384,640]{1,0:T(8,128)(2,1)}, bf16[384,640]{1,0:T(8,128)(2,1)}, f32[1,640]{1,0:T(1,128)}, bf16[272,768]{1,0:T(8,128)(2,1)}, bf16[272,...) custom-call(s32[2]{0:T(128)} %pad_add_fusion.refs_0_.rank, bf16[256,768]{1,0:T(8,128)(2,1)} %copy-done.10, ...), custom_call_target="tpu_custom_call" | custom-call | flops 2013265920 | bytes 10981896 | tf_op jit(solution)/shard_map/row_project_back/pallas_call | solution.py:655
  238.0 4.9 %collective-permute-start.27 = (bf16[272,768]{1,0:T(8,128)(2,1)}, bf16[272,768]{1,0:T(8,128)(2,1)S(1)}, u32[]{:S(2)}, u32[]{:S(2)}) collective-permute-start(bf16[272,768]{1,0:T(8,128)(2,1)} %get-tuple-element.164), channel_id=1, source_target_pairs={{0,3},{1,0},{2,1},{3,2},{4,7},{5,4},{6,5},{7,6},{8,11},{9,8},{10,9... | collective-permute-start | bytes 1253384 | tf_op jit(solution)/shard_map/ppermute | solution.py:541
  244.3 8.9 %collective-permute-done.27 = bf16[272,768]{1,0:T(8,128)(2,1)S(1)} collective-permute-done((bf16[272,768]{1,0:T(8,128)(2,1)}, bf16[272,768]{1,0:T(8,128)(2,1)S(1)}, u32[]{:S(2)}, u32[]{:S(2)}) %collective-permute-start.27) | collective-permute-done | bytes 417824 | tf_op jit(solution)/shard_map/ppermute | solution.py:541
  254.1 8.5 %collective-permute-done.28 = bf16[272,768]{1,0:T(8,128)(2,1)S(1)} collective-permute-done((bf16[272,768]{1,0:T(8,128)(2,1)}, bf16[272,768]{1,0:T(8,128)(2,1)S(1)}, u32[]{:S(2)}, u32[]{:S(2)}) %collective-permute-start.28) | collective-permute-done | bytes 417824 | tf_op jit(solution)/shard_map/ppermute | solution.py:541
  262.7 1.8 fusion.5
  264.5 1.7 collective-permute-start.34
  266.2 2.4 collective-permute-start.35
  268.6 1.7 add_convert_fusion.3
  270.3 9.8 %collective-permute-done.33 = bf16[272,768]{1,0:T(8,128)(2,1)S(1)} collective-permute-done((bf16[272,768]{1,0:T(8,128)(2,1)}, bf16[272,768]{1,0:T(8,128)(2,1)S(1)}, u32[]{:S(2)}, u32[]{:S(2)}) %collective-permute-start.33) | collective-permute-done | bytes 417824 | tf_op jit(solution)/shard_map/ppermute | solution.py:541
  281.0 2.6 fusion.3
  287.2 2.3 collective-permute-start.40
  293.1 1.6 fusion.25
  295.9 1.6 collective-permute-start.36
  297.5 2.3 collective-permute-start.37
  299.9 1.7 copy.74
  302.0 3.7 %collective-permute-done.39 = bf16[96,5,192]{2,0,1:T(8,128)(2,1)S(1)} collective-permute-done((bf16[96,5,192]{2,0,1:T(8,128)(2,1)}, bf16[96,5,192]{2,0,1:T(8,128)(2,1)S(1)}, u32[]{:S(2)}, u32[]{:S(2)}) %collective-permute-start.39) | collective-permute-done | bytes 184352 | tf_op jit(solution)/shard_map/ppermute | solution.py:541
  305.7 4.9 %collective-permute-done.38 = bf16[96,5,192]{2,0,1:T(8,128)(2,1)S(1)} collective-permute-done((bf16[96,5,192]{2,0,1:T(8,128)(2,1)}, bf16[96,5,192]{2,0,1:T(8,128)(2,1)S(1)}, u32[]{:S(2)}, u32[]{:S(2)}) %collective-permute-start.38) | collective-permute-done | bytes 184352 | tf_op jit(solution)/shard_map/ppermute | solution.py:541
  310.7 4.0 %collective-permute-start.43 = (f32[11,768]{1,0:T(8,128)S(1)}, f32[11,768]{1,0:T(8,128)S(1)}, u32[]{:S(2)}, u32[]{:S(2)}) collective-permute-start(f32[11,768]{1,0:T(8,128)S(1)} %fusion.36), channel_id=1, source_target_pairs={{0,4},{1,5},{2,6},{3,7},{4,0},{5,1},{6,2},{7,3},{8,12},{9,13},{10,... | collective-permute-start | bytes 101384 | tf_op jit(solution)/shard_map/ppermute | solution.py:541
  322.0 1.7 copy.75
  327.5 3.3 reduce-scatter.5.cloned.1.call-done
  (257 shorter events, 55.4 us)
Async XLA Ops:
  7.2 148.2 %all-gather.3.cloned.1.call-start = ((), (), s32[]{:S(2)}) async-start(), calls=%async_computation.4 | async-start | bytes 9732096 | tf_op jit(solution)/shard_map/all_gather | solution.py:1149
  16.8 278.3 %reduce-scatter.3.cloned.1.call-start = ((), (), s32[]{:S(2)}) async-start(), calls=%async_computation.2 | async-start | bytes 10616832 | tf_op jit(solution)/shard_map/reduce_scatter | solution.py:1373
  16.9 8.7 %collective-permute-start.1 = (bf16[256,768]{1,0:T(8,128)(2,1)S(1)}, bf16[256,768]{1,0:T(8,128)(2,1)S(1)}, u32[]{:S(2)}, u32[]{:S(2)}) collective-permute-start(bf16[256,768]{1,0:T(8,128)(2,1)S(1)} %copy-done.11), channel_id=1, source_target_pairs={{0,8},{1,9},{2,10},{3,11},{4,0},{5,1},{6,2},{7,3},{8,12},{9,13},{1... | collective-permute-start | bytes 1179656 | tf_op jit(solution)/shard_map/ppermute | solution.py:541
  17.3 8.3 %collective-permute-start = (bf16[264,768]{1,0:T(8,128)(2,1)S(1)}, bf16[264,768]{1,0:T(8,128)(2,1)S(1)}, u32[]{:S(2)}, u32[]{:S(2)}) collective-permute-start(bf16[264,768]{1,0:T(8,128)(2,1)S(1)} %copy-done.9), channel_id=1, source_target_pairs={{0,0},{1,1},{2,2},{3,3},{4,8},{5,9},{6,10},{7,11},{8,4},{9,5},{10,... | collective-permute-start | bytes 1216520 | tf_op jit(solution)/shard_map/ppermute | solution.py:541
  26.3 11.5 %collective-permute-start.2 = (bf16[144,768]{1,0:T(8,128)(2,1)S(1)}, bf16[144,768]{1,0:T(8,128)(2,1)S(1)}, u32[]{:S(2)}, u32[]{:S(2)}) collective-permute-start(bf16[144,768]{1,0:T(8,128)(2,1)S(1)} %copy-done.42), channel_id=1, source_target_pairs={{0,1},{1,2},{2,3},{3,0},{4,5},{5,6},{6,7},{7,4},{8,9},{9,10},{10,1... | collective-permute-start | bytes 663560 | tf_op jit(solution)/shard_map/ppermute | solution.py:541
  28.5 23.8 %collective-permute-start.3 = (bf16[144,768]{1,0:T(8,128)(2,1)S(1)}, bf16[144,768]{1,0:T(8,128)(2,1)S(1)}, u32[]{:S(2)}, u32[]{:S(2)}) collective-permute-start(bf16[144,768]{1,0:T(8,128)(2,1)S(1)} %copy-done.42), channel_id=1, source_target_pairs={{0,2},{1,3},{2,0},{3,1},{4,6},{5,7},{6,4},{7,5},{8,10},{9,11},{10,... | collective-permute-start | bytes 663560 | tf_op jit(solution)/shard_map/ppermute | solution.py:541
  31.1 21.2 %collective-permute-start.4 = (bf16[144,768]{1,0:T(8,128)(2,1)S(1)}, bf16[144,768]{1,0:T(8,128)(2,1)S(1)}, u32[]{:S(2)}, u32[]{:S(2)}) collective-permute-start(bf16[144,768]{1,0:T(8,128)(2,1)S(1)} %copy-done.42), channel_id=1, source_target_pairs={{0,3},{1,0},{2,1},{3,2},{4,7},{5,4},{6,5},{7,6},{8,11},{9,8},{10,9... | collective-permute-start | bytes 663560 | tf_op jit(solution)/shard_map/ppermute | solution.py:541
  52.3 21.2 %collective-permute-start.5 = (bf16[256,768]{1,0:T(8,128)(2,1)S(1)}, bf16[256,768]{1,0:T(8,128)(2,1)}, u32[]{:S(2)}, u32[]{:S(2)}) collective-permute-start(bf16[256,768]{1,0:T(8,128)(2,1)S(1)} %add_convert_fusion.2.refs_0_.refs_1_), channel_id=1, source_target_pairs={{0,1},{1,2},{2,3},{3,0},{4,5},{5,6},{6,7},{7,4},{8,9},{9,10},{10,1... | collective-permute-start | bytes 1179656 | tf_op jit(solution)/shard_map/ppermute | solution.py:541
  57.6 38.8 %collective-permute-start.6 = (bf16[256,768]{1,0:T(8,128)(2,1)S(1)}, bf16[256,768]{1,0:T(8,128)(2,1)}, u32[]{:S(2)}, u32[]{:S(2)}) collective-permute-start(bf16[256,768]{1,0:T(8,128)(2,1)S(1)} %add_convert_fusion.2.refs_0_.refs_1_), channel_id=1, source_target_pairs={{0,2},{1,3},{2,0},{3,1},{4,6},{5,7},{6,4},{7,5},{8,10},{9,11},{10,... | collective-permute-start | bytes 1179656 | tf_op jit(solution)/shard_map/ppermute | solution.py:541
  57.6 38.8 %collective-permute-start.7 = (bf16[256,768]{1,0:T(8,128)(2,1)S(1)}, bf16[256,768]{1,0:T(8,128)(2,1)}, u32[]{:S(2)}, u32[]{:S(2)}) collective-permute-start(bf16[256,768]{1,0:T(8,128)(2,1)S(1)} %add_convert_fusion.2.refs_0_.refs_1_), channel_id=1, source_target_pairs={{0,3},{1,0},{2,1},{3,2},{4,7},{5,4},{6,5},{7,6},{8,11},{9,8},{10,9... | collective-permute-start | bytes 1179656 | tf_op jit(solution)/shard_map/ppermute | solution.py:541
  61.0 12.5 %collective-permute-start.8 = (bf16[3,64,768]{2,1,0:T(8,128)(2,1)}, bf16[3,64,768]{2,1,0:T(8,128)(2,1)S(1)}, u32[]{:S(2)}, u32[]{:S(2)}) collective-permute-start(bf16[3,64,768]{2,1,0:T(8,128)(2,1)} %get-tuple-element.280), channel_id=1, source_target_pairs={{0,4},{1,5},{2,6},{3,7},{4,0},{5,1},{6,2},{7,3},{8,12},{9,13},{10,... | collective-permute-start | bytes 884744 | tf_op jit(solution)/shard_map/ppermute | solution.py:541
  61.0 12.5 %collective-permute-start.9 = (bf16[3,64,768]{2,1,0:T(8,128)(2,1)S(1)}, bf16[3,64,768]{2,1,0:T(8,128)(2,1)S(1)}, u32[]{:S(2)}, u32[]{:S(2)}) collective-permute-start(bf16[3,64,768]{2,1,0:T(8,128)(2,1)S(1)} %get-tuple-element.279), channel_id=1, source_target_pairs={{0,16},{1,17},{2,18},{3,19},{4,20},{5,21},{6,22},{7,23},{8,24},{9,... | collective-permute-start | bytes 884744 | tf_op jit(solution)/shard_map/ppermute | solution.py:541
  100.5 4.9 %collective-permute-start.10 = (bf16[6,512,128]{2,1,0:T(8,128)(2,1)}, bf16[6,512,128]{2,1,0:T(8,128)(2,1)}, u32[]{:S(2)}, u32[]{:S(2)}) collective-permute-start(bf16[6,512,128]{2,1,0:T(8,128)(2,1)} %get-tuple-element.119.kv.refs_1_), channel_id=1, source_target_pairs={{0,8},{1,9},{2,10},{3,11},{4,12},{5,13},{6,14},{7,15},{8,0},{9,1},... | collective-permute-start | bytes 2359304 | tf_op jit(solution)/shard_map/ppermute | solution.py:541
  101.6 28.6 %collective-permute-start.15 = (bf16[2,3,64,768]{3,2,1,0:T(8,128)(2,1)}, bf16[2,3,64,768]{3,2,1,0:T(8,128)(2,1)S(1)}, u32[]{:S(2)}, u32[]{:S(2)}) collective-permute-start(bf16[2,3,64,768]{3,2,1,0:T(8,128)(2,1)} %pad_maximum_fusion.2), channel_id=1, source_target_pairs={{0,4},{1,5},{2,6},{3,7},{4,0},{5,1},{6,2},{7,3},{8,12},{9,13},{10,... | collective-permute-start | bytes 1769480 | tf_op jit(solution)/shard_map/ppermute | solution.py:541
  102.5 28.5 %collective-permute-start.14 = (bf16[2,3,64,768]{3,2,1,0:T(8,128)(2,1)}, bf16[2,3,64,768]{3,2,1,0:T(8,128)(2,1)S(1)}, u32[]{:S(2)}, u32[]{:S(2)}) collective-permute-start(bf16[2,3,64,768]{3,2,1,0:T(8,128)(2,1)} %pad_maximum_fusion.1), channel_id=1, source_target_pairs={{0,16},{1,17},{2,18},{3,19},{4,20},{5,21},{6,22},{7,23},{8,24},{9,... | collective-permute-start | bytes 1769480 | tf_op jit(solution)/shard_map/ppermute | solution.py:541
  114.6 16.5 %collective-permute-start.11 = (bf16[3,128,128]{2,1,0:T(8,128)(2,1)}, bf16[3,128,128]{2,1,0:T(8,128)(2,1)S(1)}, u32[]{:S(2)}, u32[]{:S(2)}) collective-permute-start(bf16[3,128,128]{2,1,0:T(8,128)(2,1)} %get-tuple-element.121), channel_id=1, source_target_pairs={{0,3},{1,0},{2,1},{3,2},{4,7},{5,4},{6,5},{7,6},{8,11},{9,8},{10,9... | collective-permute-start | bytes 294920 | tf_op jit(solution)/shard_map/ppermute | solution.py:541
  126.5 15.1 %collective-permute-start.12 = (bf16[3,128,128]{2,1,0:T(8,128)(2,1)}, bf16[3,128,128]{2,1,0:T(8,128)(2,1)S(1)}, u32[]{:S(2)}, u32[]{:S(2)}) collective-permute-start(bf16[3,128,128]{2,1,0:T(8,128)(2,1)} %get-tuple-element.122), channel_id=1, source_target_pairs={{0,2},{1,3},{2,0},{3,1},{4,6},{5,7},{6,4},{7,5},{8,10},{9,11},{10,... | collective-permute-start | bytes 294920 | tf_op jit(solution)/shard_map/ppermute | solution.py:541
  126.5 15.1 %collective-permute-start.13 = (bf16[3,128,128]{2,1,0:T(8,128)(2,1)}, bf16[3,128,128]{2,1,0:T(8,128)(2,1)S(1)}, u32[]{:S(2)}, u32[]{:S(2)}) collective-permute-start(bf16[3,128,128]{2,1,0:T(8,128)(2,1)} %get-tuple-element.123), channel_id=1, source_target_pairs={{0,1},{1,2},{2,3},{3,0},{4,5},{5,6},{6,7},{7,4},{8,9},{9,10},{10,1... | collective-permute-start | bytes 294920 | tf_op jit(solution)/shard_map/ppermute | solution.py:541
  130.2 14.9 %collective-permute-start.16 = (bf16[3,144,768]{2,1,0:T(8,128)(2,1)S(1)}, bf16[3,144,768]{2,1,0:T(8,128)(2,1)S(1)}, u32[]{:S(2)}, u32[]{:S(2)}) collective-permute-start(bf16[3,144,768]{2,1,0:T(8,128)(2,1)S(1)} %pad_maximum_fusion.refs_4_.refs_0_), channel_id=1, source_target_pairs={{0,8},{1,9},{2,10},{3,11},{4,12},{5,13},{6,14},{7,15},{8,0},{9,1},... | collective-permute-start | bytes 1990664 | tf_op jit(solution)/shard_map/ppermute | solution.py:541
  141.6 4.6 %collective-permute-start.19 = (bf16[2,3,64,768]{3,2,1,0:T(8,128)(2,1)S(1)}, bf16[2,3,64,768]{3,2,1,0:T(8,128)(2,1)}, u32[]{:S(2)}, u32[]{:S(2)}) collective-permute-start(bf16[2,3,64,768]{3,2,1,0:T(8,128)(2,1)S(1)} %collective-permute-done.14.refs_7_.refs_3_), channel_id=1, source_target_pairs={{0,8},{1,9},{2,10},{3,11},{4,12},{5,13},{6,14},{7,15},{8,0},{9,1},... | collective-permute-start | bytes 1769480 | tf_op jit(solution)/shard_map/ppermute | solution.py:541
  141.7 4.9 %collective-permute-start.20 = (bf16[2,3,64,768]{3,2,1,0:T(8,128)(2,1)S(1)}, bf16[2,3,64,768]{3,2,1,0:T(8,128)(2,1)}, u32[]{:S(2)}, u32[]{:S(2)}) collective-permute-start(bf16[2,3,64,768]{3,2,1,0:T(8,128)(2,1)S(1)} %collective-permute-done.15.refs_8_.refs_4_), channel_id=1, source_target_pairs={{0,8},{1,9},{2,10},{3,11},{4,12},{5,13},{6,14},{7,15},{8,0},{9,1},... | collective-permute-start | bytes 1769480 | tf_op jit(solution)/shard_map/ppermute | solution.py:541
  142.7 3.5 %collective-permute-start.18 = (bf16[3,64,768]{2,1,0:T(8,128)(2,1)S(1)}, bf16[3,64,768]{2,1,0:T(8,128)(2,1)S(1)}, u32[]{:S(2)}, u32[]{:S(2)}) collective-permute-start(bf16[3,64,768]{2,1,0:T(8,128)(2,1)S(1)} %collective-permute-done.9.refs_6_.refs_2_), channel_id=1, source_target_pairs={{0,8},{1,9},{2,10},{3,11},{4,12},{5,13},{6,14},{7,15},{8,0},{9,1},... | collective-permute-start | bytes 884744 | tf_op jit(solution)/shard_map/ppermute | solution.py:541
  173.1 157.7 %reduce-scatter.5.cloned.1.call-start = ((), (), s32[]{:S(2)}) async-start(), calls=%async_computation.3 | async-start | bytes 1474560 | tf_op jit(solution)/shard_map/reduce_scatter | solution.py:1375
  174.1 27.0 %collective-permute-start.21 = (bf16[128,768]{1,0:T(8,128)(2,1)S(1)}, bf16[128,768]{1,0:T(8,128)(2,1)S(1)}, u32[]{:S(2)}, u32[]{:S(2)}) collective-permute-start(bf16[128,768]{1,0:T(8,128)(2,1)S(1)} %get-tuple-element.298), channel_id=1, source_target_pairs={{0,0},{1,1},{2,2},{3,3},{4,8},{5,9},{6,10},{7,11},{8,4},{9,5},{10,... | collective-permute-start | bytes 589832 | tf_op jit(solution)/shard_map/ppermute | solution.py:541
  174.7 26.3 %collective-permute-start.22 = (bf16[128,768]{1,0:T(8,128)(2,1)S(1)}, bf16[128,768]{1,0:T(8,128)(2,1)S(1)}, u32[]{:S(2)}, u32[]{:S(2)}) collective-permute-start(bf16[128,768]{1,0:T(8,128)(2,1)S(1)} %get-tuple-element.299), channel_id=1, source_target_pairs={{0,4},{1,5},{2,6},{3,7},{4,12},{5,13},{6,14},{7,15},{8,0},{9,1},{1... | collective-permute-start | bytes 589832 | tf_op jit(solution)/shard_map/ppermute | solution.py:541
  188.1 9.0 %collective-permute-start.23 = (bf16[3,128,128]{2,1,0:T(8,128)(2,1)}, bf16[3,128,128]{2,1,0:T(8,128)(2,1)S(1)}, u32[]{:S(2)}, u32[]{:S(2)}) collective-permute-start(bf16[3,128,128]{2,1,0:T(8,128)(2,1)} %get-tuple-element.146), channel_id=1, source_target_pairs={{0,1},{1,2},{2,3},{3,0},{4,5},{5,6},{6,7},{7,4},{8,9},{9,10},{10,1... | collective-permute-start | bytes 294920 | tf_op jit(solution)/shard_map/ppermute | solution.py:541
  192.4 8.6 %collective-permute-start.24 = (bf16[3,128,128]{2,1,0:T(8,128)(2,1)}, bf16[3,128,128]{2,1,0:T(8,128)(2,1)S(1)}, u32[]{:S(2)}, u32[]{:S(2)}) collective-permute-start(bf16[3,128,128]{2,1,0:T(8,128)(2,1)} %get-tuple-element.147), channel_id=1, source_target_pairs={{0,2},{1,3},{2,0},{3,1},{4,6},{5,7},{6,4},{7,5},{8,10},{9,11},{10,... | collective-permute-start | bytes 294920 | tf_op jit(solution)/shard_map/ppermute | solution.py:541
  194.2 6.8 %collective-permute-start.25 = (bf16[3,128,128]{2,1,0:T(8,128)(2,1)}, bf16[3,128,128]{2,1,0:T(8,128)(2,1)S(1)}, u32[]{:S(2)}, u32[]{:S(2)}) collective-permute-start(bf16[3,128,128]{2,1,0:T(8,128)(2,1)} %get-tuple-element.148), channel_id=1, source_target_pairs={{0,3},{1,0},{2,1},{3,2},{4,7},{5,4},{6,5},{7,6},{8,11},{9,8},{10,9... | collective-permute-start | bytes 294920 | tf_op jit(solution)/shard_map/ppermute | solution.py:541
  220.9 5.6 %collective-permute-start.29 = (bf16[2,384,1920]{2,1,0:T(8,128)(2,1)}, bf16[2,384,1920]{2,1,0:T(8,128)(2,1)S(1)}, u32[]{:S(2)}, u32[]{:S(2)}) collective-permute-start(bf16[2,384,1920]{2,1,0:T(8,128)(2,1)} %get-tuple-element.166), channel_id=1, source_target_pairs={{0,8},{1,9},{2,10},{3,11},{4,12},{5,13},{6,14},{7,15},{8,0},{9,1},... | collective-permute-start | bytes 8847368 | tf_op jit(solution)/shard_map/ppermute | solution.py:541
  230.4 32.2 %collective-permute-start.30 = (bf16[192,1920]{1,0:T(8,128)(2,1)}, bf16[192,1920]{1,0:T(8,128)(2,1)}, u32[]{:S(2)}, u32[]{:S(2)}) collective-permute-start(bf16[192,1920]{1,0:T(8,128)(2,1)} %get-tuple-element.276), channel_id=1, source_target_pairs={{0,4},{1,5},{2,6},{3,7},{4,0},{5,1},{6,2},{7,3},{8,12},{9,13},{10,... | collective-permute-start | bytes 2211848 | tf_op jit(solution)/shard_map/ppermute | solution.py:541
  231.1 31.6 %collective-permute-start.31 = (bf16[192,1920]{1,0:T(8,128)(2,1)}, bf16[192,1920]{1,0:T(8,128)(2,1)}, u32[]{:S(2)}, u32[]{:S(2)}) collective-permute-start(bf16[192,1920]{1,0:T(8,128)(2,1)} %get-tuple-element.275), channel_id=1, source_target_pairs={{0,16},{1,17},{2,18},{3,19},{4,20},{5,21},{6,22},{7,23},{8,24},{9,... | collective-permute-start | bytes 2211848 | tf_op jit(solution)/shard_map/ppermute | solution.py:541
  237.9 24.7 %collective-permute-start.32 = (bf16[384,640]{1,0:T(8,128)(2,1)}, bf16[384,640]{1,0:T(8,128)(2,1)}, u32[]{:S(2)}, u32[]{:S(2)}) collective-permute-start(bf16[384,640]{1,0:T(8,128)(2,1)} %get-tuple-element.167), channel_id=1, source_target_pairs={{0,8},{1,9},{2,10},{3,11},{4,12},{5,13},{6,14},{7,15},{8,0},{9,1},... | collective-permute-start | bytes 1474568 | tf_op jit(solution)/shard_map/ppermute | solution.py:541
  238.0 15.2 %collective-permute-start.27 = (bf16[272,768]{1,0:T(8,128)(2,1)}, bf16[272,768]{1,0:T(8,128)(2,1)S(1)}, u32[]{:S(2)}, u32[]{:S(2)}) collective-permute-start(bf16[272,768]{1,0:T(8,128)(2,1)} %get-tuple-element.164), channel_id=1, source_target_pairs={{0,3},{1,0},{2,1},{3,2},{4,7},{5,4},{6,5},{7,6},{8,11},{9,8},{10,9... | collective-permute-start | bytes 1253384 | tf_op jit(solution)/shard_map/ppermute | solution.py:541
  242.9 19.7 %collective-permute-start.28 = (bf16[272,768]{1,0:T(8,128)(2,1)}, bf16[272,768]{1,0:T(8,128)(2,1)S(1)}, u32[]{:S(2)}, u32[]{:S(2)}) collective-permute-start(bf16[272,768]{1,0:T(8,128)(2,1)} %get-tuple-element.165), channel_id=1, source_target_pairs={{0,1},{1,2},{2,3},{3,0},{4,5},{5,6},{6,7},{7,4},{8,9},{9,10},{10,1... | collective-permute-start | bytes 1253384 | tf_op jit(solution)/shard_map/ppermute | solution.py:541
  253.2 26.9 %collective-permute-start.33 = (bf16[272,768]{1,0:T(8,128)(2,1)}, bf16[272,768]{1,0:T(8,128)(2,1)S(1)}, u32[]{:S(2)}, u32[]{:S(2)}) collective-permute-start(bf16[272,768]{1,0:T(8,128)(2,1)} %get-tuple-element.169), channel_id=1, source_target_pairs={{0,2},{1,3},{2,0},{3,1},{4,6},{5,7},{6,4},{7,5},{8,10},{9,11},{10,... | collective-permute-start | bytes 1253384 | tf_op jit(solution)/shard_map/ppermute | solution.py:541
  264.5 15.7 %collective-permute-start.34 = (bf16[96,1920]{1,0:T(8,128)(2,1)S(1)}, bf16[96,1920]{1,0:T(8,128)(2,1)S(1)}, u32[]{:S(2)}, u32[]{:S(2)}) collective-permute-start(bf16[96,1920]{1,0:T(8,128)(2,1)S(1)} %get-tuple-element.274), channel_id=1, source_target_pairs={{0,16},{1,17},{2,18},{3,19},{4,20},{5,21},{6,22},{7,23},{8,24},{9,... | collective-permute-start | bytes 1105928 | tf_op jit(solution)/shard_map/ppermute | solution.py:541
  266.2 13.9 %collective-permute-start.35 = (bf16[96,1920]{1,0:T(8,128)(2,1)S(1)}, bf16[96,1920]{1,0:T(8,128)(2,1)S(1)}, u32[]{:S(2)}, u32[]{:S(2)}) collective-permute-start(bf16[96,1920]{1,0:T(8,128)(2,1)S(1)} %get-tuple-element.273), channel_id=1, source_target_pairs={{0,4},{1,5},{2,6},{3,7},{4,0},{5,1},{6,2},{7,3},{8,12},{9,13},{10,... | collective-permute-start | bytes 1105928 | tf_op jit(solution)/shard_map/ppermute | solution.py:541
  270.3 25.6 %collective-permute-start.41 = (bf16[192,640]{1,0:T(8,128)(2,1)}, bf16[192,640]{1,0:T(8,128)(2,1)}, u32[]{:S(2)}, u32[]{:S(2)}) collective-permute-start(bf16[192,640]{1,0:T(8,128)(2,1)} %add_convert_fusion.3), channel_id=1, source_target_pairs={{0,4},{1,5},{2,6},{3,7},{4,0},{5,1},{6,2},{7,3},{8,12},{9,13},{10,... | collective-permute-start | bytes 737288 | tf_op jit(solution)/shard_map/ppermute | solution.py:541
  281.0 16.5 %collective-permute-start.42 = (f32[11,768]{1,0:T(8,128)S(1)}, f32[11,768]{1,0:T(8,128)S(1)}, u32[]{:S(2)}, u32[]{:S(2)}) collective-permute-start(f32[11,768]{1,0:T(8,128)S(1)} %pad_maximum_fusion.7), channel_id=1, source_target_pairs={{0,8},{1,9},{2,10},{3,11},{4,12},{5,13},{6,14},{7,15},{8,0},{9,1},... | collective-permute-start | bytes 101384 | tf_op jit(solution)/shard_map/ppermute | solution.py:541
  286.5 19.2 %collective-permute-start.39 = (bf16[96,5,192]{2,0,1:T(8,128)(2,1)}, bf16[96,5,192]{2,0,1:T(8,128)(2,1)S(1)}, u32[]{:S(2)}, u32[]{:S(2)}) collective-permute-start(bf16[96,5,192]{2,0,1:T(8,128)(2,1)} %bitcast.144), channel_id=1, source_target_pairs={{0,2},{1,3},{2,0},{3,1},{4,6},{5,7},{6,4},{7,5},{8,10},{9,11},{10,... | collective-permute-start | bytes 552968 | tf_op jit(solution)/shard_map/ppermute | solution.py:541
  287.2 18.5 %collective-permute-start.40 = (bf16[96,5,192]{2,0,1:T(8,128)(2,1)}, bf16[96,5,192]{2,0,1:T(8,128)(2,1)}, u32[]{:S(2)}, u32[]{:S(2)}) collective-permute-start(bf16[96,5,192]{2,0,1:T(8,128)(2,1)} %bitcast.143), channel_id=1, source_target_pairs={{0,1},{1,2},{2,3},{3,0},{4,5},{5,6},{6,7},{7,4},{8,9},{9,10},{10,1... | collective-permute-start | bytes 552968 | tf_op jit(solution)/shard_map/ppermute | solution.py:541
  291.6 19.1 %collective-permute-start.38 = (bf16[96,5,192]{2,0,1:T(8,128)(2,1)}, bf16[96,5,192]{2,0,1:T(8,128)(2,1)S(1)}, u32[]{:S(2)}, u32[]{:S(2)}) collective-permute-start(bf16[96,5,192]{2,0,1:T(8,128)(2,1)} %bitcast.142), channel_id=1, source_target_pairs={{0,3},{1,0},{2,1},{3,2},{4,7},{5,4},{6,5},{7,6},{8,11},{9,8},{10,9... | collective-permute-start | bytes 552968 | tf_op jit(solution)/shard_map/ppermute | solution.py:541
  295.9 14.7 %collective-permute-start.36 = (bf16[128,768]{1,0:T(8,128)(2,1)}, bf16[128,768]{1,0:T(8,128)(2,1)S(1)}, u32[]{:S(2)}, u32[]{:S(2)}) collective-permute-start(bf16[128,768]{1,0:T(8,128)(2,1)} %get-tuple-element.295), channel_id=1, source_target_pairs={{0,0},{1,1},{2,2},{3,3},{4,8},{5,9},{6,10},{7,11},{8,4},{9,5},{10,... | collective-permute-start | bytes 589832 | tf_op jit(solution)/shard_map/ppermute | solution.py:541
  297.5 13.1 %collective-permute-start.37 = (bf16[128,768]{1,0:T(8,128)(2,1)}, bf16[128,768]{1,0:T(8,128)(2,1)S(1)}, u32[]{:S(2)}, u32[]{:S(2)}) collective-permute-start(bf16[128,768]{1,0:T(8,128)(2,1)} %get-tuple-element.294), channel_id=1, source_target_pairs={{0,4},{1,5},{2,6},{3,7},{4,12},{5,13},{6,14},{7,15},{8,0},{9,1},{1... | collective-permute-start | bytes 589832 | tf_op jit(solution)/shard_map/ppermute | solution.py:541
  310.7 13.0 %collective-permute-start.43 = (f32[11,768]{1,0:T(8,128)S(1)}, f32[11,768]{1,0:T(8,128)S(1)}, u32[]{:S(2)}, u32[]{:S(2)}) collective-permute-start(f32[11,768]{1,0:T(8,128)S(1)} %fusion.36), channel_id=1, source_target_pairs={{0,4},{1,5},{2,6},{3,7},{4,0},{5,1},{6,2},{7,3},{8,12},{9,13},{10,... | collective-permute-start | bytes 101384 | tf_op jit(solution)/shard_map/ppermute | solution.py:541
  314.7 9.0 %collective-permute-start.44 = (f32[11,768]{1,0:T(8,128)S(1)}, f32[11,768]{1,0:T(8,128)S(1)}, u32[]{:S(2)}, u32[]{:S(2)}) collective-permute-start(f32[11,768]{1,0:T(8,128)S(1)} %fusion.36), channel_id=1, source_target_pairs={{0,16},{1,17},{2,18},{3,19},{4,20},{5,21},{6,22},{7,23},{8,24},{9,... | collective-permute-start | bytes 101384 | tf_op jit(solution)/shard_map/ppermute | solution.py:541
  316.1 7.7 %collective-permute-start.45 = (f32[11,768]{1,0:T(8,128)S(1)}, f32[11,768]{1,0:T(8,128)S(1)}, u32[]{:S(2)}, u32[]{:S(2)}) collective-permute-start(f32[11,768]{1,0:T(8,128)S(1)} %fusion.36), channel_id=1, source_target_pairs={{0,20},{1,21},{2,22},{3,23},{4,16},{5,17},{6,18},{7,19},{8,28},{9,... | collective-permute-start | bytes 101384 | tf_op jit(solution)/shard_map/ppermute | solution.py:541
  320.5 5.1 %collective-permute-start.46 = (bf16[96,640]{1,0:T(8,128)(2,1)S(1)}, bf16[96,640]{1,0:T(8,128)(2,1)S(1)}, u32[]{:S(2)}, u32[]{:S(2)}) collective-permute-start(bf16[96,640]{1,0:T(8,128)(2,1)S(1)} %add_convert_fusion.4), channel_id=1, source_target_pairs={{0,16},{1,17},{2,18},{3,19},{4,20},{5,21},{6,22},{7,23},{8,24},{9,... | collective-permute-start | bytes 368648 | tf_op jit(solution)/shard_map/ppermute | solution.py:541
  (49 other events, 682.1 us)
Sparse Core Ops, SparseCore 0:
  16.9 130.9 all-gather.2
  173.2 90.4 reduce-scatter.2
  302.1 28.6 reduce-scatter.4

commit v2 on v1

--- a/solution.py
+++ b/solution.py
@@ -546,6 +546,21 @@
     return routed(values, lambda d, s, m: (d, s, (m + step) % mps))
 
 
+def along_mp(values, pairs):
+    groups = range(lax.axis_size(DP) * lax.axis_size(SEQ))
+    size = lax.axis_size(MP)
+    return lax.ppermute(values, AXES, [(g * size + a, g * size + b) for g in groups for a, b in pairs])
+
+
+def from_others(values):
+    z = lax.axis_index(MP)
+    far = along_mp(values, [(0, 2), (1, 3), (2, 0), (3, 1)])
+    up = along_mp(values, [(0, 1), (1, 2), (2, 3)])
+    down = along_mp(values, [(1, 0), (2, 1), (3, 2)])
+    last = along_mp(far, [(2, 3), (1, 0)])
+    return [jnp.where(z == 0, last, up), far, jnp.where(z == 3, last, down)]
+
+
 def to_sibling(values):
     return routed(values, lambda d, s, m: (d ^ 1, s, m))
 
@@ -587,18 +602,13 @@
         jnp.concatenate([mine[i * half : (i + 1) * half], other[i * half : (i + 1) * half]])
         for i in range(len(arrays))
     ]
-    return found, mine[len(arrays) * half :], sent
-
-
-def send_from_work(values):
-    half = values.shape[0] // 2
-    return routed(values[:half], straight), routed(values[half:], crossed_back)
-
-
-def from_work(mine, other):
-    x = lax.axis_index(SEQ)
-    halves = [jnp.where(x == 0, mine, other), jnp.where(x == 0, other, mine)]
-    return jnp.concatenate(halves).astype(jnp.float32)[None, :, None]
+    return found, mine[len(arrays) * half :]
+
+
+def send_from_work(arrays):
+    half = arrays[0].shape[0] // 2
+    mine, other = (jnp.concatenate([a[at : at + half] for a in arrays]) for at in (0, half))
+    return routed(mine, straight), routed(other, crossed_back)
 
 
 def dot(a, b, dims):
@@ -640,7 +650,7 @@
 PAIR = 2 * HD
 
 
-def kernel_call(body, name, in_memory, outs, scratch, flops, args, scalars=(), waits=()):
+def kernel_call(body, name, in_memory, outs, scratch, flops, args, scalars=(), waits=(), out_places=()):
     count, given = len(args), body
     if waits:
         args = list(args) + list(waits)
@@ -660,7 +670,7 @@
             ANYWHERE if i in in_memory else (IN_SMEM if i in scalars else IN_VMEM)
             for i in range(len(args))
         ],
-        out_specs=[IN_VMEM] * len(outs),
+        out_specs=[ANYWHERE if i in out_places else IN_VMEM for i in range(len(outs))],
         scratch_shapes=scratch,
         cost_estimate=pl.CostEstimate(flops=flops, bytes_accessed=moved, transcendentals=0),
     )(*args)
@@ -711,36 +721,24 @@
     return merged(a, b, piece % 2)
 
 
-def load_shards(rank, own, parts, target, sems):
-    shards, half = target.shape[0], parts[1].shape[1]
-    copies = [pltpu.make_async_copy(own, target.at[0], sems.at[0])]
-    for bit, (away, near1, near2, pair1, pair2) in ((0, parts[:5]), (BIT_CORE, parts[5:])):
-        found = (
-            (0, 0, away.at[:, pl.ds(0, half)]),
-            (0, 1, away.at[:, pl.ds(half, half)]),
-            (BIT_X, 0, near1),
-            (BIT_Y, 1, near2),
-            (BIT_Y, 0, pair1.at[0]),
-            (BIT_X, 1, pair2.at[0]),
-            (BIT_X | BIT_Y, 0, pair1.at[1]),
-            (BIT_X | BIT_Y, 1, pair2.at[1]),
+def loads_of(own, gathered, at, target, sems, first):
+    rows, chunk = target.shape[1], own.shape[0] // gathered.shape[0]
+    copies = [pltpu.make_async_copy(own.at[pl.ds(at, rows)], target.at[0], sems.at[first])]
+    done = 0
+    while done < rows:
+        place = at + done
+        size = min(rows - done, chunk - place % chunk)
+        copies.append(
+            pltpu.make_async_copy(
+                gathered.at[place // chunk, :, pl.ds(place % chunk, size)],
+                target.at[pl.ds(1, target.shape[0] - 1), pl.ds(done, size)],
+                sems.at[first + len(copies)],
+            )
         )
-        for bits, which, part in found:
-            place = pl.multiple_of(((rank[0] ^ (bit | bits)) * 2 + which) * half, half)
-            copies.append(
-                pltpu.make_async_copy(
-                    part,
-                    target.at[pl.ds(1, shards - 1), pl.ds(place, half)],
-                    sems.at[len(copies)],
-                )
-            )
+        done += size
     for copy in copies:
         copy.start()
     return copies
-
-
-def matrix(shards, t, hs):
-    return shards[:, t * hs : (t + 1) * hs].reshape(-1, shards.shape[2])
 
 
 def finish(copies):
@@ -763,27 +761,41 @@
     return mm_nt(values.astype(jnp.bfloat16), ones)
 
 
-def pack_kernel(rank, q, k, v, wo, wr, bias, w1, w2, own_out, share_out, ffn_out, sems):
-    rows1 = w1.shape[1]
+def pack_kernel(
+    rank, q, k, v, wo, wr, b1, bq, bv, w1, w2, own_out, share_out, sems
+):
+    rows, rows1, rows2 = own_out.shape[0] // 8, w1.shape[1], w2.shape[1]
     copies = [
-        pltpu.make_async_copy(w1.at[rank[0]], ffn_out.at[pl.ds(0, rows1)], sems.at[0]),
+        pltpu.make_async_copy(w1.at[rank[0]], share_out.at[pl.ds(rows, rows1)], sems.at[0]),
         pltpu.make_async_copy(
-            w2.at[rank[0]], ffn_out.at[pl.ds(rows1, w2.shape[1])], sems.at[1]
+            w2.at[rank[0]], share_out.at[pl.ds(rows + rows1, rows2)], sems.at[1]
         ),
     ]
     for copy in copies:
         copy.start()
     hs = wo.shape[0]
-    for i, part in enumerate((q, k, v)):
+    for i, part in enumerate((q, k, v, wo, wr)):
         own_out[i * hs : (i + 1) * hs] = part[...]
-    own_out[3 * hs : 4 * hs] = wo[...]
-    own_out[4 * hs : 5 * hs] = wr[...]
-    rest = own_out.shape[0] - 5 * hs
-    own_out[5 * hs :] = jnp.zeros((rest, own_out.shape[1]), jnp.bfloat16)
-    rows = own_out.shape[0] // 8
+    at = 5 * hs
+    own_out[at:] = jnp.zeros((own_out.shape[0] - at, own_out.shape[1]), jnp.bfloat16)
+    place = rows + rows1 + rows2
+    share_out[place:] = jnp.zeros((16, own_out.shape[1]), jnp.bfloat16)
+    for i, vector in enumerate((b1, bq, bv)):
+        upper = vector[...].astype(jnp.bfloat16)
+        lower = (vector[...] - upper.astype(jnp.float32)).astype(jnp.bfloat16)
+        share_out[place + 2 * i : place + 2 * i + 1, : vector.shape[1]] = upper
+        share_out[place + 2 * i + 1 : place + 2 * i + 2, : vector.shape[1]] = lower
     share_out[:rows] = own_out[pl.ds(pl.multiple_of(rank[0] * rows, rows), rows)]
-    share_out[rows:] = bias[...]
     finish(copies)
+
+
+def home_kernel(x, mine, other, *outs):
+    half = mine.shape[0] // len(outs)
+    for i, target in enumerate(outs):
+        here = slice(i * half, (i + 1) * half)
+        a, b = mine[here].astype(jnp.float32), other[here].astype(jnp.float32)
+        target[0, :half, 0] = jnp.where(x[0] == 0, a, b)
+        target[0, half:, 0] = jnp.where(x[0] == 0, b, a)
 
 
 def row_project_kernel(blocks, half, heads, *refs):
@@ -808,13 +820,15 @@
             pltpu.roll(kv_sibling[heads + h].astype(jnp.float32), HD, 1).astype(jnp.bfloat16),
         ]
         keys, values = jnp.concatenate(keys, axis=0), jnp.concatenate(values, axis=0)
-        for k in range(blocks):
-            rows = slice(k * half, (k + 1) * half)
+        for i in range(0, blocks, 2):
+            rows = slice(i * half, (i + 2) * half)
             scores = jnp.where(mask[...] > 0, mm_nt(q[h, rows], keys) * scale, -1e30)
             powers = jnp.exp(scores - jnp.max(scores, axis=-1, keepdims=True))
-            weights = (powers / jnp.sum(powers, axis=-1, keepdims=True)).astype(jnp.bfloat16)
+            over = 1.0 / jnp.sum(powers, axis=-1, keepdims=True)
+            weights = (powers * over).astype(jnp.bfloat16)
             p_out[h, rows] = weights
-            o_out[k][h] = mm(weights, values).astype(jnp.bfloat16)
+            o = mm(weights, values).astype(jnp.bfloat16)
+            o_out[i][h], o_out[i + 1][h] = o[:half], o[half:]
         return carry
 
     lax.fori_loop(0, heads, one_head, 0)
@@ -856,10 +870,10 @@
     keep_out, theirs_out, bias_out = refs[blocks + 9 : blocks + 12]
     send_out, (sums, g, whole) = refs[blocks + 12 : 2 * blocks + 12], refs[2 * blocks + 12 :]
     sums[...] = jnp.zeros_like(sums)
+    over_gain = 1.0 / gain[...]
     sums[2:3] = col_sums[3:4]
     sums[3:6] = col_sums[0:3]
     sums[6:9] = ffn_sums[0:3]
-    sums[9:11] = col_sums[4:6]
     for k in range(blocks):
         rows = slice(k * half, (k + 1) * half)
         pieces = [gq[h, rows].astype(jnp.float32) for h in range(heads)] + [
@@ -872,10 +886,14 @@
         g[2 * k * half : 2 * (k + 1) * half] = y
         grad = mm(y, w[...])
         send_out[k][: 2 * half] = grad.astype(jnp.bfloat16)
-        unit = (hidden[k][...].astype(jnp.float32) - bias[...]) / gain[...]
+        unit = (hidden[k][...].astype(jnp.float32) - bias[...]) * over_gain
         sums[0:1] += row_sum(grad * unit)
         sums[1:2] += row_sum(grad)
+    hs = heads * HD
     for k in range(blocks):
+        here = slice(k * hs, (k + 1) * hs)
+        sums[9:10, :hs] = col_sums[4:5, here]
+        sums[10:11, :hs] = col_sums[5:6, here]
         sums[11:12] = b1_sums[k : k + 1]
         send_out[k][2 * half :] = sums[...].astype(jnp.bfloat16)
     bias_out[...] = row_sum(g[...].astype(jnp.float32))
@@ -897,32 +915,38 @@
 
 
 def column_kernel(
-    blocks, heads, rank, stream, own, row_bo, gain, bias, bq, bv, col_bo, ffn_gain, ffn_bias,
+    blocks, heads, stream, own, gathered, row_bo, gain, bias, bq, bv, col_bo, ffn_gain, ffn_bias,
     *refs
 ):
-    o, parts, refs = refs[:blocks], refs[blocks : blocks + 10], refs[blocks + 10 :]
+    o, refs = refs[:blocks], refs[blocks:]
     row_heads_out, row_out, normed_out, q_out, k_out, v_out, heads_out, col_out, ffn_out = refs[:9]
-    shards, sems = refs[9:]
-    hs = heads * HD
+    wq, wk, wv, wo, wr, sems = refs[9:]
+    hs, width = wq.shape[1], stream.shape[1]
     half = stream.shape[0] // 2
-    copies = load_shards(rank, own, parts, shards, sems)
+    loads, used = [], 0
+    for t, target in ((4, wr), (0, wq), (1, wk), (2, wv), (3, wo)):
+        loads.append(loads_of(own, gathered, t * hs, target, sems, used))
+        used += len(loads[-1])
     pieces = [o[-k % blocks][h] for k in range(blocks) for h in range(heads)]
     row_heads = jnp.concatenate([joined(pieces, 0), joined(pieces, 1)], axis=0).astype(
         jnp.bfloat16
     )
     row_heads_out[...] = row_heads
-    finish(copies)
-    after_row = stream[...] + mm(row_heads, matrix(shards, 4, hs)) + row_bo[...]
+    finish(loads[0])
+    after_row = stream[...] + mm(row_heads, wr[...].reshape(-1, width)) + row_bo[...]
     row_out[...] = after_row
     _, _, normed = norm_in_kernel(after_row, gain[...], bias[...])
     normed_out[...] = normed
-    q = (mm_nt(normed, matrix(shards, 0, hs)) + bq[...]).astype(jnp.bfloat16)
+    finish(loads[1])
+    q = (mm_nt(normed, wq[...].reshape(-1, width)) + bq[...]).astype(jnp.bfloat16)
     q_out[...] = q
-    k = mm_nt(normed, matrix(shards, 1, hs)).astype(jnp.bfloat16)
+    finish(loads[2])
+    k = mm_nt(normed, wk[...].reshape(-1, width)).astype(jnp.bfloat16)
     k_out[...] = k
-    v = (mm_nt(normed, matrix(shards, 2, hs)) + bv[...]).astype(jnp.bfloat16)
+    finish(loads[3])
+    v = (mm_nt(normed, wv[...].reshape(-1, width)) + bv[...]).astype(jnp.bfloat16)
     v_out[...] = v
-    ones = head_map(stream.shape[1])
+    ones = head_map(width)
     k32, v32 = k.astype(jnp.float32), v.astype(jnp.float32)
     k_gap = k32[:half] - k32[half:]
     for r in range(2):
@@ -931,26 +955,30 @@
         first = over_features(1.0 / (1.0 + jnp.exp(-gap)), ones)
         second = over_features(1.0 / (1.0 + jnp.exp(gap)), ones)
         heads_out[rows] = (first * v32[:half] + second * v32[half:]).astype(jnp.bfloat16)
-    after_col = after_row + mm(heads_out[...], matrix(shards, 3, hs)) + col_bo[...]
+    finish(loads[4])
+    after_col = after_row + mm(heads_out[...], wo[...].reshape(-1, width)) + col_bo[...]
     col_out[...] = after_col
     _, _, ffn_normed = norm_in_kernel(after_col, ffn_gain[...], ffn_bias[...])
     ffn_out[...] = ffn_normed
 
 
 def ffn_kernel(
-    rank, normed, stream, grad_low, gathered, b1, b2, gain,
+    rank, normed, stream, grad_low, own1, own2, gathered, b1, b2, gain,
     out, grad_out, low_out, weights_out, sums_out, b1_out,
-    w1, w2, normed_t, low_t, total_out, total_back, sems,
+    w1, w2, products, normed_t, low_t, total_out, total_back, sems, out_sems,
 ):
     blocks, peers, rows1, size = w1.shape
     width = normed.shape[1]
+    first = gathered.shape[2] - rows1 - w2.shape[2]
     copies = []
     for k in range(blocks):
-        shard = (rank[1] + blocks - k) % blocks
-        pair = (
-            (gathered.at[:, shard, pl.ds(0, rows1)], w1.at[k]),
-            (gathered.at[:, shard, pl.ds(rows1, w2.shape[2])], w2.at[k]),
-        )
+        if k == 0:
+            pair = [(own1, w1.at[0]), (own2, w2.at[0])]
+        else:
+            pair = [
+                (gathered.at[:, k - 1, pl.ds(first, rows1)], w1.at[k]),
+                (gathered.at[:, k - 1, pl.ds(first + rows1, w2.shape[2])], w2.at[k]),
+            ]
         for i, (source, target) in enumerate(pair):
             copies.append(pltpu.make_async_copy(source, target, sems.at[2 * k + i]))
             copies[-1].start()
@@ -958,10 +986,19 @@
     low_t[...] = turned(grad_low[...])
     total_out[...] = jnp.zeros_like(total_out)
     total_back[...] = jnp.zeros_like(total_back)
-    finish(copies)
+    finish(copies[:2])
+
+    def leaving(k):
+        shard = (rank[1] + blocks - k) % blocks
+        return pltpu.make_async_copy(products.at[k], weights_out.at[:, shard], out_sems.at[k])
 
     def one_shard(k, carry):
-        shard = (rank[1] + blocks - k) % blocks
+        @pl.when(k > 0)
+        def _():
+            for i, (at, target) in enumerate(((first, w1), (first + rows1, w2))):
+                part = gathered.at[:, k - 1, pl.ds(at, target.shape[2])]
+                pltpu.make_async_copy(part, target.at[k], sems.at[2 * k + i]).wait()
+
         weight1 = w1[k].reshape(width, size)
         weight2 = w2[k].reshape(size, width)
         up = mm(normed[...], weight1) + b1[pl.ds(k, 1)]
@@ -974,7 +1011,8 @@
         b1_out[pl.ds(k, 1)] = row_sum(grad_up.astype(jnp.float32))
         for i, (left, right) in enumerate(((normed_t, grad_up), (low_t, activated))):
             product = mm(left[...], right).astype(jnp.bfloat16).reshape(peers, rows1, size)
-            weights_out[:, shard, :, i * size : (i + 1) * size] = product
+            products[k, :, :, i * size : (i + 1) * size] = product
+        leaving(k).start()
         return carry
 
     lax.fori_loop(0, blocks, one_shard, 0)
@@ -988,20 +1026,24 @@
     grad = grad_low[...].astype(jnp.float32) + norm_pull(unit, scale, gain[...], grad_normed)
     grad_out[...] = grad
     low_out[...] = grad.astype(jnp.bfloat16)
+    for k in range(blocks):
+        leaving(k).wait()
 
 
 def column_back_kernel(
-    blocks, heads, rank, grad, grad_low, q, k, v, row_stream, own, gain, *refs
+    blocks, heads, grad, grad_low, q, k, v, row_stream, own, gathered, gain,
+    gq_out, gk_out, gv_out, grad_out, low_out, sums_out, *refs
 ):
-    parts, refs = refs[:10], refs[10:]
-    gq_out, gk_out, gv_out, grad_out, low_out, sums_out = refs[:6]
-    d_out, (shards, sems) = refs[6 : 6 + blocks], refs[6 + blocks :]
-    hs, width = heads * HD, grad.shape[1]
+    d_out, (wq, wk, wv, wo, wr, sems) = refs[:blocks], refs[blocks:]
+    hs, width = wq.shape[1], grad.shape[1]
     half = grad.shape[0] // 2
-    copies = load_shards(rank, own, parts, shards, sems)
+    loads, used = [], 0
+    for t, target in ((3, wo), (0, wq), (1, wk), (2, wv), (4, wr)):
+        loads.append(loads_of(own, gathered, t * hs, target, sems, used))
+        used += len(loads[-1])
     ones = head_map(width)
-    finish(copies)
-    grad_heads = mm_nt(grad_low[...], matrix(shards, 3, hs)).astype(jnp.bfloat16)
+    finish(loads[0])
+    grad_heads = mm_nt(grad_low[...], wo[...].reshape(-1, width)).astype(jnp.bfloat16)
     g32 = grad_heads.astype(jnp.float32)
     k32, v32, q32 = (a[...].astype(jnp.float32) for a in (k, v, q))
     k_gap, v_gap = k32[:half] - k32[half:], v32[:half] - v32[half:]
@@ -1021,10 +1063,12 @@
     gk_out[half:] = (-grad_k).astype(jnp.bfloat16)
     gv_out[:half] = grad_v[0].astype(jnp.bfloat16)
     gv_out[half:] = grad_v[1].astype(jnp.bfloat16)
+    for load in loads[1:4]:
+        finish(load)
     grad_normed = (
-        mm(gq_out[...], matrix(shards, 0, hs))
-        + mm(gk_out[...], matrix(shards, 1, hs))
-        + mm(gv_out[...], matrix(shards, 2, hs))
+        mm(gq_out[...], wq[...].reshape(-1, width))
+        + mm(gk_out[...], wk[...].reshape(-1, width))
+        + mm(gv_out[...], wv[...].reshape(-1, width))
     )
     unit, scale = norm_parts(row_stream[...])
     total = grad[...] + norm_pull(unit, scale, gain[...], grad_normed)
@@ -1038,7 +1082,8 @@
     sums_out[3:4] = row_sum(low.astype(jnp.float32))
     sums_out[4:5] = row_sum(gq_out[...].astype(jnp.float32))
     sums_out[5:6] = row_sum(gv_out[...].astype(jnp.float32))
-    grad_o = mm_nt(low, matrix(shards, 4, hs)).astype(jnp.bfloat16).astype(jnp.float32)
+    finish(loads[4])
+    grad_o = mm_nt(low, wr[...].reshape(-1, width)).astype(jnp.bfloat16).astype(jnp.float32)
     for b in range(blocks):
         for h in range(heads):
             piece = parted(grad_o[:half], grad_o[half:], b * heads + h)
@@ -1046,10 +1091,12 @@
 
 
 def weights_kernel(
-    rank, normed, col_low, row_low, gq, gk, gv, col_heads, row_heads, keep_out, send_out, left
+    rank, normed, col_low, row_low, gq, gk, gv, col_heads, row_heads, *refs
 ):
+    keep_outs, send_outs, (left, found, sems) = refs[:2], refs[2:4], refs[4:]
     width = normed.shape[1]
     rows, kept, part = width // 8, width // 2, width // 2
+    copies = []
     for i, source in enumerate((normed, col_low, row_low)):
         left[3 * i] = turned(source[...])
         for order, bits in enumerate((X_FIRST, Y_FIRST)):
@@ -1057,13 +1104,26 @@
                 peer = rank[0] ^ (bits[j % 4] | (BIT_CORE if j >= 4 else 0))
                 block = left[3 * i, pl.ds(pl.multiple_of(peer * rows, rows), rows)]
                 left[3 * i + 1 + order, j * rows : (j + 1) * rows] = block
-    for t, right in enumerate((gq, gk, gv, col_heads, row_heads)):
-        for order in range(2):
-            product = mm(
+    hs = part // 2
+    spare = jnp.zeros((width, found.shape[3] - 5 * hs), jnp.float32)
+    for order in range(2):
+        products = [
+            mm(
                 left[3 * max(t - 2, 0) + 1 + order], right[:, order * part : (order + 1) * part]
+            )
+            for t, right in enumerate((gq, gk, gv, col_heads, row_heads))
+        ]
+        for k in range(2):
+            product = jnp.concatenate(
+                [p[:, k * hs : (k + 1) * hs] for p in products] + [spare], axis=1
             ).astype(jnp.bfloat16)
-            keep_out[order, :, t * part : (t + 1) * part] = product[:kept]
-            send_out[order, :, t * part : (t + 1) * part] = product[kept:]
+            found[order, k] = product
+            for i, target in enumerate((send_outs[order], keep_outs[order])):
+                half = found.at[order, k, pl.ds((1 - i) * kept, kept)]
+                sem = sems.at[len(copies)]
+                copies.append(pltpu.make_async_copy(half, target.at[k], sem))
+                copies[-1].start()
+    finish(copies)
 
 
 def on_device_columns(
@@ -1111,7 +1171,7 @@
     columns = col_mask.shape[1]
     mask_rows = -(-columns // (8 * width)) * 8
     padded = jnp.pad(col_mask[0].astype(b16), (0, mask_rows * width - columns))
-    (start, grad_start), mask, sent = to_work(
+    (start, grad_start), mask = to_work(
         (acts[0, :, 0], cotangent[0, :, 0]), padded.reshape(mask_rows, width)
     )
     mask = mask.reshape(-1)[:columns]
@@ -1121,48 +1181,35 @@
     row_unit, row_scale = norm_parts(stream)
     normed = low(row_unit * ln_row_gain + ln_row_bias)
 
-    def two_parts(v):
-        upper = low(v)
-        return upper, low(v - upper.astype(f32))
-
-    b1_parts, bq_parts, bv_parts = two_parts(ffn_b1), two_parts(col_bq), two_parts(col_bv)
-    bias_rows = jnp.concatenate(
-        b1_parts + (jnp.concatenate(bq_parts + bv_parts, axis=1), jnp.zeros((13, width), b16))
-    )
-    chunk = -(-5 * hs // (32 * ranks)) * 32
+    chunk = -(-5 * hs // (16 * ranks)) * 16
     fc, dc = fs // ranks, width // ranks
     own_w1, own_w2 = ffn_w1[0].reshape(ranks, dc, fs), ffn_w2[0].reshape(ranks, fc, width)
-    own_attention, pack_attention, pack_ffn = kernel_call(
+    own_attention, pack = kernel_call(
         pack_kernel,
         "pack",
-        (7, 8),
-        [((chunk * ranks, width), b16), ((chunk + 16, width), b16), ((dc + fc, width), b16)],
+        (9, 10),
+        [((chunk * ranks, width), b16), ((chunk + dc + fc + 16, width), b16)],
         [bf_dma((2,))],
         0,
-        [rank_ref, col_wq[0].T, col_wk[0].T, col_wv[0].T, col_wo[0], row_wo[0], bias_rows]
-        + [own_w1, own_w2],
+        [rank_ref, col_wq[0].T, col_wk[0].T, col_wv[0].T, col_wo[0], row_wo[0], ffn_b1]
+        + [col_bq, col_bv, own_w1, own_w2],
         (0,),
-        sent,
-    )
-
-
-    whole_ffn = lax.all_gather(pack_ffn, AXES, axis=0, tiled=False)
-    whole_ffn = whole_ffn.reshape(ranks, mps, dc + fc, width)
-    pack_attention, normed = together(pack_attention, normed)
-    away = [shifted(pack_attention, k) for k in range(1, mps)]
-    normed, *away = together(normed, *away)
-    away = jnp.stack(away)
-    hidden = [shifted(normed, k) for k in range(1, mps)]
-    got = together(*hidden, to_x(away[:, : chunk // 2]), to_y(away[:, chunk // 2 : chunk]))
-    hidden, near1, near2 = [normed, *got[: mps - 1]], got[mps - 1], got[mps]
-    pair1 = to_y(jnp.stack([away[:, : chunk // 2], near1]))
-    pair2 = to_x(jnp.stack([away[:, chunk // 2 : chunk], near2]))
-    bias_away = away[:, chunk : chunk + 3].astype(f32)
-    b1 = jnp.concatenate([ffn_b1, bias_away[:, 0] + bias_away[:, 1]])
-    bias_qv = bias_away[:, 2].reshape(mps - 1, 2, 2, hs).sum(axis=2)
-    bq = jnp.concatenate([col_bq, bias_qv[:, 0].reshape(1, -1)], axis=1)
-    bv = jnp.concatenate([col_bv, bias_qv[:, 1].reshape(1, -1)], axis=1)
-
+    )
+
+
+    pack, normed = together(pack, normed)
+    away = from_others(pack)
+    place = chunk + dc + fc
+    whole = lax.all_gather(
+        jnp.stack([part[:place] for part in away]), (DP, SEQ), axis=0, tiled=False
+    )
+    bias_away = jnp.stack([part[place : place + 6] for part in away]).astype(f32)
+    bias_away = bias_away.reshape(mps - 1, 3, 2, width).sum(axis=2)
+    b1 = jnp.concatenate([ffn_b1, bias_away[:, 0]])
+    bq = jnp.concatenate([col_bq, bias_away[:, 1, :hs].reshape(1, -1)], axis=1)
+    bv = jnp.concatenate([col_bv, bias_away[:, 2, :hs].reshape(1, -1)], axis=1)
+
+    hidden = [normed] + from_others(normed)
     odd = 3 * heads % 2 * HD
     row_w = jnp.concatenate(
         [row_wq[0].T, row_wk[0].T, row_wv[0].T, jnp.zeros((odd, width), b16)]
@@ -1172,6 +1219,13 @@
         [row_bq, jnp.zeros_like(row_bq), row_bv, jnp.zeros((1, odd), f32)], axis=1
     )
     here = mps * half
+    score_scale = 1.0 / math.sqrt(HD * 2)
+    near = (z - jnp.arange(mps)) % mps
+    pick = (near[:, None] == jnp.arange(mps)).astype(f32)
+    mask_blocks = jnp.einsum(
+        "kz,zsi->ski", pick, mask.reshape(mps, 2, half).astype(f32), precision="highest"
+    )
+    mask_near = jnp.where(c == 0, mask_blocks, mask_blocks[::-1]).reshape(1, -1)
     q_h, kv_h = kernel_call(
         functools.partial(row_project_kernel, mps, half, heads),
         "row_project",
@@ -1180,15 +1234,9 @@
         [],
         2 * mps * tokens * width * row_width,
         hidden + [row_w, row_b],
+        waits=[mask_near, grad_start, stream, b1, bq, bv],
     )
     kv_sibling = to_sibling(kv_h)
-    score_scale = 1.0 / math.sqrt(HD * 2)
-    near = (z - jnp.arange(mps)) % mps
-    pick = (near[:, None] == jnp.arange(mps)).astype(f32)
-    mask_blocks = jnp.einsum(
-        "kz,zsi->ski", pick, mask.reshape(mps, 2, half).astype(f32), precision="highest"
-    )
-    mask_near = jnp.where(c == 0, mask_blocks, mask_blocks[::-1]).reshape(1, -1)
     p_h, *o_blocks = kernel_call(
         functools.partial(row_attend_kernel, heads, half, score_scale),
         "row_attend",
@@ -1199,35 +1247,30 @@
         [q_h, kv_h, kv_sibling, mask_near],
     )
     o_from = [o_blocks[0]] + [shifted(o_blocks[k], -k) for k in range(1, mps)]
-    *o_from, pair1, pair2 = together(*o_from, pair1, pair2)
-    parts = [away, near1, near2, pair1, pair2]
-    parts += [to_sibling(part) for part in parts]
-
-    weight_scratch = [pltpu.VMEM((mps, chunk * ranks, width), b16), bf_dma((17,))]
+
+    weight_scratch = [pltpu.VMEM((mps, hs, width), b16)] * 5 + [bf_dma((20,))]
     square = tokens * width * width * 2
     row_heads, row_stream, col_normed, col_q, col_k, col_v, col_heads, col_stream, ffn_normed = (
         kernel_call(
             functools.partial(column_kernel, mps, heads),
             "column",
-            (2,) + tuple(range(11 + mps, 21 + mps)),
+            (1, 2),
             [
                 ((tokens, width), kind)
                 for kind in (b16, f32, b16, b16, b16, b16, b16, f32, b16)
             ],
             weight_scratch,
             5 * square,
-            [rank_ref, stream, own_attention, row_bo, ln_col_gain, ln_col_bias, bq, bv]
+            [stream, own_attention, whole, row_bo, ln_col_gain, ln_col_bias, bq, bv]
             + [col_bo, ln_ffn_gain, ln_ffn_bias]
-            + o_from
-            + parts,
-            (0,),
+            + o_from,
         )
     )
 
     out_low, ffn_grad, col_low, grad_ffn, ffn_sums, grad_b1 = kernel_call(
         ffn_kernel,
         "ffn",
-        (4,),
+        (4, 5, 6),
         [
             ((tokens, width), b16),
             ((tokens, width), f32),
@@ -1239,22 +1282,25 @@
         [
             pltpu.VMEM((mps, ranks, dc, fs), b16),
             pltpu.VMEM((mps, ranks, fc, width), b16),
+            pltpu.VMEM((mps, ranks, dc, 2 * fs), b16),
             pltpu.VMEM((width, tokens), b16),
             pltpu.VMEM((width, tokens), b16),
             pltpu.VMEM((tokens, width), f32),
             pltpu.VMEM((tokens, width), f32),
             bf_dma((2 * mps,)),
+            bf_dma((mps,)),
         ],
         12 * tokens * width * fs * mps,
-        [rank_ref, ffn_normed, col_stream, grad_start, whole_ffn, b1, ffn_b2, ln_ffn_gain],
+        [rank_ref, ffn_normed, col_stream, grad_start, own_w1, own_w2, whole, b1, ffn_b2]
+        + [ln_ffn_gain],
         (0,),
-    )
-    out_halves = send_from_work(out_low)
+        out_places=(3,),
+    )
 
     grad_q, grad_k, grad_v, row_grad, row_low, col_sums, *d_blocks = kernel_call(
         functools.partial(column_back_kernel, mps, heads),
         "column_back",
-        (7,) + tuple(range(9, 19)),
+        (6, 7),
         [
             ((tokens, width), b16),
             ((tokens, width), b16),
@@ -1266,9 +1312,8 @@
         + [((heads, half, PAIR), b16)] * mps,
         weight_scratch,
         5 * square,
-        [rank_ref, ffn_grad, col_low, col_q, col_k, col_v, row_stream, own_attention, ln_col_gain]
-        + parts,
-        (0,),
+        [ffn_grad, col_low, col_q, col_k, col_v, row_stream, own_attention, whole]
+        + [ln_col_gain],
     )
     d_from = [d_blocks[0]] + [shifted(d_blocks[k], -k) for k in range(1, mps)]
     def both(a, b, here):
@@ -1286,19 +1331,24 @@
         [],
         16 * heads * here * here * PAIR,
         [q_h, kv_h, kv_sibling, p_h] + [d_from[-k % mps] for k in range(mps)],
-        waits=out_halves,
     )
     gkv_sibling = to_sibling(gkv_theirs)
-    att_keep, att_send = kernel_call(
+    lanes = -(-5 * hs // 128) * 128
+    *att_keep, att_send0, att_send1 = kernel_call(
         weights_kernel,
         "weights",
         (),
-        [((2, width // 2, 5 * width // 2), b16)] * 2,
-        [pltpu.VMEM((9, width, tokens), b16)],
+        [((2, width // 2, lanes), b16)] * 4,
+        [
+            pltpu.VMEM((9, width, tokens), b16),
+            pltpu.VMEM((2, 2, width, lanes), b16),
+            bf_dma((8,)),
+        ],
         5 * square,
         [rank_ref, col_normed, col_low, row_low, grad_q, grad_k, grad_v, col_heads, row_heads],
         (0,),
         [gkv_sibling],
+        (0, 1, 2, 3),
     )
     row_keep, row_theirs, row_bias, *g_send = kernel_call(
         functools.partial(row_project_back_kernel, mps, half, heads),
@@ -1319,95 +1369,89 @@
         [rank_ref] + hidden + [row_w, ln_row_gain, ln_row_bias, gq_h, gkv_h, gkv_sibling]
         + [col_sums, ffn_sums, grad_b1],
         (0,),
-        [att_keep],
+        att_keep,
     )
     part = width // 4
     upper, lower = slice(0, part // 2), slice(part // 2, part)
-    att_theirs = to_sibling(att_send)
+    *att_theirs, row_keep = together(to_sibling(att_send0), to_sibling(att_send1), row_keep)
     hops = ((to_x, to_y), (to_y, to_x))
 
     def chip_sum(i, here):
-        return both(att_keep[i], att_theirs[i], here)
-
-    far = mps // 2
-    near = [k for k in range(1, mps) if k != far]
-    g_parts = {0: g_send[0], far: shifted(g_send[far], -far)}
+        return att_keep[i][:, here].astype(f32) + att_theirs[i][:, here].astype(f32)
+
     got = together(
-        *(shifted(g_send[k], -k) for k in near),
+        *(shifted(g_send[k], -k) for k in range(1, mps)),
         *(hops[i][0](low(chip_sum(i, slice(part, None)))) for i in range(2)),
         to_sibling(row_theirs),
-    )
-    g_parts |= dict(zip(near, got))
-    arrived, row_peer = got[len(near) : -1], got[-1]
-    g_parts[far], *second = together(
-        g_parts[far],
+        lax.psum_scatter(grad_ffn, (DP, SEQ), scatter_dimension=0, tiled=True)[0],
+    )
+    first, row_peer, ffn_mine = got[mps - 1 : -2], got[-2], got[-1]
+    ffn_total = lax.psum_scatter(ffn_mine, MP, scatter_dimension=0, tiled=True)[0].astype(f32)
+    g_sum = sum(g.astype(f32) for g in (g_send[0], *got[: mps - 1]))
+    gradient = row_grad + norm_pull(row_unit, row_scale, ln_row_gain, g_sum[:tokens])
+
+    summed = jnp.concatenate(
+        [g_sum[tokens : tokens + 12], jnp.pad(row_bias, ((0, 0), (0, width - row_width)))]
+    )
+
+    *second, their_sum, gradient = together(
         *(
-            hops[i][1](low(chip_sum(i, lower) + arrived[i][lower].astype(f32)))
+            hops[i][1](low(chip_sum(i, lower) + first[i][:, lower].astype(f32)))
             for i in range(2)
         ),
-    )
-    g_parts = [g_parts[k] for k in range(mps)]
-    grad_normed = sum(g[:tokens].astype(f32) for g in g_parts)
-    gradient = row_grad + norm_pull(row_unit, row_scale, ln_row_gain, grad_normed)
-
-    tails = [g[tokens:].astype(f32) for g in g_parts]
-    near_sum = sum(t[:9] for t in tails)
-    shard = [
-        sum(t[row, k * hs : (k + 1) * hs] for k, t in enumerate(tails))[None] for row in (9, 10)
-    ]
-    shard += [row_bias[:, :hs], row_bias[:, 2 * hs : 3 * hs]]
-    summed = jnp.concatenate(
-        [near_sum, jnp.concatenate(shard, axis=1), sum(t[11:12] for t in tails)]
-    )
-
+        to_sibling(summed),
+        gradient,
+    )
+    summed = summed + their_sum
     finals = [
-        (
-            chip_sum(i, upper) + arrived[i][upper].astype(f32) + second[i].astype(f32)
-        ).reshape(part // 2, 5, -1, hs)
+        chip_sum(i, upper) + first[i][:, upper].astype(f32) + second[i].astype(f32)
         for i in range(2)
     ]
-
-    def shard_of(k):
-        return finals[k // (mps // 2)][:, :, k % (mps // 2)]
-
-    ffn_mine = lax.psum_scatter(grad_ffn, (DP, SEQ), scatter_dimension=0, tiled=True)[0]
-    ffn_mine, gradient = together(ffn_mine, gradient)
-    ffn_total = lax.psum_scatter(ffn_mine, MP, scatter_dimension=0, tiled=True)[0].astype(f32)
-    got = together(
-        *send_from_work(low(gradient)),
-        *(shifted(low(shard_of(k)), -k) for k in range(1, mps)),
-        to_x(low(both(row_keep, row_peer, slice(part, None)))),
-        to_sibling(summed),
-    )
-    grad_acts = from_work(*got[:2])
-    row_arrived, summed = got[-2], summed + got[-1]
-    attention_total = shard_of(0) + sum(g.astype(f32) for g in got[2:-2])
-
-    row_total = (
-        both(row_keep, row_peer, upper)
-        + row_arrived[upper].astype(f32)
-        + to_y(low(both(row_keep, row_peer, lower) + row_arrived[lower].astype(f32))).astype(f32)
-    )
-    diagonal = routed(summed, lambda d, s, m: (d ^ 2, s ^ 1, m))
-    summed = summed + to_x(summed) + (to_y(summed) + diagonal)
+    shards = [finals[k // 2][k % 2] for k in range(mps)]
+
+    def to_xy(values):
+        return routed(values, lambda d, s, m: (d ^ 2, s ^ 1, m))
+
+    quarter = part // 2
+    row_sums = [both(row_keep, row_peer, slice(i * quarter, (i + 1) * quarter)) for i in range(4)]
+    row_go = [low(v) for v in row_sums[1:]]
+    *shards, row_go[0] = together(*shards, row_go[0])
+    attention_total = shards[0]
+    for k in range(1, mps):
+        attention_total += shifted(low(shards[k]), -k).astype(f32)
+    attention_total = attention_total[:, : 5 * hs].reshape(part // 2, 5, hs)
+    out, grad_acts = kernel_call(
+        home_kernel,
+        "home",
+        (),
+        [((1, tokens, 1, width), f32)] * 2,
+        [],
+        0,
+        [lax.axis_index(SEQ).reshape(1).astype(jnp.int32)]
+        + list(send_from_work([out_low, low(gradient)])),
+        (0,),
+    )
+    row_total = row_sums[0]
+    for hop, values in zip((to_y, to_x, to_xy), row_go):
+        row_total += hop(values).astype(f32)
+    summed = summed + to_x(summed) + (to_y(summed) + to_xy(summed))
     device = rank * mps + z
     vectors = summed[:9].reshape(9, ranks * mps, -1)
     vectors = lax.dynamic_index_in_dim(vectors, device, axis=1, keepdims=False)
-    biases = summed[9:10]
 
     def transposed(v):
         return v.T[None]
 
     return (
-        from_work(*out_halves),
+        out,
         grad_acts,
         vectors[0][None],
         vectors[1][None],
         row_total[:, :hs][None],
         row_total[:, hs : 2 * hs][None],
         row_total[:, 2 * hs : 3 * hs][None],
-        biases[:, 2 * hs : 3 * hs],
-        biases[:, 3 * hs : 4 * hs],
+        summed[12:13, :hs],
+        summed[12:13, 2 * hs : 3 * hs],
         transposed(attention_total[:, 4]),
         vectors[2][None],
         vectors[3][None],
@@ -1415,14 +1459,14 @@
         attention_total[:, 0][None],
         attention_total[:, 1][None],
         attention_total[:, 2][None],
-        biases[:, :hs],
-        biases[:, hs : 2 * hs],
+        summed[9:10, :hs],
+        summed[10:11, :hs],
         transposed(attention_total[:, 3]),
         vectors[5][None],
         vectors[6][None],
         vectors[7][None],
         ffn_total[:, :fs][None],
-        summed[10:11],
+        summed[11:12],
         transposed(ffn_total[:, fs:]),
         vectors[8][None],
     )

time: 340 us -> 314 us (0.924)
  waiting for transfers between devices: 125 us -> 107 us
  local copies, waits for them, and re-layouts: 23.1 us -> 15.7 us
  Pallas kernels: 75.6 us -> 70.1 us
    ppermute x47 -> x32, waiting for transfers between devices: 122 us -> 50.4 us  [routed(): return lax.ppermute(values, AXES, pairs)]
    ppermute x0 -> x8, waiting for transfers between devices: none -> 53.4 us  [along_mp(): lax.ppermute(values, AXES, [(g * size + a, g * size + b) for g in groups...]
    ppermute x0 -> x8, starting transfers between devices: none -> 19.2 us  [along_mp(): lax.ppermute(values, AXES, [(g * size + a, g * size + b) for g in groups...]
    ppermute x47 -> x32, starting transfers between devices: 70 us -> 53.2 us  [routed(): return lax.ppermute(values, AXES, pairs)]
    pallas_call x9 -> x10, Pallas kernels: 75.6 us -> 70.1 us  [kernel_call(): pl.pallas_call(body, name=name, out_shape=[jax.ShapeDtypeStruct(shape, ki...]
    add x9 -> x8, other arithmetic: 2.64 us -> 8.15 us  [the longest x2 3.02 us: on_device_columns(): chip_sum(i, upper) + first[i][:, upper].astype(f32) + second[i].astype(f32)]
    unnamed x100 -> x72, local copies, waits for them, and re-layouts: 10.7 us -> 6.64 us
    convert_element_type x7 -> x6, other arithmetic: 9.43 us -> 10.1 us  [low(): return values.astype(jnp.bfloat16)]
  transfers between devices with their start and end apart: 50 -> 43, of which waited for: 20 -> 21; matrix products, arithmetic and copies ran while one was open for 12% -> 10% of each run, Pallas kernels for 16% -> 15%
where the time goes in v2:
time: 314 us; the launch traced here: 311 us
  waiting for transfers between devices  107 us (34%)
  starting transfers between devices  72.5 us (23%)
  Pallas kernels  70.1 us (22%)
  other arithmetic  31.2 us (10%)
  local copies, waits for them, and re-layouts  15.7 us (5%)
  between operations  14.5 us (5%)
    pallas_call x10, Pallas kernels, kernel_call(): pl.pallas_call(body, name=name, out_shape=[jax.ShapeDtypeStruct(shape, ki...  70.1 us
    ppermute x8, waiting for transfers between devices, along_mp(): lax.ppermute(values, AXES, [(g * size + a, g * size + b) for g in groups...  53.4 us
    ppermute x32, starting transfers between devices, routed(): return lax.ppermute(values, AXES, pairs)  53.2 us
    ppermute x32, waiting for transfers between devices, routed(): return lax.ppermute(values, AXES, pairs)  50.4 us
    ppermute x8, starting transfers between devices, along_mp(): lax.ppermute(values, AXES, [(g * size + a, g * size + b) for g in groups...  19.2 us
    convert_element_type x6, other arithmetic, low(): return values.astype(jnp.bfloat16)  10.1 us
    unnamed x72, local copies, waits for them, and re-layouts  6.64 us
  transfers between devices with their start and end apart: 43, of which 21 were waited for; matrix products, arithmetic and copies ran while one was open for 10% of the time, Pallas kernels for 15%

profile of v2, /device:TPU:0, one launch (start us, length us, event | category | flops | bytes accessed | tf_op | source)
XLA Modules:
  0.0 311.3 jit_solution(3035244054632385207)
XLA Ops:
  10.5 3.7 %pack.1 = (bf16[1024,768]{1,0:T(8,128)(2,1)}, bf16[336,768]{1,0:T(8,128)(2,1)}) custom-call(s32[2]{0:T(128)} %pad_add_fusion.rank.refs_0_, bf16[192,768]{1,0:T(8,128)(2,1)} %bitcast.123, bf16[192,768]{1,0:T(8,128)(2,1)} %bitcast.124, bf16[192,768]{1,0:T(8,128)(2,1)} %bitcast.125, bf16[192,768]{1,0:T(8,128)(2,1)} %bitcast.126, bf16[192,768]{1,0:T(8,128)(2,1)} %bitcast.127, ...), custom_call_target="tpu_custom_call" | custom-call | bytes 5927432 | tf_op jit(solution)/shard_map/pack/pallas_call | solution.py:665
  14.2 3.1 collective-permute-done.1
  18.4 3.2 %collective-permute-start.2 = (bf16[336,768]{1,0:T(8,128)(2,1)}, bf16[336,768]{1,0:T(8,128)(2,1)S(1)}, u32[]{:S(2)}, u32[]{:S(2)}) collective-permute-start(bf16[336,768]{1,0:T(8,128)(2,1)} %get-tuple-element.99), channel_id=1, source_target_pairs={{0,2},{1,3},{2,0},{3,1},{4,6},{5,7},{6,4},{7,5},{8,10},{9,11},{10,... | collective-permute-start | bytes 1548296 | tf_op jit(solution)/shard_map/ppermute | solution.py:552
  21.6 3.5 %collective-permute-start.4 = (bf16[336,768]{1,0:T(8,128)(2,1)}, bf16[336,768]{1,0:T(8,128)(2,1)S(1)}, u32[]{:S(2)}, u32[]{:S(2)}) collective-permute-start(bf16[336,768]{1,0:T(8,128)(2,1)} %get-tuple-element.99), channel_id=1, source_target_pairs={{0,1},{1,2},{2,3},{4,5},{5,6},{6,7},{8,9},{9,10},{10,11},{12,13},{... | collective-permute-start | bytes 1548296 | tf_op jit(solution)/shard_map/ppermute | solution.py:552
  26.4 17.7 %collective-permute-done.2 = bf16[336,768]{1,0:T(8,128)(2,1)S(1)} collective-permute-done((bf16[336,768]{1,0:T(8,128)(2,1)}, bf16[336,768]{1,0:T(8,128)(2,1)S(1)}, u32[]{:S(2)}, u32[]{:S(2)}) %collective-permute-start.2) | collective-permute-done | bytes 516128 | tf_op jit(solution)/shard_map/ppermute | solution.py:552
  45.4 3.7 %collective-permute-done.5 = bf16[336,768]{1,0:T(8,128)(2,1)S(1)} collective-permute-done((bf16[336,768]{1,0:T(8,128)(2,1)}, bf16[336,768]{1,0:T(8,128)(2,1)S(1)}, u32[]{:S(2)}, u32[]{:S(2)}) %collective-permute-start.5) | collective-permute-done | bytes 516128 | tf_op jit(solution)/shard_map/ppermute | solution.py:552
  49.1 11.6 %collective-permute-done.3 = bf16[336,768]{1,0:T(8,128)(2,1)} collective-permute-done((bf16[336,768]{1,0:T(8,128)(2,1)S(1)}, bf16[336,768]{1,0:T(8,128)(2,1)}, u32[]{:S(2)}, u32[]{:S(2)}) %collective-permute-start.3) | collective-permute-done | bytes 516128 | tf_op jit(solution)/shard_map/ppermute | solution.py:552
  64.8 2.2 collective-permute-start.6
  69.0 5.1 %collective-permute-start.8 = (bf16[256,768]{1,0:T(8,128)(2,1)S(1)}, bf16[256,768]{1,0:T(8,128)(2,1)S(1)}, u32[]{:S(2)}, u32[]{:S(2)}) collective-permute-start(bf16[256,768]{1,0:T(8,128)(2,1)S(1)} %add_convert_fusion.4.refs_0_.refs_1_), channel_id=1, source_target_pairs={{0,1},{1,2},{2,3},{4,5},{5,6},{6,7},{8,9},{9,10},{10,11},{12,13},{... | collective-permute-start | bytes 1179656 | tf_op jit(solution)/shard_map/ppermute | solution.py:552
  74.4 11.7 %collective-permute-done.6.refs_2_.refs_3_ = bf16[256,768]{1,0:T(8,128)(2,1)S(1)} collective-permute-done((bf16[256,768]{1,0:T(8,128)(2,1)S(1)}, bf16[256,768]{1,0:T(8,128)(2,1)S(1)}, u32[]{:S(2)}, u32[]{:S(2)}) %collective-permute-start.6) | collective-permute-done | bytes 393248 | tf_op jit(solution)/shard_map/ppermute | solution.py:552
  90.5 8.7 %collective-permute-done.7 = bf16[256,768]{1,0:T(8,128)(2,1)} collective-permute-done((bf16[256,768]{1,0:T(8,128)(2,1)S(1)}, bf16[256,768]{1,0:T(8,128)(2,1)}, u32[]{:S(2)}, u32[]{:S(2)}) %collective-permute-start.7) | collective-permute-done | bytes 393248 | tf_op jit(solution)/shard_map/ppermute | solution.py:552
  99.1 2.0 broadcast_select_fusion.2
  103.4 4.1 %row_project.1 = (bf16[3,512,128]{2,1,0:T(8,128)(2,1)}, bf16[6,512,128]{2,1,0:T(8,128)(2,1)}) custom-call(bf16[256,768]{1,0:T(8,128)(2,1)} %copy-done.2, bf16[256,768]{1,0:T(8,128)(2,1)} %get-tuple-element.247.refs_1_.refs_2_, bf16[256,768]{1,0:T(8,128)(2,1)} %copy-done.3, bf16[256,768]{1,0:T(8,128)(2,1)} %get-tuple-element.246.refs_3_.refs_4_, ...), custom_call_target="tpu_custom_call" | custom-call | flops 1006632960 | bytes 4940288 | tf_op jit(solution)/shard_map/row_project/pallas_call | solution.py:665
  107.6 2.8 collective-permute-done.10.kv_sibling
  111.2 7.3 %row_attend.1 = (bf16[3,512,1024]{2,1,0:T(8,128)(2,1)}, bf16[3,128,128]{2,1,0:T(8,128)(2,1)}, bf16[3,128,128]{2,1,0:T(8,128)(2,1)}, bf16[3,128,128]{2,1,0:T(8,128)(2,1)}, bf16[3,128,128]{2,1,0:T(8,128)(2,1)}) custom-call(bf16[3,512,128]{2,1,0:T(8,128)(2,1)} %get-tuple-element.101.q, bf16[6,512,128]{2,1,0:T(8,128)(2,1)} %get-tuple-element.102.kv, ...), custom_call_target="tpu_custom_call" | custom-call | flops 805306368 | bytes 5509120 | tf_op jit(solution)/shard_map/row_attend/pallas_call | solution.py:665
  118.5 3.3 %collective-permute-start.11 = (bf16[3,128,128]{2,1,0:T(8,128)(2,1)}, bf16[3,128,128]{2,1,0:T(8,128)(2,1)S(1)}, u32[]{:S(2)}, u32[]{:S(2)}) collective-permute-start(bf16[3,128,128]{2,1,0:T(8,128)(2,1)} %get-tuple-element.104), channel_id=1, source_target_pairs={{0,3},{1,0},{2,1},{3,2},{4,7},{5,4},{6,5},{7,6},{8,11},{9,8},{10,9... | collective-permute-start | bytes 294920 | tf_op jit(solution)/shard_map/ppermute | solution.py:541
  122.5 2.9 collective-permute-done.11.refs_1_
  125.3 6.1 %collective-permute-done.12.refs_2_ = bf16[3,128,128]{2,1,0:T(8,128)(2,1)S(1)} collective-permute-done((bf16[3,128,128]{2,1,0:T(8,128)(2,1)}, bf16[3,128,128]{2,1,0:T(8,128)(2,1)S(1)}, u32[]{:S(2)}, u32[]{:S(2)}) %collective-permute-start.12) | collective-permute-done | bytes 98336 | tf_op jit(solution)/shard_map/ppermute | solution.py:541
  131.4 1.8 all-gather.3.cloned.1.call-done
  133.3 8.0 %column.1 = (bf16[256,768]{1,0:T(8,128)(2,1)}, f32[256,768]{1,0:T(8,128)}, bf16[256,768]{1,0:T(8,128)(2,1)}, bf16[256,768]{1,0:T(8,128)(2,1)}, bf16[256,768]{1,0...) custom-call(f32[256,768]{1,0:T(8,128)} %fusion.18.refs_8_.stream, ...), custom_call_target="tpu_custom_call" | custom-call | flops 1509949440 | bytes 18898944 | tf_op jit(solution)/shard_map/column/pallas_call | solution.py:665
  141.3 13.8 %ffn.1 = (bf16[256,768]{1,0:T(8,128)(2,1)}, f32[256,768]{1,0:T(8,128)}, bf16[256,768]{1,0:T(8,128)(2,1)}, bf16[8,4,96,1536]{3,2,1,0:T(8,128)(2,1)}, f32[8,768]{1,0:T(8,128)}, /*index=5*/f32[4,768]{1,0:T(4,128)}) custom-call(s32[2]{0:T(128)} %pad_add_fusion.rank.refs_0_, bf16[256,768]{1,0:T(8,128)(2,1)} %get-tuple-element.107.normed, ...), custom_call_target="tpu_custom_call" | custom-call | flops 7247757312 | bytes 26793992 | tf_op jit(solution)/shard_map/ffn/pallas_call | solution.py:665
  155.2 8.3 %column_back.1 = (bf16[256,768]{1,0:T(8,128)(2,1)}, bf16[256,768]{1,0:T(8,128)(2,1)}, bf16[256,768]{1,0:T(8,128)(2,1)}, f32[256,768]{1,0:T(8,128)}, bf16[256,768...) custom-call(f32[256,768]{1,0:T(8,128)} %get-tuple-element.112.grad, ...), custom_call_target="tpu_custom_call" | custom-call | flops 1509949440 | bytes 19295232 | tf_op jit(solution)/shard_map/column_back/pallas_call | solution.py:665
  165.1 2.5 collective-permute-start.15
  169.1 2.3 collective-permute-done.14.refs_1_
  171.4 3.5 %collective-permute-done.15.refs_2_ = bf16[3,128,128]{2,1,0:T(8,128)(2,1)S(1)} collective-permute-done((bf16[3,128,128]{2,1,0:T(8,128)(2,1)}, bf16[3,128,128]{2,1,0:T(8,128)(2,1)S(1)}, u32[]{:S(2)}, u32[]{:S(2)}) %collective-permute-start.15) | collective-permute-done | bytes 98336 | tf_op jit(solution)/shard_map/ppermute | solution.py:541
  175.6 8.5 %row_attend_back.1 = (bf16[3,512,128]{2,1,0:T(8,128)(2,1)}, f32[6,512,128]{2,1,0:T(8,128)}, bf16[6,512,128]{2,1,0:T(8,128)(2,1)}) custom-call(bf16[3,512,128]{2,1,0:T(8,128)(2,1)} %get-tuple-element.101.q, bf16[6,512,128]{2,1,0:T(8,128)(2,1)} %get-tuple-element.102.kv, bf16[6,512,128]{2,1,0:T(8,128)(2,1)} %copy-done.30, ...), custom_call_target="tpu_custom_call" | custom-call | flops 1610612736 | bytes 8257536 | tf_op jit(solution)/shard_map/row_attend_back/pallas_call | solution.py:665
  184.1 2.5 collective-permute-done.17.refs_9_.refs_10_
  187.5 6.7 %weights.1 = (bf16[2,384,1024]{2,1,0:T(8,128)(2,1)}, bf16[2,384,1024]{2,1,0:T(8,128)(2,1)}, bf16[2,384,1024]{2,1,0:T(8,128)(2,1)}, bf16[2,384,1024]{2,1,0:T(8,128)(2,1)}) custom-call(s32[2]{0:T(128)} %pad_add_fusion.rank.refs_0_, bf16[256,768]{1,0:T(8,128)(2,1)} %get-tuple-element.110.refs_1_, bf16[256,768]{1,0:T(8,128)(2,1)} %get-tuple-element.111.grad_low.refs_2_, ...), custom_call_target="tpu_custom_call" | custom-call | flops 1509949440 | bytes 10223624 | tf_op jit(solution)/shard_map/weights/pallas_call | solution.py:665
  194.8 7.1 %row_project_back.1 = (bf16[384,640]{1,0:T(8,128)(2,1)}, bf16[384,640]{1,0:T(8,128)(2,1)}, f32[1,640]{1,0:T(1,128)}, bf16[272,768]{1,0:T(8,128)(2,1)}, bf16[272,...) custom-call(s32[2]{0:T(128)} %pad_add_fusion.rank.refs_0_, bf16[256,768]{1,0:T(8,128)(2,1)} %copy-done.2, ...), custom_call_target="tpu_custom_call" | custom-call | flops 2013265920 | bytes 11178504 | tf_op jit(solution)/shard_map/row_project_back/pallas_call | solution.py:665
  201.9 3.5 %collective-permute-start.20 = (bf16[272,768]{1,0:T(8,128)(2,1)}, bf16[272,768]{1,0:T(8,128)(2,1)}, u32[]{:S(2)}, u32[]{:S(2)}) collective-permute-start(bf16[272,768]{1,0:T(8,128)(2,1)} %get-tuple-element.140), channel_id=1, source_target_pairs={{0,3},{1,0},{2,1},{3,2},{4,7},{5,4},{6,5},{7,6},{8,11},{9,8},{10,9... | collective-permute-start | bytes 1253384 | tf_op jit(solution)/shard_map/ppermute | solution.py:541
  208.4 2.3 add_convert_fusion
  211.8 4.0 %collective-permute-done.20 = bf16[272,768]{1,0:T(8,128)(2,1)} collective-permute-done((bf16[272,768]{1,0:T(8,128)(2,1)}, bf16[272,768]{1,0:T(8,128)(2,1)}, u32[]{:S(2)}, u32[]{:S(2)}) %collective-permute-start.20) | collective-permute-done | bytes 417824 | tf_op jit(solution)/shard_map/ppermute | solution.py:541
  215.8 19.1 %collective-permute-start.22 = (bf16[272,768]{1,0:T(8,128)(2,1)}, bf16[272,768]{1,0:T(8,128)(2,1)}, u32[]{:S(2)}, u32[]{:S(2)}) collective-permute-start(bf16[272,768]{1,0:T(8,128)(2,1)} %get-tuple-element.142), channel_id=1, source_target_pairs={{0,1},{1,2},{2,3},{3,0},{4,5},{5,6},{6,7},{7,4},{8,9},{9,10},{10,1... | collective-permute-start | bytes 1253384 | tf_op jit(solution)/shard_map/ppermute | solution.py:541
  234.9 1.8 fusion.20
  236.7 6.2 %collective-permute-done.21 = bf16[272,768]{1,0:T(8,128)(2,1)} collective-permute-done((bf16[272,768]{1,0:T(8,128)(2,1)}, bf16[272,768]{1,0:T(8,128)(2,1)}, u32[]{:S(2)}, u32[]{:S(2)}) %collective-permute-start.21) | collective-permute-done | bytes 417824 | tf_op jit(solution)/shard_map/ppermute | solution.py:541
  244.2 1.6 convert_add_fusion
  246.2 2.0 add_convert_fusion.3
  248.8 2.2 add_convert_fusion.2
  252.1 1.8 add_convert_fusion.7
  253.9 1.9 collective-permute-start.36
  259.7 3.6 %collective-permute-done.27 = bf16[2,96,1024]{2,1,0:T(8,128)(2,1)} collective-permute-done((bf16[2,96,1024]{2,1,0:T(8,128)(2,1)}, bf16[2,96,1024]{2,1,0:T(8,128)(2,1)}, u32[]{:S(2)}, u32[]{:S(2)}) %collective-permute-start.27) | collective-permute-done | bytes 393248 | tf_op jit(solution)/shard_map/ppermute | solution.py:541
  264.1 1.6 collective-permute-start.32
  269.1 1.7 convert_add_fusion.1
  272.4 2.3 collective-permute-start.30
  280.1 2.6 collective-permute-start.37
  284.5 4.4 %collective-permute-done.39 = bf16[96,1024]{1,0:T(8,128)(2,1)S(1)} collective-permute-done((bf16[96,1024]{1,0:T(8,128)(2,1)S(1)}, bf16[96,1024]{1,0:T(8,128)(2,1)S(1)}, u32[]{:S(2)}, u32[]{:S(2)}) %collective-permute-start.39) | collective-permute-done | bytes 196640 | tf_op jit(solution)/shard_map/ppermute | solution.py:541
  289.0 7.4 %collective-permute-done.38 = bf16[96,1024]{1,0:T(8,128)(2,1)S(1)} collective-permute-done((bf16[96,1024]{1,0:T(8,128)(2,1)S(1)}, bf16[96,1024]{1,0:T(8,128)(2,1)S(1)}, u32[]{:S(2)}, u32[]{:S(2)}) %collective-permute-start.38) | collective-permute-done | bytes 196640 | tf_op jit(solution)/shard_map/ppermute | solution.py:541
  300.4 2.5 home.1
  (210 shorter events, 56.3 us)
Async XLA Ops:
  7.2 126.1 %all-gather.3.cloned.1.call-start = ((), (), s32[]{:S(2)}) async-start(), calls=%async_computation.4 | async-start | bytes 13271040 | tf_op jit(solution)/shard_map/all_gather | solution.py:1203
  8.6 8.7 %collective-permute-start.1 = (bf16[256,768]{1,0:T(8,128)(2,1)S(1)}, bf16[256,768]{1,0:T(8,128)(2,1)S(1)}, u32[]{:S(2)}, u32[]{:S(2)}) collective-permute-start(bf16[256,768]{1,0:T(8,128)(2,1)S(1)} %pad_maximum_fusion.2), channel_id=1, source_target_pairs={{0,8},{1,9},{2,10},{3,11},{4,0},{5,1},{6,2},{7,3},{8,12},{9,13},{1... | collective-permute-start | bytes 1179656 | tf_op jit(solution)/shard_map/ppermute | solution.py:541
  9.2 8.2 %collective-permute-start = (bf16[264,768]{1,0:T(8,128)(2,1)S(1)}, bf16[264,768]{1,0:T(8,128)(2,1)S(1)}, u32[]{:S(2)}, u32[]{:S(2)}) collective-permute-start(bf16[264,768]{1,0:T(8,128)(2,1)S(1)} %pad_maximum_fusion.1), channel_id=1, source_target_pairs={{0,0},{1,1},{2,2},{3,3},{4,8},{5,9},{6,10},{7,11},{8,4},{9,5},{10,... | collective-permute-start | bytes 1216520 | tf_op jit(solution)/shard_map/ppermute | solution.py:541
  18.4 50.5 %copy-start.2 = (bf16[256,768]{1,0:T(8,128)(2,1)}, bf16[256,768]{1,0:T(8,128)(2,1)S(1)}, u32[]{:S(2)}) copy-start(bf16[256,768]{1,0:T(8,128)(2,1)S(1)} %add_convert_fusion.4.refs_0_.refs_1_) | copy-start | bytes 1179652
  18.4 25.7 %collective-permute-start.2 = (bf16[336,768]{1,0:T(8,128)(2,1)}, bf16[336,768]{1,0:T(8,128)(2,1)S(1)}, u32[]{:S(2)}, u32[]{:S(2)}) collective-permute-start(bf16[336,768]{1,0:T(8,128)(2,1)} %get-tuple-element.99), channel_id=1, source_target_pairs={{0,2},{1,3},{2,0},{3,1},{4,6},{5,7},{6,4},{7,5},{8,10},{9,11},{10,... | collective-permute-start | bytes 1548296 | tf_op jit(solution)/shard_map/ppermute | solution.py:552
  21.6 23.8 %collective-permute-start.4 = (bf16[336,768]{1,0:T(8,128)(2,1)}, bf16[336,768]{1,0:T(8,128)(2,1)S(1)}, u32[]{:S(2)}, u32[]{:S(2)}) collective-permute-start(bf16[336,768]{1,0:T(8,128)(2,1)} %get-tuple-element.99), channel_id=1, source_target_pairs={{0,1},{1,2},{2,3},{4,5},{5,6},{6,7},{8,9},{9,10},{10,11},{12,13},{... | collective-permute-start | bytes 1548296 | tf_op jit(solution)/shard_map/ppermute | solution.py:552
  25.1 24.0 %collective-permute-start.5 = (bf16[336,768]{1,0:T(8,128)(2,1)}, bf16[336,768]{1,0:T(8,128)(2,1)S(1)}, u32[]{:S(2)}, u32[]{:S(2)}) collective-permute-start(bf16[336,768]{1,0:T(8,128)(2,1)} %get-tuple-element.99), channel_id=1, source_target_pairs={{1,0},{2,1},{3,2},{5,4},{6,5},{7,6},{9,8},{10,9},{11,10},{13,12},{... | collective-permute-start | bytes 1548296 | tf_op jit(solution)/shard_map/ppermute | solution.py:552
  44.1 16.7 %collective-permute-start.3 = (bf16[336,768]{1,0:T(8,128)(2,1)S(1)}, bf16[336,768]{1,0:T(8,128)(2,1)}, u32[]{:S(2)}, u32[]{:S(2)}) collective-permute-start(bf16[336,768]{1,0:T(8,128)(2,1)S(1)} %collective-permute-done.2), channel_id=1, source_target_pairs={{2,3},{1,0},{6,7},{5,4},{10,11},{9,8},{14,15},{13,12},{18,19},{17,... | collective-permute-start | bytes 1548296 | tf_op jit(solution)/shard_map/ppermute | solution.py:552
  63.4 180.9 %reduce-scatter.3.cloned.1.call-start = ((), (), s32[]{:S(2)}) async-start(), calls=%async_computation.2 | async-start | bytes 10616832 | tf_op jit(solution)/shard_map/reduce_scatter | solution.py:1386
  64.8 21.2 %collective-permute-start.6 = (bf16[256,768]{1,0:T(8,128)(2,1)S(1)}, bf16[256,768]{1,0:T(8,128)(2,1)S(1)}, u32[]{:S(2)}, u32[]{:S(2)}) collective-permute-start(bf16[256,768]{1,0:T(8,128)(2,1)S(1)} %add_convert_fusion.4.refs_0_.refs_1_), channel_id=1, source_target_pairs={{0,2},{1,3},{2,0},{3,1},{4,6},{5,7},{6,4},{7,5},{8,10},{9,11},{10,... | collective-permute-start | bytes 1179656 | tf_op jit(solution)/shard_map/ppermute | solution.py:552
  67.7 22.8 %collective-permute-start.9 = (bf16[256,768]{1,0:T(8,128)(2,1)S(1)}, bf16[256,768]{1,0:T(8,128)(2,1)S(1)}, u32[]{:S(2)}, u32[]{:S(2)}) collective-permute-start(bf16[256,768]{1,0:T(8,128)(2,1)S(1)} %add_convert_fusion.4.refs_0_.refs_1_), channel_id=1, source_target_pairs={{1,0},{2,1},{3,2},{5,4},{6,5},{7,6},{9,8},{10,9},{11,10},{13,12},{... | collective-permute-start | bytes 1179656 | tf_op jit(solution)/shard_map/ppermute | solution.py:552
  69.0 21.5 %collective-permute-start.8 = (bf16[256,768]{1,0:T(8,128)(2,1)S(1)}, bf16[256,768]{1,0:T(8,128)(2,1)S(1)}, u32[]{:S(2)}, u32[]{:S(2)}) collective-permute-start(bf16[256,768]{1,0:T(8,128)(2,1)S(1)} %add_convert_fusion.4.refs_0_.refs_1_), channel_id=1, source_target_pairs={{0,1},{1,2},{2,3},{4,5},{5,6},{6,7},{8,9},{9,10},{10,11},{12,13},{... | collective-permute-start | bytes 1179656 | tf_op jit(solution)/shard_map/ppermute | solution.py:552
  86.1 15.0 %copy-start.3 = (bf16[256,768]{1,0:T(8,128)(2,1)}, bf16[256,768]{1,0:T(8,128)(2,1)S(1)}, u32[]{:S(2)}) copy-start(bf16[256,768]{1,0:T(8,128)(2,1)S(1)} %collective-permute-done.6.refs_2_.refs_3_) | copy-start | bytes 1179652
  86.1 13.1 %collective-permute-start.7 = (bf16[256,768]{1,0:T(8,128)(2,1)S(1)}, bf16[256,768]{1,0:T(8,128)(2,1)}, u32[]{:S(2)}, u32[]{:S(2)}) collective-permute-start(bf16[256,768]{1,0:T(8,128)(2,1)S(1)} %collective-permute-done.6.refs_2_.refs_3_), channel_id=1, source_target_pairs={{2,3},{1,0},{6,7},{5,4},{10,11},{9,8},{14,15},{13,12},{18,19},{17,... | collective-permute-start | bytes 1179656 | tf_op jit(solution)/shard_map/ppermute | solution.py:552
  88.2 13.3 %copy-start.26 = (f32[1,192]{1,0:T(1,128)S(1)}, f32[1,192]{1,0:T(1,128)}, u32[]{:S(2)}) copy-start(f32[1,192]{1,0:T(1,128)} %bq.1) | copy-start | bytes 2308
  88.2 14.0 %copy-start.27 = (f32[1,192]{1,0:T(1,128)S(1)}, f32[1,192]{1,0:T(1,128)}, u32[]{:S(2)}) copy-start(f32[1,192]{1,0:T(1,128)} %bv.1) | copy-start | bytes 2308
  88.2 14.7 %copy-start.23 = (f32[1,768]{1,0:T(1,128)S(1)}, f32[1,768]{1,0:T(1,128)}, u32[]{:S(2)}) copy-start(f32[1,768]{1,0:T(1,128)} %b1.1) | copy-start | bytes 9220
  107.6 2.8 collective-permute-start.10
  118.5 6.8 %collective-permute-start.11 = (bf16[3,128,128]{2,1,0:T(8,128)(2,1)}, bf16[3,128,128]{2,1,0:T(8,128)(2,1)S(1)}, u32[]{:S(2)}, u32[]{:S(2)}) collective-permute-start(bf16[3,128,128]{2,1,0:T(8,128)(2,1)} %get-tuple-element.104), channel_id=1, source_target_pairs={{0,3},{1,0},{2,1},{3,2},{4,7},{5,4},{6,5},{7,6},{8,11},{9,8},{10,9... | collective-permute-start | bytes 294920 | tf_op jit(solution)/shard_map/ppermute | solution.py:541
  121.8 9.6 %collective-permute-start.12 = (bf16[3,128,128]{2,1,0:T(8,128)(2,1)}, bf16[3,128,128]{2,1,0:T(8,128)(2,1)S(1)}, u32[]{:S(2)}, u32[]{:S(2)}) collective-permute-start(bf16[3,128,128]{2,1,0:T(8,128)(2,1)} %get-tuple-element.105), channel_id=1, source_target_pairs={{0,2},{1,3},{2,0},{3,1},{4,6},{5,7},{6,4},{7,5},{8,10},{9,11},{10,... | collective-permute-start | bytes 294920 | tf_op jit(solution)/shard_map/ppermute | solution.py:541
  121.8 9.6 %collective-permute-start.13 = (bf16[3,128,128]{2,1,0:T(8,128)(2,1)}, bf16[3,128,128]{2,1,0:T(8,128)(2,1)S(1)}, u32[]{:S(2)}, u32[]{:S(2)}) collective-permute-start(bf16[3,128,128]{2,1,0:T(8,128)(2,1)} %get-tuple-element.106), channel_id=1, source_target_pairs={{0,1},{1,2},{2,3},{3,0},{4,5},{5,6},{6,7},{7,4},{8,9},{9,10},{10,1... | collective-permute-start | bytes 294920 | tf_op jit(solution)/shard_map/ppermute | solution.py:541
  155.2 147.7 %reduce-scatter.5.cloned.1.call-start = ((), (), s32[]{:S(2)}) async-start(), calls=%async_computation.3 | async-start | bytes 1474560 | tf_op jit(solution)/shard_map/reduce_scatter | solution.py:1389
  163.6 7.8 %collective-permute-start.14 = (bf16[3,128,128]{2,1,0:T(8,128)(2,1)}, bf16[3,128,128]{2,1,0:T(8,128)(2,1)S(1)}, u32[]{:S(2)}, u32[]{:S(2)}) collective-permute-start(bf16[3,128,128]{2,1,0:T(8,128)(2,1)} %get-tuple-element.125), channel_id=1, source_target_pairs={{0,1},{1,2},{2,3},{3,0},{4,5},{5,6},{6,7},{7,4},{8,9},{9,10},{10,1... | collective-permute-start | bytes 294920 | tf_op jit(solution)/shard_map/ppermute | solution.py:541
  165.1 9.8 %collective-permute-start.15 = (bf16[3,128,128]{2,1,0:T(8,128)(2,1)}, bf16[3,128,128]{2,1,0:T(8,128)(2,1)S(1)}, u32[]{:S(2)}, u32[]{:S(2)}) collective-permute-start(bf16[3,128,128]{2,1,0:T(8,128)(2,1)} %get-tuple-element.126), channel_id=1, source_target_pairs={{0,2},{1,3},{2,0},{3,1},{4,6},{5,7},{6,4},{7,5},{8,10},{9,11},{10,... | collective-permute-start | bytes 294920 | tf_op jit(solution)/shard_map/ppermute | solution.py:541
  167.6 7.3 %collective-permute-start.16 = (bf16[3,128,128]{2,1,0:T(8,128)(2,1)}, bf16[3,128,128]{2,1,0:T(8,128)(2,1)S(1)}, u32[]{:S(2)}, u32[]{:S(2)}) collective-permute-start(bf16[3,128,128]{2,1,0:T(8,128)(2,1)} %get-tuple-element.127), channel_id=1, source_target_pairs={{0,3},{1,0},{2,1},{3,2},{4,7},{5,4},{6,5},{7,6},{8,11},{9,8},{10,9... | collective-permute-start | bytes 294920 | tf_op jit(solution)/shard_map/ppermute | solution.py:541
  184.1 2.5 collective-permute-start.17
  194.2 11.2 %collective-permute-start.18 = (bf16[2,384,1024]{2,1,0:T(8,128)(2,1)}, bf16[2,384,1024]{2,1,0:T(8,128)(2,1)}, u32[]{:S(2)}, u32[]{:S(2)}) collective-permute-start(bf16[2,384,1024]{2,1,0:T(8,128)(2,1)} %get-tuple-element.130), channel_id=1, source_target_pairs={{0,8},{1,9},{2,10},{3,11},{4,12},{5,13},{6,14},{7,15},{8,0},{9,1},... | collective-permute-start | bytes 4718600 | tf_op jit(solution)/shard_map/ppermute | solution.py:541
  194.3 11.2 %collective-permute-start.19 = (bf16[2,384,1024]{2,1,0:T(8,128)(2,1)}, bf16[2,384,1024]{2,1,0:T(8,128)(2,1)}, u32[]{:S(2)}, u32[]{:S(2)}) collective-permute-start(bf16[2,384,1024]{2,1,0:T(8,128)(2,1)} %get-tuple-element.131), channel_id=1, source_target_pairs={{0,8},{1,9},{2,10},{3,11},{4,12},{5,13},{6,14},{7,15},{8,0},{9,1},... | collective-permute-start | bytes 4718600 | tf_op jit(solution)/shard_map/ppermute | solution.py:541
  201.9 13.9 %collective-permute-start.20 = (bf16[272,768]{1,0:T(8,128)(2,1)}, bf16[272,768]{1,0:T(8,128)(2,1)}, u32[]{:S(2)}, u32[]{:S(2)}) collective-permute-start(bf16[272,768]{1,0:T(8,128)(2,1)} %get-tuple-element.140), channel_id=1, source_target_pairs={{0,3},{1,0},{2,1},{3,2},{4,7},{5,4},{6,5},{7,6},{8,11},{9,8},{10,9... | collective-permute-start | bytes 1253384 | tf_op jit(solution)/shard_map/ppermute | solution.py:541
  206.9 36.0 %collective-permute-start.23 = (bf16[2,192,1024]{2,1,0:T(8,128)(2,1)S(1)}, bf16[2,192,1024]{2,1,0:T(8,128)(2,1)S(1)}, u32[]{:S(2)}, u32[]{:S(2)}) collective-permute-start(bf16[2,192,1024]{2,1,0:T(8,128)(2,1)S(1)} %add_convert_fusion.1), channel_id=1, source_target_pairs={{0,4},{1,5},{2,6},{3,7},{4,0},{5,1},{6,2},{7,3},{8,12},{9,13},{10,... | collective-permute-start | bytes 2359304 | tf_op jit(solution)/shard_map/ppermute | solution.py:541
  210.7 32.2 %collective-permute-start.24 = (bf16[2,192,1024]{2,1,0:T(8,128)(2,1)}, bf16[2,192,1024]{2,1,0:T(8,128)(2,1)}, u32[]{:S(2)}, u32[]{:S(2)}) collective-permute-start(bf16[2,192,1024]{2,1,0:T(8,128)(2,1)} %add_convert_fusion), channel_id=1, source_target_pairs={{0,16},{1,17},{2,18},{3,19},{4,20},{5,21},{6,22},{7,23},{8,24},{9,... | collective-permute-start | bytes 2359304 | tf_op jit(solution)/shard_map/ppermute | solution.py:541
  211.3 31.6 %collective-permute-start.25 = (bf16[384,640]{1,0:T(8,128)(2,1)}, bf16[384,640]{1,0:T(8,128)(2,1)}, u32[]{:S(2)}, u32[]{:S(2)}) collective-permute-start(bf16[384,640]{1,0:T(8,128)(2,1)} %get-tuple-element.144), channel_id=1, source_target_pairs={{0,8},{1,9},{2,10},{3,11},{4,12},{5,13},{6,14},{7,15},{8,0},{9,1},... | collective-permute-start | bytes 1474568 | tf_op jit(solution)/shard_map/ppermute | solution.py:541
  211.3 31.5 %collective-permute-start.21 = (bf16[272,768]{1,0:T(8,128)(2,1)}, bf16[272,768]{1,0:T(8,128)(2,1)}, u32[]{:S(2)}, u32[]{:S(2)}) collective-permute-start(bf16[272,768]{1,0:T(8,128)(2,1)} %get-tuple-element.141), channel_id=1, source_target_pairs={{0,2},{1,3},{2,0},{3,1},{4,6},{5,7},{6,4},{7,5},{8,10},{9,11},{10,... | collective-permute-start | bytes 1253384 | tf_op jit(solution)/shard_map/ppermute | solution.py:541
  215.8 27.1 %collective-permute-start.22 = (bf16[272,768]{1,0:T(8,128)(2,1)}, bf16[272,768]{1,0:T(8,128)(2,1)}, u32[]{:S(2)}, u32[]{:S(2)}) collective-permute-start(bf16[272,768]{1,0:T(8,128)(2,1)} %get-tuple-element.142), channel_id=1, source_target_pairs={{0,1},{1,2},{2,3},{3,0},{4,5},{5,6},{6,7},{7,4},{8,9},{9,10},{10,1... | collective-permute-start | bytes 1253384 | tf_op jit(solution)/shard_map/ppermute | solution.py:541
  248.2 11.4 %collective-permute-start.26 = (bf16[2,96,1024]{2,1,0:T(8,128)(2,1)}, bf16[2,96,1024]{2,1,0:T(8,128)(2,1)}, u32[]{:S(2)}, u32[]{:S(2)}) collective-permute-start(bf16[2,96,1024]{2,1,0:T(8,128)(2,1)} %add_convert_fusion.3), channel_id=1, source_target_pairs={{0,16},{1,17},{2,18},{3,19},{4,20},{5,21},{6,22},{7,23},{8,24},{9,... | collective-permute-start | bytes 1179656 | tf_op jit(solution)/shard_map/ppermute | solution.py:541
  251.0 12.3 %collective-permute-start.27 = (bf16[2,96,1024]{2,1,0:T(8,128)(2,1)}, bf16[2,96,1024]{2,1,0:T(8,128)(2,1)}, u32[]{:S(2)}, u32[]{:S(2)}) collective-permute-start(bf16[2,96,1024]{2,1,0:T(8,128)(2,1)} %add_convert_fusion.2), channel_id=1, source_target_pairs={{0,4},{1,5},{2,6},{3,7},{4,0},{5,1},{6,2},{7,3},{8,12},{9,13},{10,... | collective-permute-start | bytes 1179656 | tf_op jit(solution)/shard_map/ppermute | solution.py:541
  252.0 6.4 %collective-permute-start.28 = (f32[13,768]{1,0:T(8,128)S(1)}, f32[13,768]{1,0:T(8,128)}, u32[]{:S(2)}, u32[]{:S(2)}) collective-permute-start(f32[13,768]{1,0:T(8,128)S(1)} %select_maximum_fusion), channel_id=1, source_target_pairs={{0,8},{1,9},{2,10},{3,11},{4,12},{5,13},{6,14},{7,15},{8,0},{9,1},... | collective-permute-start | bytes 119816 | tf_op jit(solution)/shard_map/ppermute | solution.py:541
  253.9 24.1 %collective-permute-start.36 = (bf16[96,640]{1,0:T(8,128)(2,1)}, bf16[96,640]{1,0:T(8,128)(2,1)S(1)}, u32[]{:S(2)}, u32[]{:S(2)}) collective-permute-start(bf16[96,640]{1,0:T(8,128)(2,1)} %get-tuple-element.225), channel_id=1, source_target_pairs={{0,20},{1,21},{2,22},{3,23},{4,16},{5,17},{6,18},{7,19},{8,28},{9,... | collective-permute-start | bytes 368648 | tf_op jit(solution)/shard_map/ppermute | solution.py:541
  255.9 22.9 %collective-permute-start.35 = (bf16[96,640]{1,0:T(8,128)(2,1)}, bf16[96,640]{1,0:T(8,128)(2,1)}, u32[]{:S(2)}, u32[]{:S(2)}) collective-permute-start(bf16[96,640]{1,0:T(8,128)(2,1)} %get-tuple-element.226), channel_id=1, source_target_pairs={{0,4},{1,5},{2,6},{3,7},{4,0},{5,1},{6,2},{7,3},{8,12},{9,13},{10,... | collective-permute-start | bytes 368648 | tf_op jit(solution)/shard_map/ppermute | solution.py:541
  264.1 7.6 %collective-permute-start.32 = (f32[13,768]{1,0:T(8,128)S(1)}, f32[13,768]{1,0:T(8,128)S(1)}, u32[]{:S(2)}, u32[]{:S(2)}) collective-permute-start(f32[13,768]{1,0:T(8,128)S(1)} %fusion.24), channel_id=1, source_target_pairs={{0,16},{1,17},{2,18},{3,19},{4,20},{5,21},{6,22},{7,23},{8,24},{9,... | collective-permute-start | bytes 119816 | tf_op jit(solution)/shard_map/ppermute | solution.py:541
  265.7 6.7 %collective-permute-start.33 = (f32[13,768]{1,0:T(8,128)S(1)}, f32[13,768]{1,0:T(8,128)S(1)}, u32[]{:S(2)}, u32[]{:S(2)}) collective-permute-start(f32[13,768]{1,0:T(8,128)S(1)} %fusion.24), channel_id=1, source_target_pairs={{0,20},{1,21},{2,22},{3,23},{4,16},{5,17},{6,18},{7,19},{8,28},{9,... | collective-permute-start | bytes 119816 | tf_op jit(solution)/shard_map/ppermute | solution.py:541
  266.7 8.1 %collective-permute-start.31 = (f32[13,768]{1,0:T(8,128)S(1)}, f32[13,768]{1,0:T(8,128)S(1)}, u32[]{:S(2)}, u32[]{:S(2)}) collective-permute-start(f32[13,768]{1,0:T(8,128)S(1)} %fusion.24), channel_id=1, source_target_pairs={{0,4},{1,5},{2,6},{3,7},{4,0},{5,1},{6,2},{7,3},{8,12},{9,13},{10,... | collective-permute-start | bytes 119816 | tf_op jit(solution)/shard_map/ppermute | solution.py:541
  271.7 27.9 %collective-permute-start.29 = (bf16[256,768]{1,0:T(8,128)(2,1)S(1)}, bf16[256,768]{1,0:T(8,128)(2,1)S(1)}, u32[]{:S(2)}, u32[]{:S(2)}) collective-permute-start(bf16[256,768]{1,0:T(8,128)(2,1)S(1)} %pad_maximum_fusion.5), channel_id=1, source_target_pairs={{0,0},{1,1},{2,2},{3,3},{4,8},{5,9},{6,10},{7,11},{8,4},{9,5},{10,... | collective-permute-start | bytes 1179656 | tf_op jit(solution)/shard_map/ppermute | solution.py:541
  272.4 27.2 %collective-permute-start.30 = (bf16[256,768]{1,0:T(8,128)(2,1)S(1)}, bf16[256,768]{1,0:T(8,128)(2,1)}, u32[]{:S(2)}, u32[]{:S(2)}) collective-permute-start(bf16[256,768]{1,0:T(8,128)(2,1)S(1)} %pad_maximum_fusion.6), channel_id=1, source_target_pairs={{0,4},{1,5},{2,6},{3,7},{4,12},{5,13},{6,14},{7,15},{8,0},{9,1},{1... | collective-permute-start | bytes 1179656 | tf_op jit(solution)/shard_map/ppermute | solution.py:541
  274.7 5.4 %collective-permute-start.34 = (bf16[96,640]{1,0:T(8,128)(2,1)S(1)}, bf16[96,640]{1,0:T(8,128)(2,1)S(1)}, u32[]{:S(2)}, u32[]{:S(2)}) collective-permute-start(bf16[96,640]{1,0:T(8,128)(2,1)S(1)} %copy-done.17), channel_id=1, source_target_pairs={{0,16},{1,17},{2,18},{3,19},{4,20},{5,21},{6,22},{7,23},{8,24},{9,... | collective-permute-start | bytes 368648 | tf_op jit(solution)/shard_map/ppermute | solution.py:541
  278.1 10.9 %collective-permute-start.39 = (bf16[96,1024]{1,0:T(8,128)(2,1)S(1)}, bf16[96,1024]{1,0:T(8,128)(2,1)S(1)}, u32[]{:S(2)}, u32[]{:S(2)}) collective-permute-start(bf16[96,1024]{1,0:T(8,128)(2,1)S(1)} %get-tuple-element.166), channel_id=1, source_target_pairs={{0,1},{1,2},{2,3},{3,0},{4,5},{5,6},{6,7},{7,4},{8,9},{9,10},{10,1... | collective-permute-start | bytes 589832 | tf_op jit(solution)/shard_map/ppermute | solution.py:541
  278.7 17.6 %collective-permute-start.38 = (bf16[96,1024]{1,0:T(8,128)(2,1)S(1)}, bf16[96,1024]{1,0:T(8,128)(2,1)S(1)}, u32[]{:S(2)}, u32[]{:S(2)}) collective-permute-start(bf16[96,1024]{1,0:T(8,128)(2,1)S(1)} %get-tuple-element.165), channel_id=1, source_target_pairs={{0,2},{1,3},{2,0},{3,1},{4,6},{5,7},{6,4},{7,5},{8,10},{9,11},{10,... | collective-permute-start | bytes 589832 | tf_op jit(solution)/shard_map/ppermute | solution.py:541
  280.1 16.2 %collective-permute-start.37 = (bf16[96,1024]{1,0:T(8,128)(2,1)S(1)}, bf16[96,1024]{1,0:T(8,128)(2,1)S(1)}, u32[]{:S(2)}, u32[]{:S(2)}) collective-permute-start(bf16[96,1024]{1,0:T(8,128)(2,1)S(1)} %slice_bitcast_fusion.5), channel_id=1, source_target_pairs={{0,3},{1,0},{2,1},{3,2},{4,7},{5,4},{6,5},{7,6},{8,11},{9,8},{10,9... | collective-permute-start | bytes 589832 | tf_op jit(solution)/shard_map/ppermute | solution.py:541
  (30 other events, 104.8 us)
Sparse Core Ops, SparseCore 0:
  63.5 69.7 all-gather.2
  155.3 88.8 reduce-scatter.2
  257.0 28.8 reduce-scatter.4
